TPU v7x, 256 devices: a whole 4x4x8 slice. The times are simulated.
256 devices in a mesh: dp: 8 (over x, core), ctx: 32 (over z, y).
Axes of the slice: x: 4, y: 4, z: 8, core: 2. Of those that a mesh axis runs over, the one named last changes fastest.
Arguments:
- queries: bfloat16 [8, 64, 24576], P('dp', 'ctx'), may hold values from -6 to 6
- grad_out: bfloat16 [8, 64, 16384], P('dp', 'ctx'), may hold values from -64 to 64
- latent: bfloat16 [8, 4096, 576], P('dp', 'ctx'), may hold values from -6 to 6
- latent_up: bfloat16 [512, 32768], P(None, 'ctx'), may hold values from -0.25 to 0.25
- query_start: int32 [8], P('dp'), may hold values from 2 to 4032
- key_lengths: int32 [8], P('dp'), may hold values from 66 to 4096, as said below
Outputs:
- grad_queries: float32 [8, 64, 24576], P('dp', 'ctx')
- grad_latent: float32 [8, 4096, 576], P('dp', 'ctx')
- grad_latent_up: float32 [512, 32768], P('dp', 'ctx')
Inputs may be any that keep to these rules, and one draw needn't show every extreme that they name: key_lengths[g] is at most query_start[g] + 64.
All inputs are finite; a program needn't handle non-finite values.
Results may differ from a plain program's by a relative error of at most 0.015.
Values may be sent and summed in bfloat16 or wider, within the bound.
No kernel may reach another device: no remote copies, remote signals or barrier semaphores. Data moves between devices by JAX's collectives and lax.ppermute only.
A program may use at most 128 MiB of HBM per device.

v0:
```python
import math

import jax
import jax.numpy as jnp
from jax import lax
from jax.experimental import pallas as pl
from jax.experimental.pallas import tpu as pltpu
from jax.sharding import Mesh
from jax.sharding import PartitionSpec as P


DN = 128
DR = 64
DV = 128
C = 512
W = C + DR
NZ = 8
NY = 4
HEADS = 4
NQ = 64
ROWS = NQ * HEADS
WIDE = 2 * C + 2 * DR
BLK = 128
DP = ("x", "core")
CTX = ("z", "y")
MSCALE = 0.1 * math.log(40.0) + 1.0
SCALE = MSCALE * MSCALE / math.sqrt(DN + DR)
NEG_FILL = -1e30
BF = jnp.bfloat16
F32 = jnp.float32
OFFSETS = (0, 4, -3, 3, -2, 2, -1, 1)
KEYS = 2 * NZ * BLK
TILE = 256


def turned(flip):
    pairs = []
    for c in range(2):
        for y in range(NY):
            v, w = y >> 1, y & 1
            pairs.append((c * NY + y, v * NY + 2 * c + (w ^ flip)))
    return pairs


def swap_pairs():
    pairs = []
    for c in range(2):
        for y in range(NY):
            home = (y >> 1) == c
            pairs.append((c * NY + y, c * NY + y if home else (1 - c) * NY + 3 - y))
    return pairs


def swap(v):
    return lax.ppermute(v, ("core", "y"), swap_pairs())


def turn(v, flip):
    return lax.ppermute(v, ("core", "y"), turned(flip))


def other_core(v):
    return lax.ppermute(v, "core", [(0, 1), (1, 0)])


def pair_y(v):
    return lax.ppermute(v, "y", [(i, i ^ 1) for i in range(NY)])


def along_z(v, step):
    return lax.ppermute(v, "z", [(i, (i + step) % NZ) for i in range(NZ)])


def dot(a, b, da=1, db=0):
    return lax.dot_general(a, b, (((da,), (db,)), ((), ())), preferred_element_type=F32)


def vmem(shape, dtype):
    return jax.ShapeDtypeStruct(shape, dtype)


def call(body, out_shape, args, flops, scratch=(), smem=0, mib=32):
    specs = [pl.BlockSpec(memory_space=pltpu.SMEM)] * smem
    specs += [pl.BlockSpec(memory_space=pltpu.VMEM)] * (len(args) - smem)
    size = sum(a.size * a.dtype.itemsize for a in args)
    size += sum(o.size * o.dtype.itemsize for o in out_shape)
    return pl.pallas_call(
        body,
        out_shape=out_shape,
        in_specs=specs,
        out_specs=[pl.BlockSpec(memory_space=pltpu.VMEM)] * len(out_shape),
        scratch_shapes=list(scratch),
        compiler_params=pltpu.CompilerParams(vmem_limit_bytes=mib * 1024 * 1024),
        cost_estimate=pl.CostEstimate(flops=flops, bytes_accessed=size, transcendentals=0),
    )(*args)


def latents_body(start, length, both, w, out):
    lane = lax.broadcasted_iota(jnp.int32, (NQ, DR), 1)
    note = jnp.zeros((NQ, DR), F32)
    low = start[0] + NQ - length[0]
    for n, v in enumerate((start[0] // NQ, start[0] % NQ, low // NQ, low % NQ)):
        note = jnp.where(lane == n, v.astype(F32), note)
    note = note.astype(BF)
    for h in range(HEADS):
        rows = slice(h * NQ, (h + 1) * NQ)
        nope = both[:, h * (DN + DR) : h * (DN + DR) + DN]
        rope = both[:, h * (DN + DR) + DN : (h + 1) * (DN + DR)]
        at = HEADS * (DN + DR) + h * DV
        grad = both[:, at : at + DV]
        wk = w[:, h * (DN + DV) : h * (DN + DV) + DN]
        wv = w[:, h * (DN + DV) + DN : (h + 1) * (DN + DV)]
        out[rows, :C] = dot(grad, wv, 1, 1).astype(BF)
        out[rows, C : 2 * C] = dot(nope, wk, 1, 1).astype(BF)
        out[rows, 2 * C : C + W] = rope
        out[rows, C + W :] = note


def join_body(*refs):
    for b in range(NZ):
        refs[NZ][:, b * BLK : (b + 1) * BLK] = refs[b][...]


def scores_body(*refs):
    scal, mine, other = refs[:3]
    keys = refs[3:5]
    e_mine, e_their, kt, stats, s_ref, gp_ref = refs[5:]
    z, y_own = scal[0], scal[1]
    for n in range(2):
        kt[:, n * NZ * BLK : (n + 1) * NZ * BLK] = keys[n][...]
    for half, qg in ((0, mine), (1, other)):
        rows = slice(half * ROWS, (half + 1) * ROWS)
        q = qg[:, C : C + W]
        g = qg[:, :C]
        for t in range(KEYS // TILE):
            cols = slice(t * TILE, (t + 1) * TILE)
            s_ref[rows, cols] = dot(q, kt[:, cols])
            gp_ref[rows, cols] = dot(g, kt[:C, cols])
    step = 16
    lane = lax.broadcasted_iota(jnp.int32, (step, BLK), 1)
    sub = lax.broadcasted_iota(jnp.int32, (step, 1), 0)
    pos = []
    for y in (y_own, 3 - y_own):
        for d in OFFSETS:
            pos.append(((z + d + NZ) % NZ) * (NY * BLK) + y * BLK + lane)

    @pl.loop(0, 2 * ROWS // step)
    def _(i):
        r0 = pl.multiple_of(i * step, step)
        here = pl.ds(r0, step)
        below = pl.ds(pl.multiple_of(2 * ROWS + r0, step), step)
        note = mine[pl.ds(pl.multiple_of(lax.rem(r0, ROWS), step), step), 2 * C :].astype(F32)
        note = note.astype(jnp.int32)
        start = note[:, DR : DR + 1] * NQ + note[:, DR + 1 : DR + 2]
        low = note[:, DR + 2 : DR + 3] * NQ + note[:, DR + 3 : DR + 4]
        last = start + lax.rem(r0, NQ) + sub
        peak = None
        for b in range(16):
            cols = slice(b * BLK, (b + 1) * BLK)
            ok = (pos[b] >= low) & (pos[b] <= last)
            v = jnp.where(ok, s_ref[here, cols] * SCALE, NEG_FILL)
            s_ref[here, cols] = v
            peak = v if peak is None else jnp.maximum(peak, v)
        m = jnp.max(peak, axis=1, keepdims=True)
        total = jnp.zeros((step, BLK), F32)
        rsum = jnp.zeros((step, BLK), F32)
        for b in range(16):
            cols = slice(b * BLK, (b + 1) * BLK)
            v = s_ref[here, cols]
            e = jnp.where(v > 0.5 * NEG_FILL, jnp.exp(v - m), 0.0)
            s_ref[here, cols] = e
            total = total + e
            rsum = rsum + e * gp_ref[here, cols]
        l = jnp.sum(total, axis=1, keepdims=True)
        rd = jnp.sum(rsum, axis=1, keepdims=True) / jnp.where(l > 0.0, l, 1.0)
        for b in range(16):
            cols = slice(b * BLK, (b + 1) * BLK)
            out = e_mine if b < 8 else e_their
            oc = slice((b % 8) * BLK, (b % 8 + 1) * BLK)
            e = s_ref[here, cols]
            out[here, oc] = (e * (gp_ref[here, cols] - rd)).astype(BF)
            out[below, oc] = e.astype(BF)
        stats[here, :] = jnp.where(lane == 0, m, jnp.where(lane == 1, l, rd))


def key_parts(qq, ee, out):
    for k in range(NZ // 2):
        r = dot(qq[...], ee[:, k * TILE : (k + 1) * TILE], 0, 0)
        for n in range(2):
            out[2 * k + n] = r[:, n * BLK : (n + 1) * BLK].astype(BF)


def add_body(a, b, *outs):
    for k in range(NZ):
        outs[k][...] = (a[k].astype(F32) + b[k].astype(F32)).astype(BF)


def total_body(*refs):
    acc = refs[0][...].astype(F32)
    for k in range(1, NZ):
        acc = acc + refs[k][...].astype(F32)
    refs[NZ][...] = acc.astype(BF)


def first_body(st, their, mine, other, ee, qq, ws, out):
    step = 64

    def body(rows, trows, qg, qrows):
        m, l, rd = st[rows, 0:1], st[rows, 1:2], st[rows, 2:3]
        m2, l2, rd2 = their[trows, 0:1], their[trows, 1:2], their[trows, 2:3]
        top = jnp.maximum(m, m2)
        a = jnp.exp(m - top)
        a2 = jnp.exp(m2 - top)
        denom = l * a + l2 * a2
        shift = (rd * l * a + rd2 * l2 * a2) / denom - rd
        w = a / denom
        sw = SCALE * w
        q = qg[qrows, C : C + W].astype(F32)
        g = qg[qrows, :C].astype(F32)
        qs = q * sw
        qq[rows, :] = qs.astype(BF)
        qd = qs * shift
        low_rows = pl.ds(pl.multiple_of(rows.start + 2 * ROWS, step), step)
        qq[low_rows, :C] = (g * w - qd[:, :C]).astype(BF)
        qq[low_rows, C:] = (-qd[:, C:]).astype(BF)
        lane = lax.broadcasted_iota(jnp.int32, (step, BLK), 1)
        ws[rows, :] = jnp.where(lane == 0, w, shift)

    for half, qg in ((0, mine), (1, other)):

        @pl.loop(0, ROWS // step)
        def _(i):
            r = pl.multiple_of(i * step, step)
            mine_at = pl.multiple_of(half * ROWS + r, step)
            their_at = pl.multiple_of((1 - half) * ROWS + r, step)
            body(pl.ds(mine_at, step), pl.ds(their_at, step), qg, pl.ds(r, step))

    key_parts(qq, ee, out)


def parts_body(qq, ee, out):
    key_parts(qq, ee, out)


def query_body(ws, kt, e0, e1, mine, other):
    for half, out in ((0, mine), (1, other)):
        xs = []
        for top in (0, 2 * ROWS):
            rows = slice(top + half * ROWS, top + (half + 1) * ROWS)
            acc = None
            at = 0
            for e in (e0, e1):
                n = e.shape[1]
                r = dot(e[rows, :], kt[:, at : at + n], 1, 1)
                acc = r if acc is None else acc + r
                at += n
            xs.append(acc)
        rows = slice(half * ROWS, (half + 1) * ROWS)
        w = ws[rows, 0:1]
        shift = ws[rows, 1:2]
        out[:, :C] = (w * xs[1][:, :C]).astype(out.dtype)
        out[:, C : C + W] = ((SCALE * w) * (xs[0] - shift * xs[1])).astype(out.dtype)
        out[:, C + W :] = jnp.zeros((ROWS, DR), out.dtype)


def tail_body(scal, qo, both, w, gq, keep, send, terms):
    for h in range(HEADS):
        rows = slice(h * NQ, (h + 1) * NQ)
        o = qo[rows, :C]
        lat = qo[rows, C : 2 * C]
        nope = both[:, h * (DN + DR) : h * (DN + DR) + DN]
        at = HEADS * (DN + DR) + h * DV
        grad = both[:, at : at + DV]
        c0 = h * (DN + DV)
        terms[:, c0 : c0 + DN] = dot(lat, nope, 0, 0).astype(BF)
        terms[:, c0 + DN : c0 + DN + DV] = dot(o, grad, 0, 0).astype(BF)
        q0 = h * (DN + DR)
        gq[:, q0 : q0 + DN] = dot(lat, w[:, c0 : c0 + DN]).astype(BF)
        gq[:, q0 + DN : q0 + DN + DR] = qo[rows, 2 * C : C + W]
    x, c = scal[2], scal[3]
    n = C // 8
    for k in range(4):
        base = lax.rem(x + k, 4) * (2 * n)
        slot = slice(k * n, (k + 1) * n)
        keep[slot, :] = terms[pl.ds(pl.multiple_of(base + c * n, n), n), :]
        send[slot, :] = terms[pl.ds(pl.multiple_of(base + (1 - c) * n, n), n), :]


def step(queries, grad_out, latent, latent_up, query_start, key_lengths):
    ndev = NZ * NY
    own_q = queries.shape[1]

    own = swap(latent[0].T)
    both = jnp.concatenate(
        [
            queries.reshape(own_q, ndev, HEADS * (DN + DR)),
            grad_out.reshape(own_q, ndev, HEADS * DV),
        ],
        axis=2,
    )
    both = jnp.moveaxis(both, 1, 0)
    both = lax.all_to_all(both, CTX, 0, 0, tiled=True)
    both = both.reshape(NQ, HEADS * (DN + DR + DV))

    kept = [own] + [along_z(own, -d) for d in OFFSETS[1:]]

    (qg,) = call(
        latents_body,
        [vmem((ROWS, WIDE), BF)],
        (query_start, key_lengths, both, latent_up),
        270_000_000,
        smem=2,
    )
    qg_mine = turn(qg, 0)
    qg_other = turn(qg, 1)
    (mine_side,) = call(join_body, [vmem((W, NZ * BLK), BF)], kept, 1_000_000)
    their_side = other_core(mine_side)

    zi = lax.axis_index("z")
    yi = lax.axis_index("y")
    ci = lax.axis_index("core")
    y_own = jnp.where((yi >> 1) == ci, yi, 3 - yi)
    scal = jnp.stack([zi, y_own, lax.axis_index("x"), ci]).astype(jnp.int32)
    half = vmem((4 * ROWS, NZ * BLK), BF)
    big = pltpu.VMEM((2 * ROWS, KEYS), F32)
    e_mine, e_their, kt, stats = call(
        scores_body,
        [half, half, vmem((W, KEYS), BF), vmem((2 * ROWS, BLK), F32)],
        (scal, qg_mine, qg_other, mine_side, their_side),
        2_280_000_000,
        (big, big),
        smem=1,
    )
    theirs = pair_y(stats)

    piece = vmem((NZ, W, BLK), BF)
    qq, ws, their_keys = call(
        first_body,
        [vmem((4 * ROWS, W), BF), vmem((2 * ROWS, BLK), F32), piece],
        (stats, theirs, qg_mine, qg_other, e_their),
        1_300_000_000,
    )
    their_keys = other_core(their_keys)
    (mine_keys,) = call(parts_body, [piece], (qq, e_mine), 1_200_000_000)
    sums = call(add_body, [vmem((W, BLK), BF)] * NZ, (mine_keys, their_keys), 1_000_000)
    sums, ws = lax.optimization_barrier((sums, ws))
    sums = [sums[0]] + [along_z(sums[n + 1], d) for n, d in enumerate(OFFSETS[1:])]
    (total,) = call(total_body, [vmem((W, BLK), BF)], sums, 1_000_000)
    key_grad = swap(total).astype(F32).T

    mine, other = call(
        query_body,
        [vmem((ROWS, WIDE), BF), vmem((ROWS, WIDE), BF)],
        (ws, kt, e_mine, e_their),
        2_400_000_000,
    )
    qo = (turn(mine, 0).astype(F32) + turn(other, 1).astype(F32)).astype(BF)
    wide = HEADS * (DN + DV)
    gq, keep, send = call(
        tail_body,
        [vmem((NQ, HEADS * (DN + DR)), BF)] + [vmem((C // 2, wide), BF)] * 2,
        (scal, qo, both, latent_up),
        200_000_000,
        (pltpu.VMEM((C, wide), BF),),
        smem=1,
    )
    got = other_core(send)
    n = C // 8
    grad_weights = keep[:n].astype(F32) + got[:n].astype(F32)
    for k in range(1, 4):
        rows = slice(k * n, (k + 1) * n)
        pair = (keep[rows].astype(F32) + got[rows].astype(F32)).astype(BF)
        pair = lax.ppermute(pair, "x", [(i, (i + k) % 4) for i in range(4)])
        grad_weights = grad_weights + pair.astype(F32)
    back = lax.all_to_all(gq.reshape(ndev, own_q, HEADS * (DN + DR)), CTX, 0, 0, tiled=True)
    grad_queries = jnp.moveaxis(back, 0, 1).reshape(1, own_q, -1).astype(F32)
    return (grad_queries, key_grad[None], grad_weights)


def solution(mesh):
    finer = Mesh(mesh.devices.reshape(4, 2, NZ, NY), ("x", "core", "z", "y"))
    in_specs = (
        P(DP, CTX, None),
        P(DP, CTX, None),
        P(DP, CTX, None),
        P(None, CTX),
        P(DP),
        P(DP),
    )
    out_specs = (P(DP, CTX, None), P(DP, CTX, None), P(DP, CTX))
    return jax.shard_map(step, mesh=finer, in_specs=in_specs, out_specs=out_specs, check_vma=False)
```

profile of v0, /device:TPU:1, one launch (start us, length us, event | category | flops | bytes accessed | tf_op | source)
XLA Modules:
  0.0 188.8 jit_solution(7431626327871722694)
XLA Ops:
  0.7 6.2 %collective-permute-start.2 = (bf16[576,128]{1,0:T(8,128)(2,1)}, bf16[576,128]{1,0:T(8,128)(2,1)S(1)}, u32[]{:S(2)}, u32[]{:S(2)}) collective-permute-start(bf16[576,128]{1,0:T(8,128)(2,1)} %bitcast.21), channel_id=1, source_target_pairs={{0,0},{1,1},{2,33},{3,32},{32,3},{33,2},{34,34},{35,35},{4,4},{5,5... | collective-permute-start | bytes 442376 | tf_op jit(solution)/shard_map/ppermute | solution.py:55
  6.8 3.0 %collective-permute-done.2.refs_0_ = bf16[576,128]{1,0:T(8,128)(2,1)S(1)} collective-permute-done((bf16[576,128]{1,0:T(8,128)(2,1)}, bf16[576,128]{1,0:T(8,128)(2,1)S(1)}, u32[]{:S(2)}, u32[]{:S(2)}) %collective-permute-start.2) | collective-permute-done | bytes 147488 | tf_op jit(solution)/shard_map/ppermute | solution.py:55
  9.8 5.6 %collective-permute-start.9 = (bf16[576,128]{1,0:T(8,128)(2,1)S(1)}, bf16[576,128]{1,0:T(8,128)(2,1)S(1)}, u32[]{:S(2)}, u32[]{:S(2)}) collective-permute-start(bf16[576,128]{1,0:T(8,128)(2,1)S(1)} %collective-permute-done.2.refs_0_), channel_id=1, source_target_pairs={{0,28},{4,0},{8,4},{12,8},{16,12},{20,16},{24,20},{28,24},{1,29},{... | collective-permute-start | bytes 442376 | tf_op jit(solution)/shard_map/ppermute | solution.py:71
  15.4 1.9 %collective-permute-start.7 = (bf16[576,128]{1,0:T(8,128)(2,1)S(1)}, bf16[576,128]{1,0:T(8,128)(2,1)S(1)}, u32[]{:S(2)}, u32[]{:S(2)}) collective-permute-start(bf16[576,128]{1,0:T(8,128)(2,1)S(1)} %collective-permute-done.2.refs_0_), channel_id=1, source_target_pairs={{0,24},{4,28},{8,0},{12,4},{16,8},{20,12},{24,16},{28,20},{1,25},{... | collective-permute-start | bytes 442376 | tf_op jit(solution)/shard_map/ppermute | solution.py:71
  17.8 2.5 %collective-permute-start.5 = (bf16[576,128]{1,0:T(8,128)(2,1)S(1)}, bf16[576,128]{1,0:T(8,128)(2,1)S(1)}, u32[]{:S(2)}, u32[]{:S(2)}) collective-permute-start(bf16[576,128]{1,0:T(8,128)(2,1)S(1)} %collective-permute-done.2.refs_0_), channel_id=1, source_target_pairs={{0,20},{4,24},{8,28},{12,0},{16,4},{20,8},{24,12},{28,16},{1,21},{... | collective-permute-start | bytes 442376 | tf_op jit(solution)/shard_map/ppermute | solution.py:71
  20.3 0.8 collective-permute-done.9.refs_7_
  21.3 1.0 collective-permute-done.8.refs_6_
  22.3 6.3 %collective-permute-start.3 = (bf16[576,128]{1,0:T(8,128)(2,1)S(1)}, bf16[576,128]{1,0:T(8,128)(2,1)S(1)}, u32[]{:S(2)}, u32[]{:S(2)}) collective-permute-start(bf16[576,128]{1,0:T(8,128)(2,1)S(1)} %collective-permute-done.2.refs_0_), channel_id=1, source_target_pairs={{0,16},{4,20},{8,24},{12,28},{16,0},{20,4},{24,8},{28,12},{1,17},{... | collective-permute-start | bytes 442376 | tf_op jit(solution)/shard_map/ppermute | solution.py:71
  28.6 3.8 %collective-permute-done.6.refs_4_ = bf16[576,128]{1,0:T(8,128)(2,1)S(1)} collective-permute-done((bf16[576,128]{1,0:T(8,128)(2,1)S(1)}, bf16[576,128]{1,0:T(8,128)(2,1)S(1)}, u32[]{:S(2)}, u32[]{:S(2)}) %collective-permute-start.6) | collective-permute-done | bytes 147488 | tf_op jit(solution)/shard_map/ppermute | solution.py:71
  32.5 4.8 %collective-permute-done.5.refs_3_ = bf16[576,128]{1,0:T(8,128)(2,1)S(1)} collective-permute-done((bf16[576,128]{1,0:T(8,128)(2,1)S(1)}, bf16[576,128]{1,0:T(8,128)(2,1)S(1)}, u32[]{:S(2)}, u32[]{:S(2)}) %collective-permute-start.5) | collective-permute-done | bytes 147488 | tf_op jit(solution)/shard_map/ppermute | solution.py:71
  37.8 0.8 maximum_bitcast_fusion
  38.6 12.4 %all-to-all-start = ((bf16[32,2,1280]{2,1,0:T(2,128)(2,1)}), bf16[32,2,1280]{2,1,0:T(2,128)(2,1)S(1)}, u32[]{:S(2)}, u32[]{:S(2)}) async-start(bf16[32,2,1280]{2,1,0:T(2,128)(2,1)} %maximum_bitcast_fusion), calls=%async_computation | async-start | bytes 327680 | tf_op jit(solution)/shard_map/all_to_all | solution.py:302
  52.2 8.9 %all-to-all-done = bf16[32,2,1280]{2,1,0:T(2,128)(2,1)S(1)} async-done(((bf16[32,2,1280]{2,1,0:T(2,128)(2,1)}), bf16[32,2,1280]{2,1,0:T(2,128)(2,1)S(1)}, u32[]{:S(2)}, u32[]{:S(2)}) %all-to-all-start) | async-done | bytes 163872 | tf_op jit(solution)/shard_map/all_to_all | solution.py:302
  61.2 0.5 shard_map.85
  61.7 2.9 %collective-permute-start.1 = (bf16[256,1152]{1,0:T(8,128)(2,1)S(1)}, bf16[256,1152]{1,0:T(8,128)(2,1)}, u32[]{:S(2)}, u32[]{:S(2)}) collective-permute-start(bf16[256,1152]{1,0:T(8,128)(2,1)S(1)} %shard_map.85), channel_id=1, source_target_pairs={{0,1},{1,0},{2,33},{3,32},{32,3},{33,2},{34,35},{35,34},{4,5},{5,4... | collective-permute-start | bytes 1769480 | tf_op jit(solution)/shard_map/ppermute | solution.py:59
  64.6 1.9 %collective-permute-start = (bf16[256,1152]{1,0:T(8,128)(2,1)S(1)}, bf16[256,1152]{1,0:T(8,128)(2,1)}, u32[]{:S(2)}, u32[]{:S(2)}) collective-permute-start(bf16[256,1152]{1,0:T(8,128)(2,1)S(1)} %shard_map.85), channel_id=1, source_target_pairs={{0,0},{1,1},{2,32},{3,33},{32,2},{33,3},{34,34},{35,35},{4,4},{5,5... | collective-permute-start | bytes 1769480 | tf_op jit(solution)/shard_map/ppermute | solution.py:59
  66.6 12.2 %collective-permute-done.1.refs_2_.other = bf16[256,1152]{1,0:T(8,128)(2,1)} collective-permute-done((bf16[256,1152]{1,0:T(8,128)(2,1)S(1)}, bf16[256,1152]{1,0:T(8,128)(2,1)}, u32[]{:S(2)}, u32[]{:S(2)}) %collective-permute-start.1) | collective-permute-done | bytes 589856 | tf_op jit(solution)/shard_map/ppermute | solution.py:59
  78.7 16.8 %shard_map.87 = (bf16[1024,1024]{1,0:T(8,128)(2,1)S(1)}, bf16[1024,1024]{1,0:T(8,128)(2,1)S(1)}, bf16[576,2048]{1,0:T(8,128)(2,1)S(1)}, f32[512,128]{1,0:T(8,128)S(1)}) custom-call(s32[4]{0:T(128)S(1)} %pad_add_fusion.refs_0_.scal, bf16[256,1152]{1,0:T(8,128)(2,1)} %collective-permute-done.refs_1_.mine, ...), custom_call_target="tpu_custom_call" | custom-call | flops 2280000000 | bytes 10354704 | tf_op jit(solution)/shard_map/pallas_call | solution.py:87
  95.8 8.2 %collective-permute-done.11.their = f32[512,128]{1,0:T(8,128)S(1)} collective-permute-done((f32[512,128]{1,0:T(8,128)S(1)}, f32[512,128]{1,0:T(8,128)S(1)}, u32[]{:S(2)}, u32[]{:S(2)}) %collective-permute-start.11) | collective-permute-done | bytes 262176 | tf_op jit(solution)/shard_map/ppermute | solution.py:67
  104.0 5.1 %shard_map.88 = (bf16[1024,576]{1,0:T(8,128)(2,1)S(1)}, f32[512,128]{1,0:T(8,128)S(1)}, bf16[8,576,128]{2,1,0:T(8,128)(2,1)S(1)}) custom-call(f32[512,128]{1,0:T(8,128)S(1)} %get-tuple-element.32.st, f32[512,128]{1,0:T(8,128)S(1)} %collective-permute-done.11.their, bf16[256,1152]{1,0:T(8,128)(2,1)} %collective-permute-done.refs_1_.mine, ...), custom_call_target="tpu_custom_call" | custom-call | flops 1300000000 | bytes 6422528 | tf_op jit(solution)/shard_map/pallas_call | solution.py:87
  109.1 0.5 collective-permute-start.12
  109.6 1.7 shard_map.89.a
  111.3 0.7 collective-permute-done.12.b
  112.4 3.5 %shard_map.91 = (bf16[256,1152]{1,0:T(8,128)(2,1)S(1)}, bf16[256,1152]{1,0:T(8,128)(2,1)S(1)}) custom-call(f32[512,128]{1,0:T(8,128)S(1)} %get-tuple-element.46.ws, bf16[576,2048]{1,0:T(8,128)(2,1)S(1)} %get-tuple-element.47.kt, bf16[1024,1024]{1,0:T(8,128)(2,1)S(1)} %get-tuple-element.35.ee.e0, bf16[1024,1024]{1,0:T(8,128)(2,1)S(1)} %get-tuple-element.33.ee.e1), custom_call_target="tpu_custom_call" | custom-call | flops 2400000000 | bytes 7995392 | tf_op jit(solution)/shard_map/pallas_call | solution.py:87
  115.9 2.9 %collective-permute-start.13 = (bf16[256,1152]{1,0:T(8,128)(2,1)S(1)}, bf16[256,1152]{1,0:T(8,128)(2,1)S(1)}, u32[]{:S(2)}, u32[]{:S(2)}) collective-permute-start(bf16[256,1152]{1,0:T(8,128)(2,1)S(1)} %get-tuple-element.48), channel_id=1, source_target_pairs={{0,0},{1,1},{2,32},{3,33},{32,2},{33,3},{34,34},{35,35},{4,4},{5,5... | collective-permute-start | bytes 1769480 | tf_op jit(solution)/shard_map/ppermute | solution.py:59
  118.8 1.2 collective-permute-start.14
  120.0 12.8 %collective-permute-done.13 = bf16[256,1152]{1,0:T(8,128)(2,1)S(1)} collective-permute-done((bf16[256,1152]{1,0:T(8,128)(2,1)S(1)}, bf16[256,1152]{1,0:T(8,128)(2,1)S(1)}, u32[]{:S(2)}, u32[]{:S(2)}) %collective-permute-start.13) | collective-permute-done | bytes 589856 | tf_op jit(solution)/shard_map/ppermute | solution.py:59
  132.9 2.5 %collective-permute-done.14 = bf16[256,1152]{1,0:T(8,128)(2,1)S(1)} collective-permute-done((bf16[256,1152]{1,0:T(8,128)(2,1)S(1)}, bf16[256,1152]{1,0:T(8,128)(2,1)S(1)}, u32[]{:S(2)}, u32[]{:S(2)}) %collective-permute-start.14) | collective-permute-done | bytes 589856 | tf_op jit(solution)/shard_map/ppermute | solution.py:59
  135.5 1.2 shard_map.92
  136.8 0.5 collective-permute-start.15
  137.3 4.4 %collective-permute-start.16 = (bf16[576,128]{1,0:T(8,128)(2,1)S(1)}, bf16[576,128]{1,0:T(8,128)(2,1)S(1)}, u32[]{:S(2)}, u32[]{:S(2)}) collective-permute-start(bf16[576,128]{1,0:T(8,128)(2,1)S(1)} %get-tuple-element.53), channel_id=1, source_target_pairs={{0,20},{4,24},{8,28},{12,0},{16,4},{20,8},{24,12},{28,16},{1,21},{... | collective-permute-start | bytes 442376 | tf_op jit(solution)/shard_map/ppermute | solution.py:71
  141.7 3.3 %collective-permute-start.18 = (bf16[576,128]{1,0:T(8,128)(2,1)S(1)}, bf16[576,128]{1,0:T(8,128)(2,1)S(1)}, u32[]{:S(2)}, u32[]{:S(2)}) collective-permute-start(bf16[576,128]{1,0:T(8,128)(2,1)S(1)} %get-tuple-element.55), channel_id=1, source_target_pairs={{0,24},{4,28},{8,0},{12,4},{16,8},{20,12},{24,16},{28,20},{1,25},{... | collective-permute-start | bytes 442376 | tf_op jit(solution)/shard_map/ppermute | solution.py:71
  145.0 1.3 collective-permute-done.15.refs_1_
  146.3 3.1 %collective-permute-start.19 = (bf16[576,128]{1,0:T(8,128)(2,1)S(1)}, bf16[576,128]{1,0:T(8,128)(2,1)S(1)}, u32[]{:S(2)}, u32[]{:S(2)}) collective-permute-start(bf16[576,128]{1,0:T(8,128)(2,1)S(1)} %get-tuple-element.56), channel_id=1, source_target_pairs={{0,8},{4,12},{8,16},{12,20},{16,24},{20,28},{24,0},{28,4},{1,9},{5... | collective-permute-start | bytes 442376 | tf_op jit(solution)/shard_map/ppermute | solution.py:71
  149.3 0.8 collective-permute-done.16.refs_2_
  150.2 10.9 %collective-permute-start.20 = (bf16[576,128]{1,0:T(8,128)(2,1)S(1)}, bf16[576,128]{1,0:T(8,128)(2,1)S(1)}, u32[]{:S(2)}, u32[]{:S(2)}) collective-permute-start(bf16[576,128]{1,0:T(8,128)(2,1)S(1)} %get-tuple-element.57), channel_id=1, source_target_pairs={{0,28},{4,0},{8,4},{12,8},{16,12},{20,16},{24,20},{28,24},{1,29},{... | collective-permute-start | bytes 442376 | tf_op jit(solution)/shard_map/ppermute | solution.py:71
  161.1 2.3 %collective-permute-done.18.refs_4_ = bf16[576,128]{1,0:T(8,128)(2,1)S(1)} collective-permute-done((bf16[576,128]{1,0:T(8,128)(2,1)S(1)}, bf16[576,128]{1,0:T(8,128)(2,1)S(1)}, u32[]{:S(2)}, u32[]{:S(2)}) %collective-permute-start.18) | collective-permute-done | bytes 147488 | tf_op jit(solution)/shard_map/ppermute | solution.py:71
  163.3 3.1 %collective-permute-done.20.refs_6_ = bf16[576,128]{1,0:T(8,128)(2,1)S(1)} collective-permute-done((bf16[576,128]{1,0:T(8,128)(2,1)S(1)}, bf16[576,128]{1,0:T(8,128)(2,1)S(1)}, u32[]{:S(2)}, u32[]{:S(2)}) %collective-permute-start.20) | collective-permute-done | bytes 147488 | tf_op jit(solution)/shard_map/ppermute | solution.py:71
  166.6 6.7 %collective-permute-start.22 = (bf16[576,128]{1,0:T(8,128)(2,1)S(1)}, bf16[576,128]{1,0:T(8,128)(2,1)S(1)}, u32[]{:S(2)}, u32[]{:S(2)}) collective-permute-start(bf16[576,128]{1,0:T(8,128)(2,1)S(1)} %shard_map.93), channel_id=1, source_target_pairs={{0,0},{1,1},{2,33},{3,32},{32,3},{33,2},{34,34},{35,35},{4,4},{5,5... | collective-permute-start | bytes 442376 | tf_op jit(solution)/shard_map/ppermute | solution.py:55
  173.3 0.7 reshape.36
  174.0 3.9 %all-to-all-start.1 = ((bf16[32,2,768]{2,1,0:T(2,128)(2,1)}), bf16[32,2,768]{2,1,0:T(2,128)(2,1)S(1)}, u32[]{:S(2)}, u32[]{:S(2)}) async-start(bf16[32,2,768]{2,1,0:T(2,128)(2,1)} %reshape.36), calls=%async_computation.1 | async-start | bytes 196608 | tf_op jit(solution)/shard_map/all_to_all | solution.py:375
  178.0 1.3 collective-permute-start.24
  179.3 1.4 collective-permute-start.26
  180.7 1.5 collective-permute-start.25
  182.3 0.7 convert_bitcast_fusion
  183.0 4.3 %all-to-all-done.1 = bf16[32,2,768]{2,1,0:T(2,128)(2,1)S(1)} async-done(((bf16[32,2,768]{2,1,0:T(2,128)(2,1)}), bf16[32,2,768]{2,1,0:T(2,128)(2,1)S(1)}, u32[]{:S(2)}, u32[]{:S(2)}) %all-to-all-start.1) | async-done | bytes 98336 | tf_op jit(solution)/shard_map/all_to_all | solution.py:375
  187.3 0.7 convert_element_type.90
  188.0 0.8 convert_add_fusion
  (34 shorter events, 2.4 us)
Async XLA Ops:
  0.6 37.1 %copy-start.1 = (bf16[1,2,24576]{2,1,0:T(2,128)(2,1)S(1)}, bf16[1,2,24576]{2,1,0:T(2,128)(2,1)}, u32[]{:S(2)}) copy-start(bf16[1,2,24576]{2,1,0:T(2,128)(2,1)} %param.6) | copy-start | bytes 294916
  0.6 37.1 %copy-start.2 = (bf16[1,2,16384]{2,1,0:T(2,128)(2,1)S(1)}, bf16[1,2,16384]{2,1,0:T(2,128)(2,1)}, u32[]{:S(2)}) copy-start(bf16[1,2,16384]{2,1,0:T(2,128)(2,1)} %param.7) | copy-start | bytes 196612
  0.7 60.5 %copy-start = (bf16[512,1024]{1,0:T(8,128)(2,1)S(1)}, bf16[512,1024]{1,0:T(8,128)(2,1)}, u32[]{:S(2)}) copy-start(bf16[512,1024]{1,0:T(8,128)(2,1)} %w.3) | copy-start | bytes 3145732
  0.7 9.2 %collective-permute-start.2 = (bf16[576,128]{1,0:T(8,128)(2,1)}, bf16[576,128]{1,0:T(8,128)(2,1)S(1)}, u32[]{:S(2)}, u32[]{:S(2)}) collective-permute-start(bf16[576,128]{1,0:T(8,128)(2,1)} %bitcast.21), channel_id=1, source_target_pairs={{0,0},{1,1},{2,33},{3,32},{32,3},{33,2},{34,34},{35,35},{4,4},{5,5... | collective-permute-start | bytes 442376 | tf_op jit(solution)/shard_map/ppermute | solution.py:55
  9.8 11.2 %collective-permute-start.9 = (bf16[576,128]{1,0:T(8,128)(2,1)S(1)}, bf16[576,128]{1,0:T(8,128)(2,1)S(1)}, u32[]{:S(2)}, u32[]{:S(2)}) collective-permute-start(bf16[576,128]{1,0:T(8,128)(2,1)S(1)} %collective-permute-done.2.refs_0_), channel_id=1, source_target_pairs={{0,28},{4,0},{8,4},{12,8},{16,12},{20,16},{24,20},{28,24},{1,29},{... | collective-permute-start | bytes 442376 | tf_op jit(solution)/shard_map/ppermute | solution.py:71
  15.4 6.9 %collective-permute-start.8 = (bf16[576,128]{1,0:T(8,128)(2,1)S(1)}, bf16[576,128]{1,0:T(8,128)(2,1)S(1)}, u32[]{:S(2)}, u32[]{:S(2)}) collective-permute-start(bf16[576,128]{1,0:T(8,128)(2,1)S(1)} %collective-permute-done.2.refs_0_), channel_id=1, source_target_pairs={{0,4},{4,8},{8,12},{12,16},{16,20},{20,24},{24,28},{28,0},{1,5},{5... | collective-permute-start | bytes 442376 | tf_op jit(solution)/shard_map/ppermute | solution.py:71
  15.4 13.2 %collective-permute-start.7 = (bf16[576,128]{1,0:T(8,128)(2,1)S(1)}, bf16[576,128]{1,0:T(8,128)(2,1)S(1)}, u32[]{:S(2)}, u32[]{:S(2)}) collective-permute-start(bf16[576,128]{1,0:T(8,128)(2,1)S(1)} %collective-permute-done.2.refs_0_), channel_id=1, source_target_pairs={{0,24},{4,28},{8,0},{12,4},{16,8},{20,12},{24,16},{28,20},{1,25},{... | collective-permute-start | bytes 442376 | tf_op jit(solution)/shard_map/ppermute | solution.py:71
  17.3 15.1 %collective-permute-start.6 = (bf16[576,128]{1,0:T(8,128)(2,1)S(1)}, bf16[576,128]{1,0:T(8,128)(2,1)S(1)}, u32[]{:S(2)}, u32[]{:S(2)}) collective-permute-start(bf16[576,128]{1,0:T(8,128)(2,1)S(1)} %collective-permute-done.2.refs_0_), channel_id=1, source_target_pairs={{0,8},{4,12},{8,16},{12,20},{16,24},{20,28},{24,0},{28,4},{1,9},{5... | collective-permute-start | bytes 442376 | tf_op jit(solution)/shard_map/ppermute | solution.py:71
  17.8 19.5 %collective-permute-start.5 = (bf16[576,128]{1,0:T(8,128)(2,1)S(1)}, bf16[576,128]{1,0:T(8,128)(2,1)S(1)}, u32[]{:S(2)}, u32[]{:S(2)}) collective-permute-start(bf16[576,128]{1,0:T(8,128)(2,1)S(1)} %collective-permute-done.2.refs_0_), channel_id=1, source_target_pairs={{0,20},{4,24},{8,28},{12,0},{16,4},{20,8},{24,12},{28,16},{1,21},{... | collective-permute-start | bytes 442376 | tf_op jit(solution)/shard_map/ppermute | solution.py:71
  21.1 16.2 %collective-permute-start.4 = (bf16[576,128]{1,0:T(8,128)(2,1)S(1)}, bf16[576,128]{1,0:T(8,128)(2,1)S(1)}, u32[]{:S(2)}, u32[]{:S(2)}) collective-permute-start(bf16[576,128]{1,0:T(8,128)(2,1)S(1)} %collective-permute-done.2.refs_0_), channel_id=1, source_target_pairs={{0,12},{4,16},{8,20},{12,24},{16,28},{20,0},{24,4},{28,8},{1,13},{... | collective-permute-start | bytes 442376 | tf_op jit(solution)/shard_map/ppermute | solution.py:71
  22.3 15.0 %collective-permute-start.3 = (bf16[576,128]{1,0:T(8,128)(2,1)S(1)}, bf16[576,128]{1,0:T(8,128)(2,1)S(1)}, u32[]{:S(2)}, u32[]{:S(2)}) collective-permute-start(bf16[576,128]{1,0:T(8,128)(2,1)S(1)} %collective-permute-done.2.refs_0_), channel_id=1, source_target_pairs={{0,16},{4,20},{8,24},{12,28},{16,0},{20,4},{24,8},{28,12},{1,17},{... | collective-permute-start | bytes 442376 | tf_op jit(solution)/shard_map/ppermute | solution.py:71
  37.6 41.1 %collective-permute-start.10 = (bf16[576,1024]{1,0:T(8,128)(2,1)S(1)}, bf16[576,1024]{1,0:T(8,128)(2,1)}, u32[]{:S(2)}, u32[]{:S(2)}) collective-permute-start(bf16[576,1024]{1,0:T(8,128)(2,1)S(1)} %shard_map.86.refs_3_), channel_id=1, source_target_pairs={{0,32},{32,0},{1,33},{33,1},{2,34},{34,2},{3,35},{35,3},{4,36},{36... | collective-permute-start | bytes 3538952 | tf_op jit(solution)/shard_map/ppermute | solution.py:63
  38.6 22.6 %all-to-all-start = ((bf16[32,2,1280]{2,1,0:T(2,128)(2,1)}), bf16[32,2,1280]{2,1,0:T(2,128)(2,1)S(1)}, u32[]{:S(2)}, u32[]{:S(2)}) async-start(bf16[32,2,1280]{2,1,0:T(2,128)(2,1)} %maximum_bitcast_fusion), calls=%async_computation | async-start | bytes 327680 | tf_op jit(solution)/shard_map/all_to_all | solution.py:302
  61.7 17.0 %collective-permute-start.1 = (bf16[256,1152]{1,0:T(8,128)(2,1)S(1)}, bf16[256,1152]{1,0:T(8,128)(2,1)}, u32[]{:S(2)}, u32[]{:S(2)}) collective-permute-start(bf16[256,1152]{1,0:T(8,128)(2,1)S(1)} %shard_map.85), channel_id=1, source_target_pairs={{0,1},{1,0},{2,33},{3,32},{32,3},{33,2},{34,35},{35,34},{4,5},{5,4... | collective-permute-start | bytes 1769480 | tf_op jit(solution)/shard_map/ppermute | solution.py:59
  64.6 14.2 %collective-permute-start = (bf16[256,1152]{1,0:T(8,128)(2,1)S(1)}, bf16[256,1152]{1,0:T(8,128)(2,1)}, u32[]{:S(2)}, u32[]{:S(2)}) collective-permute-start(bf16[256,1152]{1,0:T(8,128)(2,1)S(1)} %shard_map.85), channel_id=1, source_target_pairs={{0,0},{1,1},{2,32},{3,33},{32,2},{33,3},{34,34},{35,35},{4,4},{5,5... | collective-permute-start | bytes 1769480 | tf_op jit(solution)/shard_map/ppermute | solution.py:59
  95.5 8.5 %collective-permute-start.11 = (f32[512,128]{1,0:T(8,128)S(1)}, f32[512,128]{1,0:T(8,128)S(1)}, u32[]{:S(2)}, u32[]{:S(2)}) collective-permute-start(f32[512,128]{1,0:T(8,128)S(1)} %get-tuple-element.32.st), channel_id=1, source_target_pairs={{0,1},{1,0},{2,3},{3,2},{4,5},{5,4},{6,7},{7,6},{8,9},{9,8},{10,11... | collective-permute-start | bytes 786440 | tf_op jit(solution)/shard_map/ppermute | solution.py:67
  109.1 2.9 %collective-permute-start.12 = (bf16[8,576,128]{2,1,0:T(8,128)(2,1)S(1)}, bf16[8,576,128]{2,1,0:T(8,128)(2,1)S(1)}, u32[]{:S(2)}, u32[]{:S(2)}) collective-permute-start(bf16[8,576,128]{2,1,0:T(8,128)(2,1)S(1)} %get-tuple-element.36), channel_id=1, source_target_pairs={{0,32},{32,0},{1,33},{33,1},{2,34},{34,2},{3,35},{35,3},{4,36},{36... | collective-permute-start | bytes 3538952 | tf_op jit(solution)/shard_map/ppermute | solution.py:63
  115.9 17.0 %collective-permute-start.13 = (bf16[256,1152]{1,0:T(8,128)(2,1)S(1)}, bf16[256,1152]{1,0:T(8,128)(2,1)S(1)}, u32[]{:S(2)}, u32[]{:S(2)}) collective-permute-start(bf16[256,1152]{1,0:T(8,128)(2,1)S(1)} %get-tuple-element.48), channel_id=1, source_target_pairs={{0,0},{1,1},{2,32},{3,33},{32,2},{33,3},{34,34},{35,35},{4,4},{5,5... | collective-permute-start | bytes 1769480 | tf_op jit(solution)/shard_map/ppermute | solution.py:59
  118.8 16.5 %collective-permute-start.14 = (bf16[256,1152]{1,0:T(8,128)(2,1)S(1)}, bf16[256,1152]{1,0:T(8,128)(2,1)S(1)}, u32[]{:S(2)}, u32[]{:S(2)}) collective-permute-start(bf16[256,1152]{1,0:T(8,128)(2,1)S(1)} %get-tuple-element.49), channel_id=1, source_target_pairs={{0,1},{1,0},{2,33},{3,32},{32,3},{33,2},{34,35},{35,34},{4,5},{5,4... | collective-permute-start | bytes 1769480 | tf_op jit(solution)/shard_map/ppermute | solution.py:59
  136.7 41.2 %collective-permute-start.23 = (bf16[256,1024]{1,0:T(8,128)(2,1)S(1)}, bf16[256,1024]{1,0:T(8,128)(2,1)S(1)}, u32[]{:S(2)}, u32[]{:S(2)}) collective-permute-start(bf16[256,1024]{1,0:T(8,128)(2,1)S(1)} %get-tuple-element.60), channel_id=1, source_target_pairs={{0,32},{32,0},{1,33},{33,1},{2,34},{34,2},{3,35},{35,3},{4,36},{36... | collective-permute-start | bytes 1572872 | tf_op jit(solution)/shard_map/ppermute | solution.py:63
  136.8 9.5 %collective-permute-start.15 = (bf16[576,128]{1,0:T(8,128)(2,1)S(1)}, bf16[576,128]{1,0:T(8,128)(2,1)S(1)}, u32[]{:S(2)}, u32[]{:S(2)}) collective-permute-start(bf16[576,128]{1,0:T(8,128)(2,1)S(1)} %get-tuple-element.52), channel_id=1, source_target_pairs={{0,16},{4,20},{8,24},{12,28},{16,0},{20,4},{24,8},{28,12},{1,17},{... | collective-permute-start | bytes 442376 | tf_op jit(solution)/shard_map/ppermute | solution.py:71
  137.3 12.9 %collective-permute-start.16 = (bf16[576,128]{1,0:T(8,128)(2,1)S(1)}, bf16[576,128]{1,0:T(8,128)(2,1)S(1)}, u32[]{:S(2)}, u32[]{:S(2)}) collective-permute-start(bf16[576,128]{1,0:T(8,128)(2,1)S(1)} %get-tuple-element.53), channel_id=1, source_target_pairs={{0,20},{4,24},{8,28},{12,0},{16,4},{20,8},{24,12},{28,16},{1,21},{... | collective-permute-start | bytes 442376 | tf_op jit(solution)/shard_map/ppermute | solution.py:71
  141.7 19.4 %collective-permute-start.17 = (bf16[576,128]{1,0:T(8,128)(2,1)S(1)}, bf16[576,128]{1,0:T(8,128)(2,1)S(1)}, u32[]{:S(2)}, u32[]{:S(2)}) collective-permute-start(bf16[576,128]{1,0:T(8,128)(2,1)S(1)} %get-tuple-element.54), channel_id=1, source_target_pairs={{0,12},{4,16},{8,20},{12,24},{16,28},{20,0},{24,4},{28,8},{1,13},{... | collective-permute-start | bytes 442376 | tf_op jit(solution)/shard_map/ppermute | solution.py:71
  141.7 21.6 %collective-permute-start.18 = (bf16[576,128]{1,0:T(8,128)(2,1)S(1)}, bf16[576,128]{1,0:T(8,128)(2,1)S(1)}, u32[]{:S(2)}, u32[]{:S(2)}) collective-permute-start(bf16[576,128]{1,0:T(8,128)(2,1)S(1)} %get-tuple-element.55), channel_id=1, source_target_pairs={{0,24},{4,28},{8,0},{12,4},{16,8},{20,12},{24,16},{28,20},{1,25},{... | collective-permute-start | bytes 442376 | tf_op jit(solution)/shard_map/ppermute | solution.py:71
  146.3 17.0 %collective-permute-start.19 = (bf16[576,128]{1,0:T(8,128)(2,1)S(1)}, bf16[576,128]{1,0:T(8,128)(2,1)S(1)}, u32[]{:S(2)}, u32[]{:S(2)}) collective-permute-start(bf16[576,128]{1,0:T(8,128)(2,1)S(1)} %get-tuple-element.56), channel_id=1, source_target_pairs={{0,8},{4,12},{8,16},{12,20},{16,24},{20,28},{24,0},{28,4},{1,9},{5... | collective-permute-start | bytes 442376 | tf_op jit(solution)/shard_map/ppermute | solution.py:71
  150.2 16.3 %collective-permute-start.20 = (bf16[576,128]{1,0:T(8,128)(2,1)S(1)}, bf16[576,128]{1,0:T(8,128)(2,1)S(1)}, u32[]{:S(2)}, u32[]{:S(2)}) collective-permute-start(bf16[576,128]{1,0:T(8,128)(2,1)S(1)} %get-tuple-element.57), channel_id=1, source_target_pairs={{0,28},{4,0},{8,4},{12,8},{16,12},{20,16},{24,20},{28,24},{1,29},{... | collective-permute-start | bytes 442376 | tf_op jit(solution)/shard_map/ppermute | solution.py:71
  161.1 5.4 %collective-permute-start.21 = (bf16[576,128]{1,0:T(8,128)(2,1)S(1)}, bf16[576,128]{1,0:T(8,128)(2,1)S(1)}, u32[]{:S(2)}, u32[]{:S(2)}) collective-permute-start(bf16[576,128]{1,0:T(8,128)(2,1)S(1)} %get-tuple-element.58), channel_id=1, source_target_pairs={{0,4},{4,8},{8,12},{12,16},{16,20},{20,24},{24,28},{28,0},{1,5},{5... | collective-permute-start | bytes 442376 | tf_op jit(solution)/shard_map/ppermute | solution.py:71
  166.6 15.7 %collective-permute-start.22 = (bf16[576,128]{1,0:T(8,128)(2,1)S(1)}, bf16[576,128]{1,0:T(8,128)(2,1)S(1)}, u32[]{:S(2)}, u32[]{:S(2)}) collective-permute-start(bf16[576,128]{1,0:T(8,128)(2,1)S(1)} %shard_map.93), channel_id=1, source_target_pairs={{0,0},{1,1},{2,33},{3,32},{32,3},{33,2},{34,34},{35,35},{4,4},{5,5... | collective-permute-start | bytes 442376 | tf_op jit(solution)/shard_map/ppermute | solution.py:55
  174.0 13.3 %all-to-all-start.1 = ((bf16[32,2,768]{2,1,0:T(2,128)(2,1)}), bf16[32,2,768]{2,1,0:T(2,128)(2,1)S(1)}, u32[]{:S(2)}, u32[]{:S(2)}) async-start(bf16[32,2,768]{2,1,0:T(2,128)(2,1)} %reshape.36), calls=%async_computation.1 | async-start | bytes 196608 | tf_op jit(solution)/shard_map/all_to_all | solution.py:375
  178.0 10.0 %collective-permute-start.24 = (bf16[64,1024]{1,0:T(8,128)(2,1)S(1)}, bf16[64,1024]{1,0:T(8,128)(2,1)S(1)}, u32[]{:S(2)}, u32[]{:S(2)}) collective-permute-start(bf16[64,1024]{1,0:T(8,128)(2,1)S(1)} %get-tuple-element.61), channel_id=1, source_target_pairs={{0,64},{64,128},{128,192},{192,0},{1,65},{65,129},{129,193},{193,1... | collective-permute-start | bytes 393224 | tf_op jit(solution)/shard_map/ppermute | solution.py:373
  179.3 8.7 %collective-permute-start.26 = (bf16[64,1024]{1,0:T(8,128)(2,1)S(1)}, bf16[64,1024]{1,0:T(8,128)(2,1)S(1)}, u32[]{:S(2)}, u32[]{:S(2)}) collective-permute-start(bf16[64,1024]{1,0:T(8,128)(2,1)S(1)} %get-tuple-element.62), channel_id=1, source_target_pairs={{0,192},{64,0},{128,64},{192,128},{1,193},{65,1},{129,65},{193,129... | collective-permute-start | bytes 393224 | tf_op jit(solution)/shard_map/ppermute | solution.py:373
  180.7 7.3 %collective-permute-start.25 = (bf16[64,1024]{1,0:T(8,128)(2,1)S(1)}, bf16[64,1024]{1,0:T(8,128)(2,1)S(1)}, u32[]{:S(2)}, u32[]{:S(2)}) collective-permute-start(bf16[64,1024]{1,0:T(8,128)(2,1)S(1)} %get-tuple-element.63), channel_id=1, source_target_pairs={{0,128},{64,192},{128,0},{192,64},{1,129},{65,193},{129,1},{193,65... | collective-permute-start | bytes 393224 | tf_op jit(solution)/shard_map/ppermute | solution.py:373
where the time goes:
time: 189 us
  starting transfers between devices  82.4 us (44%)
  waiting for transfers between devices  70.5 us (37%)
  Pallas kernels  29.6 us (16%)
  other arithmetic  3.43 us (2%)
  between operations  2.16 us (1%)
    ppermute x14, starting transfers between devices, along_z(): return lax.ppermute(v, 'z', [(i, (i + step) % NZ) for i in range(NZ)])  39.2 us
    pallas_call x9, Pallas kernels, call(): pl.pallas_call(body, out_shape=out_shape, in_specs=specs, out_specs=[pl.B...  29.6 us
    ppermute x4, waiting for transfers between devices, turn(): return lax.ppermute(v, ('core', 'y'), turned(flip))  27.5 us
    ppermute x14, waiting for transfers between devices, along_z(): return lax.ppermute(v, 'z', [(i, (i + step) % NZ) for i in range(NZ)])  17.9 us
    ppermute x2, starting transfers between devices, swap(): return lax.ppermute(v, ('core', 'y'), swap_pairs())  12.9 us
    all_to_all x1, starting transfers between devices, step(): both = lax.all_to_all(both, CTX, 0, 0, tiled=True)  12.4 us
    ppermute x4, starting transfers between devices, turn(): return lax.ppermute(v, ('core', 'y'), turned(flip))  8.91 us
    all_to_all x1, waiting for transfers between devices, step(): both = lax.all_to_all(both, CTX, 0, 0, tiled=True)  8.9 us
  transfers between devices with their start and end apart: 29, of which 16 were waited for; matrix products, arithmetic and copies ran while one was open for 2% of the time, Pallas kernels for 1%

commit v1 on v0

--- a/solution.py
+++ b/solution.py
@@ -124,10 +124,21 @@
 def scores_body(*refs):
     scal, mine, other = refs[:3]
     keys = refs[3:5]
-    e_mine, e_their, kt, stats, s_ref, gp_ref = refs[5:]
+    e_mine, e_their, kt, stats, s_ref, gp_ref, wide = refs[5:]
     z, y_own = scal[0], scal[1]
     for n in range(2):
         kt[:, n * NZ * BLK : (n + 1) * NZ * BLK] = keys[n][...]
+    note = mine[0:16, 2 * C :].astype(F32).astype(jnp.int32)[0:8, :]
+    start = note[:, DR : DR + 1] * NQ + note[:, DR + 1 : DR + 2]
+    low = note[:, DR + 2 : DR + 3] * NQ + note[:, DR + 3 : DR + 4]
+    lane = lax.broadcasted_iota(jnp.int32, (8, BLK), 1)
+    sub = lax.broadcasted_iota(jnp.int32, (8, BLK), 0)
+    above = lane - low
+    ahead = lane - start - sub
+    base = []
+    for y in (y_own, 3 - y_own):
+        for d in OFFSETS:
+            base.append(((z + d + NZ) % NZ) * (NY * BLK) + y * BLK)
     for half, qg in ((0, mine), (1, other)):
         rows = slice(half * ROWS, (half + 1) * ROWS)
         q = qg[:, C : C + W]
@@ -136,51 +147,49 @@
             cols = slice(t * TILE, (t + 1) * TILE)
             s_ref[rows, cols] = dot(q, kt[:, cols])
             gp_ref[rows, cols] = dot(g, kt[:C, cols])
-    step = 16
-    lane = lax.broadcasted_iota(jnp.int32, (step, BLK), 1)
-    sub = lax.broadcasted_iota(jnp.int32, (step, 1), 0)
-    pos = []
-    for y in (y_own, 3 - y_own):
-        for d in OFFSETS:
-            pos.append(((z + d + NZ) % NZ) * (NY * BLK) + y * BLK + lane)
-
-    @pl.loop(0, 2 * ROWS // step)
+    chunk = NQ
+
+    @pl.loop(0, 2 * ROWS // chunk)
     def _(i):
-        r0 = pl.multiple_of(i * step, step)
-        here = pl.ds(r0, step)
-        below = pl.ds(pl.multiple_of(2 * ROWS + r0, step), step)
-        note = mine[pl.ds(pl.multiple_of(lax.rem(r0, ROWS), step), step), 2 * C :].astype(F32)
-        note = note.astype(jnp.int32)
-        start = note[:, DR : DR + 1] * NQ + note[:, DR + 1 : DR + 2]
-        low = note[:, DR + 2 : DR + 3] * NQ + note[:, DR + 3 : DR + 4]
-        last = start + lax.rem(r0, NQ) + sub
-        peak = None
+        r0 = pl.multiple_of(i * chunk, chunk)
+        here = pl.ds(r0, chunk)
+        below = pl.ds(pl.multiple_of(2 * ROWS + r0, chunk), chunk)
+        peak = [None] * (chunk // 8)
         for b in range(16):
             cols = slice(b * BLK, (b + 1) * BLK)
-            ok = (pos[b] >= low) & (pos[b] <= last)
-            v = jnp.where(ok, s_ref[here, cols] * SCALE, NEG_FILL)
-            s_ref[here, cols] = v
-            peak = v if peak is None else jnp.maximum(peak, v)
-        m = jnp.max(peak, axis=1, keepdims=True)
-        total = jnp.zeros((step, BLK), F32)
-        rsum = jnp.zeros((step, BLK), F32)
+            inside = above + base[b] >= 0
+            gap = ahead + base[b]
+            for k in range(chunk // 8):
+                r = pl.ds(pl.multiple_of(r0 + 8 * k, 8), 8)
+                ok = inside & (gap <= 8 * k)
+                v = jnp.where(ok, s_ref[r, cols] * SCALE, NEG_FILL)
+                s_ref[r, cols] = v
+                peak[k] = v if peak[k] is None else jnp.maximum(peak[k], v)
+        m = jnp.max(jnp.concatenate(peak, axis=0), axis=1, keepdims=True)
+        safe = jnp.broadcast_to(jnp.maximum(m, 0.1 * NEG_FILL), (chunk, BLK))
+        total = None
+        rsum = None
         for b in range(16):
             cols = slice(b * BLK, (b + 1) * BLK)
-            v = s_ref[here, cols]
-            e = jnp.where(v > 0.5 * NEG_FILL, jnp.exp(v - m), 0.0)
+            e = jnp.exp(s_ref[here, cols] - safe)
             s_ref[here, cols] = e
-            total = total + e
-            rsum = rsum + e * gp_ref[here, cols]
+            p = e * gp_ref[here, cols]
+            total = e if total is None else total + e
+            rsum = p if rsum is None else rsum + p
         l = jnp.sum(total, axis=1, keepdims=True)
         rd = jnp.sum(rsum, axis=1, keepdims=True) / jnp.where(l > 0.0, l, 1.0)
+        rdb = jnp.broadcast_to(rd, (chunk, BLK))
         for b in range(16):
             cols = slice(b * BLK, (b + 1) * BLK)
             out = e_mine if b < 8 else e_their
             oc = slice((b % 8) * BLK, (b % 8 + 1) * BLK)
             e = s_ref[here, cols]
-            out[here, oc] = (e * (gp_ref[here, cols] - rd)).astype(BF)
+            out[here, oc] = (e * (gp_ref[here, cols] - rdb)).astype(BF)
             out[below, oc] = e.astype(BF)
-        stats[here, :] = jnp.where(lane == 0, m, jnp.where(lane == 1, l, rd))
+        col = lax.broadcasted_iota(jnp.int32, (chunk, BLK), 1)
+        wide[here, :] = jnp.where(col == 0, m, jnp.where(col == 1, l, rd))
+
+    stats[...] = jnp.transpose(wide[...])[0:8, :]
 
 
 def key_parts(qq, ee, out):
@@ -203,37 +212,35 @@
 
 
 def first_body(st, their, mine, other, ee, qq, ws, out):
+    there = jnp.concatenate([their[:, ROWS:], their[:, :ROWS]], axis=1)
+    m, l, rd = st[0:1, :], st[1:2, :], st[2:3, :]
+    m2, l2, rd2 = there[0:1, :], there[1:2, :], there[2:3, :]
+    top = jnp.maximum(m, m2)
+    a = jnp.exp(m - top)
+    a2 = jnp.exp(m2 - top)
+    denom = l * a + l2 * a2
+    shift = (rd * l * a + rd2 * l2 * a2) / denom - rd
+    w = a / denom
+    row = lax.broadcasted_iota(jnp.int32, (BLK, 2 * ROWS), 0)
+    ws[...] = jnp.transpose(jnp.where(row == 0, w, shift))
     step = 64
-
-    def body(rows, trows, qg, qrows):
-        m, l, rd = st[rows, 0:1], st[rows, 1:2], st[rows, 2:3]
-        m2, l2, rd2 = their[trows, 0:1], their[trows, 1:2], their[trows, 2:3]
-        top = jnp.maximum(m, m2)
-        a = jnp.exp(m - top)
-        a2 = jnp.exp(m2 - top)
-        denom = l * a + l2 * a2
-        shift = (rd * l * a + rd2 * l2 * a2) / denom - rd
-        w = a / denom
-        sw = SCALE * w
-        q = qg[qrows, C : C + W].astype(F32)
-        g = qg[qrows, :C].astype(F32)
-        qs = q * sw
-        qq[rows, :] = qs.astype(BF)
-        qd = qs * shift
-        low_rows = pl.ds(pl.multiple_of(rows.start + 2 * ROWS, step), step)
-        qq[low_rows, :C] = (g * w - qd[:, :C]).astype(BF)
-        qq[low_rows, C:] = (-qd[:, C:]).astype(BF)
-        lane = lax.broadcasted_iota(jnp.int32, (step, BLK), 1)
-        ws[rows, :] = jnp.where(lane == 0, w, shift)
-
     for half, qg in ((0, mine), (1, other)):
 
         @pl.loop(0, ROWS // step)
         def _(i):
             r = pl.multiple_of(i * step, step)
-            mine_at = pl.multiple_of(half * ROWS + r, step)
-            their_at = pl.multiple_of((1 - half) * ROWS + r, step)
-            body(pl.ds(mine_at, step), pl.ds(their_at, step), qg, pl.ds(r, step))
+            at = pl.multiple_of(half * ROWS + r, step)
+            rows = pl.ds(at, step)
+            below = pl.ds(pl.multiple_of(at + 2 * ROWS, step), step)
+            wv = ws[rows, 0:1]
+            dv = ws[rows, 1:2]
+            q = qg[pl.ds(r, step), C : C + W].astype(F32)
+            g = qg[pl.ds(r, step), :C].astype(F32)
+            qs = q * (SCALE * wv)
+            qq[rows, :] = qs.astype(BF)
+            qd = qs * dv
+            qq[below, :C] = (g * wv - qd[:, :C]).astype(BF)
+            qq[below, C:] = (-qd[:, C:]).astype(BF)
 
     key_parts(qq, ee, out)
 
@@ -325,10 +332,10 @@
     big = pltpu.VMEM((2 * ROWS, KEYS), F32)
     e_mine, e_their, kt, stats = call(
         scores_body,
-        [half, half, vmem((W, KEYS), BF), vmem((2 * ROWS, BLK), F32)],
+        [half, half, vmem((W, KEYS), BF), vmem((8, 2 * ROWS), F32)],
         (scal, qg_mine, qg_other, mine_side, their_side),
         2_280_000_000,
-        (big, big),
+        (big, big, pltpu.VMEM((2 * ROWS, BLK), F32)),
         smem=1,
     )
     theirs = pair_y(stats)
@@ -344,8 +351,10 @@
     (mine_keys,) = call(parts_body, [piece], (qq, e_mine), 1_200_000_000)
     sums = call(add_body, [vmem((W, BLK), BF)] * NZ, (mine_keys, their_keys), 1_000_000)
     sums, ws = lax.optimization_barrier((sums, ws))
-    sums = [sums[0]] + [along_z(sums[n + 1], d) for n, d in enumerate(OFFSETS[1:])]
-    (total,) = call(total_body, [vmem((W, BLK), BF)], sums, 1_000_000)
+    moved = [sums[0]]
+    for n, d in enumerate(OFFSETS[1:]):
+        moved.append(along_z(sums[n + 1], d))
+    (total,) = call(total_body, [vmem((W, BLK), BF)], moved, 1_000_000)
     key_grad = swap(total).astype(F32).T
 
     mine, other = call(
@@ -354,7 +363,8 @@
         (ws, kt, e_mine, e_their),
         2_400_000_000,
     )
-    qo = (turn(mine, 0).astype(F32) + turn(other, 1).astype(F32)).astype(BF)
+    mine, other = turn(mine, 0), turn(other, 1)
+    qo = (mine.astype(F32) + other.astype(F32)).astype(BF)
     wide = HEADS * (DN + DV)
     gq, keep, send = call(
         tail_body,

time: 189 us -> 179 us (0.947)
  Pallas kernels: 29.6 us -> 22.4 us
  waiting for transfers between devices: 70.5 us -> 67.4 us
    pallas_call x9, Pallas kernels: 29.6 us -> 22.4 us  [call(): pl.pallas_call(body, out_shape=out_shape, in_specs=specs, out_specs=[pl.B...]
    ppermute x1, waiting for transfers between devices: 8.18 us -> 2.92 us  [pair_y(): return lax.ppermute(v, 'y', [(i, i ^ 1) for i in range(NY)])]
    ppermute x14, waiting for transfers between devices: 17.9 us -> 20.6 us  [along_z(): return lax.ppermute(v, 'z', [(i, (i + step) % NZ) for i in range(NZ)])]
    ppermute x14, starting transfers between devices: 39.2 us -> 36.8 us  [along_z(): return lax.ppermute(v, 'z', [(i, (i + step) % NZ) for i in range(NZ)])]
    ppermute x4, starting transfers between devices: 8.91 us -> 11 us  [turn(): return lax.ppermute(v, ('core', 'y'), turned(flip))]
where the time goes in v1:
time: 179 us; the launch traced here: 178 us
  starting transfers between devices  82.2 us (46%)
  waiting for transfers between devices  67.4 us (38%)
  Pallas kernels  22.4 us (13%)
  other arithmetic  3.43 us (2%)
  between operations  2.16 us (1%)
    ppermute x14, starting transfers between devices, along_z(): return lax.ppermute(v, 'z', [(i, (i + step) % NZ) for i in range(NZ)])  36.8 us
    ppermute x4, waiting for transfers between devices, turn(): return lax.ppermute(v, ('core', 'y'), turned(flip))  26.9 us
    pallas_call x9, Pallas kernels, call(): pl.pallas_call(body, out_shape=out_shape, in_specs=specs, out_specs=[pl.B...  22.4 us
    ppermute x14, waiting for transfers between devices, along_z(): return lax.ppermute(v, 'z', [(i, (i + step) % NZ) for i in range(NZ)])  20.6 us
    ppermute x2, starting transfers between devices, swap(): return lax.ppermute(v, ('core', 'y'), swap_pairs())  13 us
    all_to_all x1, starting transfers between devices, step(): both = lax.all_to_all(both, CTX, 0, 0, tiled=True)  12.4 us
    ppermute x4, starting transfers between devices, turn(): return lax.ppermute(v, ('core', 'y'), turned(flip))  11 us
    all_to_all x1, waiting for transfers between devices, step(): both = lax.all_to_all(both, CTX, 0, 0, tiled=True)  8.9 us
  transfers between devices with their start and end apart: 29, of which 16 were waited for; matrix products, arithmetic and copies ran while one was open for 2% of the time, Pallas kernels for 1%

profile of v1, /device:TPU:1, one launch (start us, length us, event | category | flops | bytes accessed | tf_op | source)
XLA Modules:
  0.0 178.4 jit_solution(4299223454331055849)
XLA Ops:
  0.7 6.2 %collective-permute-start.2 = (bf16[576,128]{1,0:T(8,128)(2,1)}, bf16[576,128]{1,0:T(8,128)(2,1)S(1)}, u32[]{:S(2)}, u32[]{:S(2)}) collective-permute-start(bf16[576,128]{1,0:T(8,128)(2,1)} %bitcast.21), channel_id=1, source_target_pairs={{0,0},{1,1},{2,33},{3,32},{32,3},{33,2},{34,34},{35,35},{4,4},{5,5... | collective-permute-start | bytes 442376 | tf_op jit(solution)/shard_map/ppermute | solution.py:55
  6.8 3.0 %collective-permute-done.2.refs_0_ = bf16[576,128]{1,0:T(8,128)(2,1)S(1)} collective-permute-done((bf16[576,128]{1,0:T(8,128)(2,1)}, bf16[576,128]{1,0:T(8,128)(2,1)S(1)}, u32[]{:S(2)}, u32[]{:S(2)}) %collective-permute-start.2) | collective-permute-done | bytes 147488 | tf_op jit(solution)/shard_map/ppermute | solution.py:55
  9.8 5.6 %collective-permute-start.9 = (bf16[576,128]{1,0:T(8,128)(2,1)S(1)}, bf16[576,128]{1,0:T(8,128)(2,1)S(1)}, u32[]{:S(2)}, u32[]{:S(2)}) collective-permute-start(bf16[576,128]{1,0:T(8,128)(2,1)S(1)} %collective-permute-done.2.refs_0_), channel_id=1, source_target_pairs={{0,28},{4,0},{8,4},{12,8},{16,12},{20,16},{24,20},{28,24},{1,29},{... | collective-permute-start | bytes 442376 | tf_op jit(solution)/shard_map/ppermute | solution.py:71
  15.4 1.9 %collective-permute-start.7 = (bf16[576,128]{1,0:T(8,128)(2,1)S(1)}, bf16[576,128]{1,0:T(8,128)(2,1)S(1)}, u32[]{:S(2)}, u32[]{:S(2)}) collective-permute-start(bf16[576,128]{1,0:T(8,128)(2,1)S(1)} %collective-permute-done.2.refs_0_), channel_id=1, source_target_pairs={{0,24},{4,28},{8,0},{12,4},{16,8},{20,12},{24,16},{28,20},{1,25},{... | collective-permute-start | bytes 442376 | tf_op jit(solution)/shard_map/ppermute | solution.py:71
  17.8 2.5 %collective-permute-start.5 = (bf16[576,128]{1,0:T(8,128)(2,1)S(1)}, bf16[576,128]{1,0:T(8,128)(2,1)S(1)}, u32[]{:S(2)}, u32[]{:S(2)}) collective-permute-start(bf16[576,128]{1,0:T(8,128)(2,1)S(1)} %collective-permute-done.2.refs_0_), channel_id=1, source_target_pairs={{0,20},{4,24},{8,28},{12,0},{16,4},{20,8},{24,12},{28,16},{1,21},{... | collective-permute-start | bytes 442376 | tf_op jit(solution)/shard_map/ppermute | solution.py:71
  20.3 0.8 collective-permute-done.9.refs_7_
  21.3 1.0 collective-permute-done.8.refs_6_
  22.3 6.3 %collective-permute-start.3 = (bf16[576,128]{1,0:T(8,128)(2,1)S(1)}, bf16[576,128]{1,0:T(8,128)(2,1)S(1)}, u32[]{:S(2)}, u32[]{:S(2)}) collective-permute-start(bf16[576,128]{1,0:T(8,128)(2,1)S(1)} %collective-permute-done.2.refs_0_), channel_id=1, source_target_pairs={{0,16},{4,20},{8,24},{12,28},{16,0},{20,4},{24,8},{28,12},{1,17},{... | collective-permute-start | bytes 442376 | tf_op jit(solution)/shard_map/ppermute | solution.py:71
  28.6 3.8 %collective-permute-done.6.refs_4_ = bf16[576,128]{1,0:T(8,128)(2,1)S(1)} collective-permute-done((bf16[576,128]{1,0:T(8,128)(2,1)S(1)}, bf16[576,128]{1,0:T(8,128)(2,1)S(1)}, u32[]{:S(2)}, u32[]{:S(2)}) %collective-permute-start.6) | collective-permute-done | bytes 147488 | tf_op jit(solution)/shard_map/ppermute | solution.py:71
  32.5 4.8 %collective-permute-done.5.refs_3_ = bf16[576,128]{1,0:T(8,128)(2,1)S(1)} collective-permute-done((bf16[576,128]{1,0:T(8,128)(2,1)S(1)}, bf16[576,128]{1,0:T(8,128)(2,1)S(1)}, u32[]{:S(2)}, u32[]{:S(2)}) %collective-permute-start.5) | collective-permute-done | bytes 147488 | tf_op jit(solution)/shard_map/ppermute | solution.py:71
  37.8 0.8 maximum_bitcast_fusion
  38.6 12.4 %all-to-all-start = ((bf16[32,2,1280]{2,1,0:T(2,128)(2,1)}), bf16[32,2,1280]{2,1,0:T(2,128)(2,1)S(1)}, u32[]{:S(2)}, u32[]{:S(2)}) async-start(bf16[32,2,1280]{2,1,0:T(2,128)(2,1)} %maximum_bitcast_fusion), calls=%async_computation | async-start | bytes 327680 | tf_op jit(solution)/shard_map/all_to_all | solution.py:309
  52.2 8.9 %all-to-all-done = bf16[32,2,1280]{2,1,0:T(2,128)(2,1)S(1)} async-done(((bf16[32,2,1280]{2,1,0:T(2,128)(2,1)}), bf16[32,2,1280]{2,1,0:T(2,128)(2,1)S(1)}, u32[]{:S(2)}, u32[]{:S(2)}) %all-to-all-start) | async-done | bytes 163872 | tf_op jit(solution)/shard_map/all_to_all | solution.py:309
  61.2 0.5 shard_map.85
  61.7 2.9 %collective-permute-start.1 = (bf16[256,1152]{1,0:T(8,128)(2,1)S(1)}, bf16[256,1152]{1,0:T(8,128)(2,1)}, u32[]{:S(2)}, u32[]{:S(2)}) collective-permute-start(bf16[256,1152]{1,0:T(8,128)(2,1)S(1)} %shard_map.85), channel_id=1, source_target_pairs={{0,1},{1,0},{2,33},{3,32},{32,3},{33,2},{34,35},{35,34},{4,5},{5,4... | collective-permute-start | bytes 1769480 | tf_op jit(solution)/shard_map/ppermute | solution.py:59
  64.6 1.9 %collective-permute-start = (bf16[256,1152]{1,0:T(8,128)(2,1)S(1)}, bf16[256,1152]{1,0:T(8,128)(2,1)}, u32[]{:S(2)}, u32[]{:S(2)}) collective-permute-start(bf16[256,1152]{1,0:T(8,128)(2,1)S(1)} %shard_map.85), channel_id=1, source_target_pairs={{0,0},{1,1},{2,32},{3,33},{32,2},{33,3},{34,34},{35,35},{4,4},{5,5... | collective-permute-start | bytes 1769480 | tf_op jit(solution)/shard_map/ppermute | solution.py:59
  66.6 12.2 %collective-permute-done.1.refs_2_.other = bf16[256,1152]{1,0:T(8,128)(2,1)} collective-permute-done((bf16[256,1152]{1,0:T(8,128)(2,1)S(1)}, bf16[256,1152]{1,0:T(8,128)(2,1)}, u32[]{:S(2)}, u32[]{:S(2)}) %collective-permute-start.1) | collective-permute-done | bytes 589856 | tf_op jit(solution)/shard_map/ppermute | solution.py:59
  78.7 10.8 %shard_map.87 = (bf16[1024,1024]{1,0:T(8,128)(2,1)S(1)}, bf16[1024,1024]{1,0:T(8,128)(2,1)S(1)}, bf16[576,2048]{1,0:T(8,128)(2,1)S(1)}, f32[8,512]{1,0:T(8,128)S(1)}) custom-call(s32[4]{0:T(128)S(1)} %pad_add_fusion.refs_0_.scal, bf16[256,1152]{1,0:T(8,128)(2,1)} %collective-permute-done.refs_1_.mine, ...), custom_call_target="tpu_custom_call" | custom-call | flops 2280000000 | bytes 10108944 | tf_op jit(solution)/shard_map/pallas_call | solution.py:87
  89.8 2.9 %collective-permute-done.11.their = f32[8,512]{1,0:T(8,128)S(1)} collective-permute-done((f32[8,512]{1,0:T(8,128)S(1)}, f32[8,512]{1,0:T(8,128)S(1)}, u32[]{:S(2)}, u32[]{:S(2)}) %collective-permute-start.11) | collective-permute-done | bytes 16416 | tf_op jit(solution)/shard_map/ppermute | solution.py:67
  92.7 4.0 %shard_map.88 = (bf16[1024,576]{1,0:T(8,128)(2,1)S(1)}, f32[512,128]{1,0:T(8,128)S(1)}, bf16[8,576,128]{2,1,0:T(8,128)(2,1)S(1)}) custom-call(f32[8,512]{1,0:T(8,128)S(1)} %get-tuple-element.32.st, f32[8,512]{1,0:T(8,128)S(1)} %collective-permute-done.11.their, bf16[256,1152]{1,0:T(8,128)(2,1)} %collective-permute-done.refs_1_.mine, ...), custom_call_target="tpu_custom_call" | custom-call | flops 1300000000 | bytes 5931008 | tf_op jit(solution)/shard_map/pallas_call | solution.py:87
  96.7 0.5 collective-permute-start.12
  97.2 1.7 shard_map.89.a
  98.9 0.7 collective-permute-done.12.b
  99.9 3.5 %shard_map.91 = (bf16[256,1152]{1,0:T(8,128)(2,1)S(1)}, bf16[256,1152]{1,0:T(8,128)(2,1)S(1)}) custom-call(f32[512,128]{1,0:T(8,128)S(1)} %get-tuple-element.46.ws, bf16[576,2048]{1,0:T(8,128)(2,1)S(1)} %get-tuple-element.47.kt, bf16[1024,1024]{1,0:T(8,128)(2,1)S(1)} %get-tuple-element.35.ee.e0, bf16[1024,1024]{1,0:T(8,128)(2,1)S(1)} %get-tuple-element.33.ee.e1), custom_call_target="tpu_custom_call" | custom-call | flops 2400000000 | bytes 7995392 | tf_op jit(solution)/shard_map/pallas_call | solution.py:87
  103.5 5.6 %collective-permute-start.13 = (bf16[256,1152]{1,0:T(8,128)(2,1)S(1)}, bf16[256,1152]{1,0:T(8,128)(2,1)S(1)}, u32[]{:S(2)}, u32[]{:S(2)}) collective-permute-start(bf16[256,1152]{1,0:T(8,128)(2,1)S(1)} %get-tuple-element.48), channel_id=1, source_target_pairs={{0,0},{1,1},{2,32},{3,33},{32,2},{33,3},{34,34},{35,35},{4,4},{5,5... | collective-permute-start | bytes 1769480 | tf_op jit(solution)/shard_map/ppermute | solution.py:59
  109.0 0.7 collective-permute-start.14
  109.7 13.1 %collective-permute-done.13 = bf16[256,1152]{1,0:T(8,128)(2,1)S(1)} collective-permute-done((bf16[256,1152]{1,0:T(8,128)(2,1)S(1)}, bf16[256,1152]{1,0:T(8,128)(2,1)S(1)}, u32[]{:S(2)}, u32[]{:S(2)}) %collective-permute-start.13) | collective-permute-done | bytes 589856 | tf_op jit(solution)/shard_map/ppermute | solution.py:59
  122.8 1.6 collective-permute-done.14
  124.5 1.2 shard_map.92
  125.8 1.0 collective-permute-start.15
  126.8 4.0 %collective-permute-start.16 = (bf16[576,128]{1,0:T(8,128)(2,1)S(1)}, bf16[576,128]{1,0:T(8,128)(2,1)S(1)}, u32[]{:S(2)}, u32[]{:S(2)}) collective-permute-start(bf16[576,128]{1,0:T(8,128)(2,1)S(1)} %get-tuple-element.53), channel_id=1, source_target_pairs={{0,20},{4,24},{8,28},{12,0},{16,4},{20,8},{24,12},{28,16},{1,21},{... | collective-permute-start | bytes 442376 | tf_op jit(solution)/shard_map/ppermute | solution.py:71
  130.8 3.5 %collective-permute-start.18 = (bf16[576,128]{1,0:T(8,128)(2,1)S(1)}, bf16[576,128]{1,0:T(8,128)(2,1)S(1)}, u32[]{:S(2)}, u32[]{:S(2)}) collective-permute-start(bf16[576,128]{1,0:T(8,128)(2,1)S(1)} %get-tuple-element.55), channel_id=1, source_target_pairs={{0,24},{4,28},{8,0},{12,4},{16,8},{20,12},{24,16},{28,20},{1,25},{... | collective-permute-start | bytes 442376 | tf_op jit(solution)/shard_map/ppermute | solution.py:71
  134.4 1.3 collective-permute-done.15.refs_1_
  135.6 3.2 %collective-permute-start.19 = (bf16[576,128]{1,0:T(8,128)(2,1)S(1)}, bf16[576,128]{1,0:T(8,128)(2,1)S(1)}, u32[]{:S(2)}, u32[]{:S(2)}) collective-permute-start(bf16[576,128]{1,0:T(8,128)(2,1)S(1)} %get-tuple-element.56), channel_id=1, source_target_pairs={{0,8},{4,12},{8,16},{12,20},{16,24},{20,28},{24,0},{28,4},{1,9},{5... | collective-permute-start | bytes 442376 | tf_op jit(solution)/shard_map/ppermute | solution.py:71
  138.8 3.0 %collective-permute-done.16.refs_2_ = bf16[576,128]{1,0:T(8,128)(2,1)S(1)} collective-permute-done((bf16[576,128]{1,0:T(8,128)(2,1)S(1)}, bf16[576,128]{1,0:T(8,128)(2,1)S(1)}, u32[]{:S(2)}, u32[]{:S(2)}) %collective-permute-start.16) | collective-permute-done | bytes 147488 | tf_op jit(solution)/shard_map/ppermute | solution.py:71
  141.8 8.1 %collective-permute-start.20 = (bf16[576,128]{1,0:T(8,128)(2,1)S(1)}, bf16[576,128]{1,0:T(8,128)(2,1)S(1)}, u32[]{:S(2)}, u32[]{:S(2)}) collective-permute-start(bf16[576,128]{1,0:T(8,128)(2,1)S(1)} %get-tuple-element.57), channel_id=1, source_target_pairs={{0,28},{4,0},{8,4},{12,8},{16,12},{20,16},{24,20},{28,24},{1,29},{... | collective-permute-start | bytes 442376 | tf_op jit(solution)/shard_map/ppermute | solution.py:71
  149.9 2.7 %collective-permute-done.18.refs_4_ = bf16[576,128]{1,0:T(8,128)(2,1)S(1)} collective-permute-done((bf16[576,128]{1,0:T(8,128)(2,1)S(1)}, bf16[576,128]{1,0:T(8,128)(2,1)S(1)}, u32[]{:S(2)}, u32[]{:S(2)}) %collective-permute-start.18) | collective-permute-done | bytes 147488 | tf_op jit(solution)/shard_map/ppermute | solution.py:71
  152.6 3.1 %collective-permute-done.20.refs_6_ = bf16[576,128]{1,0:T(8,128)(2,1)S(1)} collective-permute-done((bf16[576,128]{1,0:T(8,128)(2,1)S(1)}, bf16[576,128]{1,0:T(8,128)(2,1)S(1)}, u32[]{:S(2)}, u32[]{:S(2)}) %collective-permute-start.20) | collective-permute-done | bytes 147488 | tf_op jit(solution)/shard_map/ppermute | solution.py:71
  155.9 6.9 %collective-permute-start.22 = (bf16[576,128]{1,0:T(8,128)(2,1)S(1)}, bf16[576,128]{1,0:T(8,128)(2,1)S(1)}, u32[]{:S(2)}, u32[]{:S(2)}) collective-permute-start(bf16[576,128]{1,0:T(8,128)(2,1)S(1)} %shard_map.93), channel_id=1, source_target_pairs={{0,0},{1,1},{2,33},{3,32},{32,3},{33,2},{34,34},{35,35},{4,4},{5,5... | collective-permute-start | bytes 442376 | tf_op jit(solution)/shard_map/ppermute | solution.py:55
  162.7 0.7 reshape.36
  163.4 3.9 %all-to-all-start.1 = ((bf16[32,2,768]{2,1,0:T(2,128)(2,1)}), bf16[32,2,768]{2,1,0:T(2,128)(2,1)S(1)}, u32[]{:S(2)}, u32[]{:S(2)}) async-start(bf16[32,2,768]{2,1,0:T(2,128)(2,1)} %reshape.36), calls=%async_computation.1 | async-start | bytes 196608 | tf_op jit(solution)/shard_map/all_to_all | solution.py:385
  167.4 1.3 collective-permute-start.24
  168.7 1.5 collective-permute-start.26
  170.2 1.5 collective-permute-start.25
  171.7 0.7 convert_bitcast_fusion
  172.5 4.4 %all-to-all-done.1 = bf16[32,2,768]{2,1,0:T(2,128)(2,1)S(1)} async-done(((bf16[32,2,768]{2,1,0:T(2,128)(2,1)}), bf16[32,2,768]{2,1,0:T(2,128)(2,1)S(1)}, u32[]{:S(2)}, u32[]{:S(2)}) %all-to-all-start.1) | async-done | bytes 98336 | tf_op jit(solution)/shard_map/all_to_all | solution.py:385
  176.8 0.7 convert_element_type.90
  177.6 0.8 convert_add_fusion
  (34 shorter events, 2.4 us)
Async XLA Ops:
  0.6 37.1 %copy-start.1 = (bf16[1,2,24576]{2,1,0:T(2,128)(2,1)S(1)}, bf16[1,2,24576]{2,1,0:T(2,128)(2,1)}, u32[]{:S(2)}) copy-start(bf16[1,2,24576]{2,1,0:T(2,128)(2,1)} %param.6) | copy-start | bytes 294916
  0.6 37.1 %copy-start.2 = (bf16[1,2,16384]{2,1,0:T(2,128)(2,1)S(1)}, bf16[1,2,16384]{2,1,0:T(2,128)(2,1)}, u32[]{:S(2)}) copy-start(bf16[1,2,16384]{2,1,0:T(2,128)(2,1)} %param.7) | copy-start | bytes 196612
  0.7 60.5 %copy-start = (bf16[512,1024]{1,0:T(8,128)(2,1)S(1)}, bf16[512,1024]{1,0:T(8,128)(2,1)}, u32[]{:S(2)}) copy-start(bf16[512,1024]{1,0:T(8,128)(2,1)} %w.3) | copy-start | bytes 3145732
  0.7 9.2 %collective-permute-start.2 = (bf16[576,128]{1,0:T(8,128)(2,1)}, bf16[576,128]{1,0:T(8,128)(2,1)S(1)}, u32[]{:S(2)}, u32[]{:S(2)}) collective-permute-start(bf16[576,128]{1,0:T(8,128)(2,1)} %bitcast.21), channel_id=1, source_target_pairs={{0,0},{1,1},{2,33},{3,32},{32,3},{33,2},{34,34},{35,35},{4,4},{5,5... | collective-permute-start | bytes 442376 | tf_op jit(solution)/shard_map/ppermute | solution.py:55
  9.8 11.2 %collective-permute-start.9 = (bf16[576,128]{1,0:T(8,128)(2,1)S(1)}, bf16[576,128]{1,0:T(8,128)(2,1)S(1)}, u32[]{:S(2)}, u32[]{:S(2)}) collective-permute-start(bf16[576,128]{1,0:T(8,128)(2,1)S(1)} %collective-permute-done.2.refs_0_), channel_id=1, source_target_pairs={{0,28},{4,0},{8,4},{12,8},{16,12},{20,16},{24,20},{28,24},{1,29},{... | collective-permute-start | bytes 442376 | tf_op jit(solution)/shard_map/ppermute | solution.py:71
  15.4 6.9 %collective-permute-start.8 = (bf16[576,128]{1,0:T(8,128)(2,1)S(1)}, bf16[576,128]{1,0:T(8,128)(2,1)S(1)}, u32[]{:S(2)}, u32[]{:S(2)}) collective-permute-start(bf16[576,128]{1,0:T(8,128)(2,1)S(1)} %collective-permute-done.2.refs_0_), channel_id=1, source_target_pairs={{0,4},{4,8},{8,12},{12,16},{16,20},{20,24},{24,28},{28,0},{1,5},{5... | collective-permute-start | bytes 442376 | tf_op jit(solution)/shard_map/ppermute | solution.py:71
  15.4 13.2 %collective-permute-start.7 = (bf16[576,128]{1,0:T(8,128)(2,1)S(1)}, bf16[576,128]{1,0:T(8,128)(2,1)S(1)}, u32[]{:S(2)}, u32[]{:S(2)}) collective-permute-start(bf16[576,128]{1,0:T(8,128)(2,1)S(1)} %collective-permute-done.2.refs_0_), channel_id=1, source_target_pairs={{0,24},{4,28},{8,0},{12,4},{16,8},{20,12},{24,16},{28,20},{1,25},{... | collective-permute-start | bytes 442376 | tf_op jit(solution)/shard_map/ppermute | solution.py:71
  17.3 15.1 %collective-permute-start.6 = (bf16[576,128]{1,0:T(8,128)(2,1)S(1)}, bf16[576,128]{1,0:T(8,128)(2,1)S(1)}, u32[]{:S(2)}, u32[]{:S(2)}) collective-permute-start(bf16[576,128]{1,0:T(8,128)(2,1)S(1)} %collective-permute-done.2.refs_0_), channel_id=1, source_target_pairs={{0,8},{4,12},{8,16},{12,20},{16,24},{20,28},{24,0},{28,4},{1,9},{5... | collective-permute-start | bytes 442376 | tf_op jit(solution)/shard_map/ppermute | solution.py:71
  17.8 19.5 %collective-permute-start.5 = (bf16[576,128]{1,0:T(8,128)(2,1)S(1)}, bf16[576,128]{1,0:T(8,128)(2,1)S(1)}, u32[]{:S(2)}, u32[]{:S(2)}) collective-permute-start(bf16[576,128]{1,0:T(8,128)(2,1)S(1)} %collective-permute-done.2.refs_0_), channel_id=1, source_target_pairs={{0,20},{4,24},{8,28},{12,0},{16,4},{20,8},{24,12},{28,16},{1,21},{... | collective-permute-start | bytes 442376 | tf_op jit(solution)/shard_map/ppermute | solution.py:71
  21.1 16.2 %collective-permute-start.4 = (bf16[576,128]{1,0:T(8,128)(2,1)S(1)}, bf16[576,128]{1,0:T(8,128)(2,1)S(1)}, u32[]{:S(2)}, u32[]{:S(2)}) collective-permute-start(bf16[576,128]{1,0:T(8,128)(2,1)S(1)} %collective-permute-done.2.refs_0_), channel_id=1, source_target_pairs={{0,12},{4,16},{8,20},{12,24},{16,28},{20,0},{24,4},{28,8},{1,13},{... | collective-permute-start | bytes 442376 | tf_op jit(solution)/shard_map/ppermute | solution.py:71
  22.3 15.0 %collective-permute-start.3 = (bf16[576,128]{1,0:T(8,128)(2,1)S(1)}, bf16[576,128]{1,0:T(8,128)(2,1)S(1)}, u32[]{:S(2)}, u32[]{:S(2)}) collective-permute-start(bf16[576,128]{1,0:T(8,128)(2,1)S(1)} %collective-permute-done.2.refs_0_), channel_id=1, source_target_pairs={{0,16},{4,20},{8,24},{12,28},{16,0},{20,4},{24,8},{28,12},{1,17},{... | collective-permute-start | bytes 442376 | tf_op jit(solution)/shard_map/ppermute | solution.py:71
  37.6 41.1 %collective-permute-start.10 = (bf16[576,1024]{1,0:T(8,128)(2,1)S(1)}, bf16[576,1024]{1,0:T(8,128)(2,1)}, u32[]{:S(2)}, u32[]{:S(2)}) collective-permute-start(bf16[576,1024]{1,0:T(8,128)(2,1)S(1)} %shard_map.86.refs_3_), channel_id=1, source_target_pairs={{0,32},{32,0},{1,33},{33,1},{2,34},{34,2},{3,35},{35,3},{4,36},{36... | collective-permute-start | bytes 3538952 | tf_op jit(solution)/shard_map/ppermute | solution.py:63
  38.6 22.6 %all-to-all-start = ((bf16[32,2,1280]{2,1,0:T(2,128)(2,1)}), bf16[32,2,1280]{2,1,0:T(2,128)(2,1)S(1)}, u32[]{:S(2)}, u32[]{:S(2)}) async-start(bf16[32,2,1280]{2,1,0:T(2,128)(2,1)} %maximum_bitcast_fusion), calls=%async_computation | async-start | bytes 327680 | tf_op jit(solution)/shard_map/all_to_all | solution.py:309
  61.7 17.0 %collective-permute-start.1 = (bf16[256,1152]{1,0:T(8,128)(2,1)S(1)}, bf16[256,1152]{1,0:T(8,128)(2,1)}, u32[]{:S(2)}, u32[]{:S(2)}) collective-permute-start(bf16[256,1152]{1,0:T(8,128)(2,1)S(1)} %shard_map.85), channel_id=1, source_target_pairs={{0,1},{1,0},{2,33},{3,32},{32,3},{33,2},{34,35},{35,34},{4,5},{5,4... | collective-permute-start | bytes 1769480 | tf_op jit(solution)/shard_map/ppermute | solution.py:59
  64.6 14.2 %collective-permute-start = (bf16[256,1152]{1,0:T(8,128)(2,1)S(1)}, bf16[256,1152]{1,0:T(8,128)(2,1)}, u32[]{:S(2)}, u32[]{:S(2)}) collective-permute-start(bf16[256,1152]{1,0:T(8,128)(2,1)S(1)} %shard_map.85), channel_id=1, source_target_pairs={{0,0},{1,1},{2,32},{3,33},{32,2},{33,3},{34,34},{35,35},{4,4},{5,5... | collective-permute-start | bytes 1769480 | tf_op jit(solution)/shard_map/ppermute | solution.py:59
  89.5 3.2 %collective-permute-start.11 = (f32[8,512]{1,0:T(8,128)S(1)}, f32[8,512]{1,0:T(8,128)S(1)}, u32[]{:S(2)}, u32[]{:S(2)}) collective-permute-start(f32[8,512]{1,0:T(8,128)S(1)} %get-tuple-element.32.st), channel_id=1, source_target_pairs={{0,1},{1,0},{2,3},{3,2},{4,5},{5,4},{6,7},{7,6},{8,9},{9,8},{10,11... | collective-permute-start | bytes 49160 | tf_op jit(solution)/shard_map/ppermute | solution.py:67
  96.7 3.0 %collective-permute-start.12 = (bf16[8,576,128]{2,1,0:T(8,128)(2,1)S(1)}, bf16[8,576,128]{2,1,0:T(8,128)(2,1)S(1)}, u32[]{:S(2)}, u32[]{:S(2)}) collective-permute-start(bf16[8,576,128]{2,1,0:T(8,128)(2,1)S(1)} %get-tuple-element.36), channel_id=1, source_target_pairs={{0,32},{32,0},{1,33},{33,1},{2,34},{34,2},{3,35},{35,3},{4,36},{36... | collective-permute-start | bytes 3538952 | tf_op jit(solution)/shard_map/ppermute | solution.py:63
  103.5 19.4 %collective-permute-start.13 = (bf16[256,1152]{1,0:T(8,128)(2,1)S(1)}, bf16[256,1152]{1,0:T(8,128)(2,1)S(1)}, u32[]{:S(2)}, u32[]{:S(2)}) collective-permute-start(bf16[256,1152]{1,0:T(8,128)(2,1)S(1)} %get-tuple-element.48), channel_id=1, source_target_pairs={{0,0},{1,1},{2,32},{3,33},{32,2},{33,3},{34,34},{35,35},{4,4},{5,5... | collective-permute-start | bytes 1769480 | tf_op jit(solution)/shard_map/ppermute | solution.py:59
  109.0 15.4 %collective-permute-start.14 = (bf16[256,1152]{1,0:T(8,128)(2,1)S(1)}, bf16[256,1152]{1,0:T(8,128)(2,1)S(1)}, u32[]{:S(2)}, u32[]{:S(2)}) collective-permute-start(bf16[256,1152]{1,0:T(8,128)(2,1)S(1)} %get-tuple-element.49), channel_id=1, source_target_pairs={{0,1},{1,0},{2,33},{3,32},{32,3},{33,2},{34,35},{35,34},{4,5},{5,4... | collective-permute-start | bytes 1769480 | tf_op jit(solution)/shard_map/ppermute | solution.py:59
  125.7 41.5 %collective-permute-start.23 = (bf16[256,1024]{1,0:T(8,128)(2,1)S(1)}, bf16[256,1024]{1,0:T(8,128)(2,1)S(1)}, u32[]{:S(2)}, u32[]{:S(2)}) collective-permute-start(bf16[256,1024]{1,0:T(8,128)(2,1)S(1)} %get-tuple-element.60), channel_id=1, source_target_pairs={{0,32},{32,0},{1,33},{33,1},{2,34},{34,2},{3,35},{35,3},{4,36},{36... | collective-permute-start | bytes 1572872 | tf_op jit(solution)/shard_map/ppermute | solution.py:63
  125.8 9.8 %collective-permute-start.15 = (bf16[576,128]{1,0:T(8,128)(2,1)S(1)}, bf16[576,128]{1,0:T(8,128)(2,1)S(1)}, u32[]{:S(2)}, u32[]{:S(2)}) collective-permute-start(bf16[576,128]{1,0:T(8,128)(2,1)S(1)} %get-tuple-element.52), channel_id=1, source_target_pairs={{0,16},{4,20},{8,24},{12,28},{16,0},{20,4},{24,8},{28,12},{1,17},{... | collective-permute-start | bytes 442376 | tf_op jit(solution)/shard_map/ppermute | solution.py:71
  126.8 15.0 %collective-permute-start.16 = (bf16[576,128]{1,0:T(8,128)(2,1)S(1)}, bf16[576,128]{1,0:T(8,128)(2,1)S(1)}, u32[]{:S(2)}, u32[]{:S(2)}) collective-permute-start(bf16[576,128]{1,0:T(8,128)(2,1)S(1)} %get-tuple-element.53), channel_id=1, source_target_pairs={{0,20},{4,24},{8,28},{12,0},{16,4},{20,8},{24,12},{28,16},{1,21},{... | collective-permute-start | bytes 442376 | tf_op jit(solution)/shard_map/ppermute | solution.py:71
  130.8 19.1 %collective-permute-start.17 = (bf16[576,128]{1,0:T(8,128)(2,1)S(1)}, bf16[576,128]{1,0:T(8,128)(2,1)S(1)}, u32[]{:S(2)}, u32[]{:S(2)}) collective-permute-start(bf16[576,128]{1,0:T(8,128)(2,1)S(1)} %get-tuple-element.54), channel_id=1, source_target_pairs={{0,12},{4,16},{8,20},{12,24},{16,28},{20,0},{24,4},{28,8},{1,13},{... | collective-permute-start | bytes 442376 | tf_op jit(solution)/shard_map/ppermute | solution.py:71
  130.8 21.7 %collective-permute-start.18 = (bf16[576,128]{1,0:T(8,128)(2,1)S(1)}, bf16[576,128]{1,0:T(8,128)(2,1)S(1)}, u32[]{:S(2)}, u32[]{:S(2)}) collective-permute-start(bf16[576,128]{1,0:T(8,128)(2,1)S(1)} %get-tuple-element.55), channel_id=1, source_target_pairs={{0,24},{4,28},{8,0},{12,4},{16,8},{20,12},{24,16},{28,20},{1,25},{... | collective-permute-start | bytes 442376 | tf_op jit(solution)/shard_map/ppermute | solution.py:71
  135.6 16.9 %collective-permute-start.19 = (bf16[576,128]{1,0:T(8,128)(2,1)S(1)}, bf16[576,128]{1,0:T(8,128)(2,1)S(1)}, u32[]{:S(2)}, u32[]{:S(2)}) collective-permute-start(bf16[576,128]{1,0:T(8,128)(2,1)S(1)} %get-tuple-element.56), channel_id=1, source_target_pairs={{0,8},{4,12},{8,16},{12,20},{16,24},{20,28},{24,0},{28,4},{1,9},{5... | collective-permute-start | bytes 442376 | tf_op jit(solution)/shard_map/ppermute | solution.py:71
  141.8 13.9 %collective-permute-start.20 = (bf16[576,128]{1,0:T(8,128)(2,1)S(1)}, bf16[576,128]{1,0:T(8,128)(2,1)S(1)}, u32[]{:S(2)}, u32[]{:S(2)}) collective-permute-start(bf16[576,128]{1,0:T(8,128)(2,1)S(1)} %get-tuple-element.57), channel_id=1, source_target_pairs={{0,28},{4,0},{8,4},{12,8},{16,12},{20,16},{24,20},{28,24},{1,29},{... | collective-permute-start | bytes 442376 | tf_op jit(solution)/shard_map/ppermute | solution.py:71
  149.9 5.8 %collective-permute-start.21 = (bf16[576,128]{1,0:T(8,128)(2,1)S(1)}, bf16[576,128]{1,0:T(8,128)(2,1)S(1)}, u32[]{:S(2)}, u32[]{:S(2)}) collective-permute-start(bf16[576,128]{1,0:T(8,128)(2,1)S(1)} %get-tuple-element.58), channel_id=1, source_target_pairs={{0,4},{4,8},{8,12},{12,16},{16,20},{20,24},{24,28},{28,0},{1,5},{5... | collective-permute-start | bytes 442376 | tf_op jit(solution)/shard_map/ppermute | solution.py:71
  155.9 15.9 %collective-permute-start.22 = (bf16[576,128]{1,0:T(8,128)(2,1)S(1)}, bf16[576,128]{1,0:T(8,128)(2,1)S(1)}, u32[]{:S(2)}, u32[]{:S(2)}) collective-permute-start(bf16[576,128]{1,0:T(8,128)(2,1)S(1)} %shard_map.93), channel_id=1, source_target_pairs={{0,0},{1,1},{2,33},{3,32},{32,3},{33,2},{34,34},{35,35},{4,4},{5,5... | collective-permute-start | bytes 442376 | tf_op jit(solution)/shard_map/ppermute | solution.py:55
  163.4 13.4 %all-to-all-start.1 = ((bf16[32,2,768]{2,1,0:T(2,128)(2,1)}), bf16[32,2,768]{2,1,0:T(2,128)(2,1)S(1)}, u32[]{:S(2)}, u32[]{:S(2)}) async-start(bf16[32,2,768]{2,1,0:T(2,128)(2,1)} %reshape.36), calls=%async_computation.1 | async-start | bytes 196608 | tf_op jit(solution)/shard_map/all_to_all | solution.py:385
  167.4 10.2 %collective-permute-start.24 = (bf16[64,1024]{1,0:T(8,128)(2,1)S(1)}, bf16[64,1024]{1,0:T(8,128)(2,1)S(1)}, u32[]{:S(2)}, u32[]{:S(2)}) collective-permute-start(bf16[64,1024]{1,0:T(8,128)(2,1)S(1)} %get-tuple-element.61), channel_id=1, source_target_pairs={{0,64},{64,128},{128,192},{192,0},{1,65},{65,129},{129,193},{193,1... | collective-permute-start | bytes 393224 | tf_op jit(solution)/shard_map/ppermute | solution.py:383
  168.7 8.9 %collective-permute-start.26 = (bf16[64,1024]{1,0:T(8,128)(2,1)S(1)}, bf16[64,1024]{1,0:T(8,128)(2,1)S(1)}, u32[]{:S(2)}, u32[]{:S(2)}) collective-permute-start(bf16[64,1024]{1,0:T(8,128)(2,1)S(1)} %get-tuple-element.62), channel_id=1, source_target_pairs={{0,192},{64,0},{128,64},{192,128},{1,193},{65,1},{129,65},{193,129... | collective-permute-start | bytes 393224 | tf_op jit(solution)/shard_map/ppermute | solution.py:383
  170.2 7.4 %collective-permute-start.25 = (bf16[64,1024]{1,0:T(8,128)(2,1)S(1)}, bf16[64,1024]{1,0:T(8,128)(2,1)S(1)}, u32[]{:S(2)}, u32[]{:S(2)}) collective-permute-start(bf16[64,1024]{1,0:T(8,128)(2,1)S(1)} %get-tuple-element.63), channel_id=1, source_target_pairs={{0,128},{64,192},{128,0},{192,64},{1,129},{65,193},{129,1},{193,65... | collective-permute-start | bytes 393224 | tf_op jit(solution)/shard_map/ppermute | solution.py:383

commit v2 on v1

--- a/solution.py
+++ b/solution.py
@@ -20,6 +20,7 @@
 NQ = 64
 ROWS = NQ * HEADS
 WIDE = 2 * C + 2 * DR
+RAW = HEADS * (DN + DR + DV)
 BLK = 128
 DP = ("x", "core")
 CTX = ("z", "y")
@@ -59,6 +60,15 @@
     return lax.ppermute(v, ("core", "y"), turned(flip))
 
 
+def relay(v):
+    pairs = []
+    for c in range(2):
+        for y in range(NY):
+            away = int((y >> 1) != c)
+            pairs.append((c * NY + y, c * NY + (y ^ away)))
+    return lax.ppermute(v, ("core", "y"), pairs)
+
+
 def other_core(v):
     return lax.ppermute(v, "core", [(0, 1), (1, 0)])
 
@@ -73,6 +83,10 @@
 
 def dot(a, b, da=1, db=0):
     return lax.dot_general(a, b, (((da,), (db,)), ((), ())), preferred_element_type=F32)
+
+
+def in_hbm(v):
+    return pltpu.with_memory_space_constraint(v, pltpu.HBM)
 
 
 def vmem(shape, dtype):
@@ -95,25 +109,36 @@
     )(*args)
 
 
-def latents_body(start, length, both, w, out):
+def latents_body(
+    scal, start, length, raw_mine, raw_other, w_own, w_relay, w_other, mine, other, w_mine
+):
     lane = lax.broadcasted_iota(jnp.int32, (NQ, DR), 1)
+    low = start[0] + NQ - length[0]
     note = jnp.zeros((NQ, DR), F32)
-    low = start[0] + NQ - length[0]
     for n, v in enumerate((start[0] // NQ, start[0] % NQ, low // NQ, low % NQ)):
         note = jnp.where(lane == n, v.astype(F32), note)
     note = note.astype(BF)
-    for h in range(HEADS):
-        rows = slice(h * NQ, (h + 1) * NQ)
-        nope = both[:, h * (DN + DR) : h * (DN + DR) + DN]
-        rope = both[:, h * (DN + DR) + DN : (h + 1) * (DN + DR)]
-        at = HEADS * (DN + DR) + h * DV
-        grad = both[:, at : at + DV]
-        wk = w[:, h * (DN + DV) : h * (DN + DV) + DN]
-        wv = w[:, h * (DN + DV) + DN : (h + 1) * (DN + DV)]
-        out[rows, :C] = dot(grad, wv, 1, 1).astype(BF)
-        out[rows, C : 2 * C] = dot(nope, wk, 1, 1).astype(BF)
-        out[rows, 2 * C : C + W] = rope
-        out[rows, C + W :] = note
+
+    @pl.when(scal[4] == 1)
+    def _():
+        w_mine[...] = w_own[...]
+
+    @pl.when(scal[4] == 0)
+    def _():
+        w_mine[...] = w_relay[...]
+
+    for raw, w, out in ((raw_mine, w_mine, mine), (raw_other, w_other, other)):
+        for h in range(HEADS):
+            rows = slice(h * NQ, (h + 1) * NQ)
+            nope = raw[:, h * (DN + DR) : h * (DN + DR) + DN]
+            at = HEADS * (DN + DR) + h * DV
+            grad = raw[:, at : at + DV]
+            wk = w[:, h * (DN + DV) : h * (DN + DV) + DN]
+            wv = w[:, h * (DN + DV) + DN : (h + 1) * (DN + DV)]
+            out[rows, :C] = dot(grad, wv, 1, 1).astype(BF)
+            out[rows, C : 2 * C] = dot(nope, wk, 1, 1).astype(BF)
+            out[rows, 2 * C : C + W] = raw[:, h * (DN + DR) + DN : (h + 1) * (DN + DR)]
+            out[rows, C + W :] = note
 
 
 def join_body(*refs):
@@ -206,9 +231,9 @@
 
 def total_body(*refs):
     acc = refs[0][...].astype(F32)
-    for k in range(1, NZ):
-        acc = acc + refs[k][...].astype(F32)
-    refs[NZ][...] = acc.astype(BF)
+    for ref in refs[1:-1]:
+        acc = acc + ref[...].astype(F32)
+    refs[-1][...] = acc.astype(BF)
 
 
 def first_body(st, their, mine, other, ee, qq, ws, out):
@@ -270,11 +295,13 @@
         out[:, C + W :] = jnp.zeros((ROWS, DR), out.dtype)
 
 
-def tail_body(scal, qo, both, w, gq, keep, send, terms):
+def tail_body(scal, came, held, both, w, gq, keep, send, terms):
+    home = scal[4].astype(F32)
     for h in range(HEADS):
         rows = slice(h * NQ, (h + 1) * NQ)
-        o = qo[rows, :C]
-        lat = qo[rows, C : 2 * C]
+        qo = (came[rows, :].astype(F32) + held[rows, :].astype(F32) * home).astype(BF)
+        o = qo[:, :C]
+        lat = qo[:, C : 2 * C]
         nope = both[:, h * (DN + DR) : h * (DN + DR) + DN]
         at = HEADS * (DN + DR) + h * DV
         grad = both[:, at : at + DV]
@@ -283,7 +310,7 @@
         terms[:, c0 + DN : c0 + DN + DV] = dot(o, grad, 0, 0).astype(BF)
         q0 = h * (DN + DR)
         gq[:, q0 : q0 + DN] = dot(lat, w[:, c0 : c0 + DN]).astype(BF)
-        gq[:, q0 + DN : q0 + DN + DR] = qo[rows, 2 * C : C + W]
+        gq[:, q0 + DN : q0 + DN + DR] = qo[:, 2 * C : C + W]
     x, c = scal[2], scal[3]
     n = C // 8
     for k in range(4):
@@ -297,6 +324,13 @@
     ndev = NZ * NY
     own_q = queries.shape[1]
 
+    zi = lax.axis_index("z")
+    yi = lax.axis_index("y")
+    ci = lax.axis_index("core")
+    home = (yi >> 1) == ci
+    y_own = jnp.where(home, yi, 3 - yi)
+    scal = jnp.stack([zi, y_own, lax.axis_index("x"), ci, home.astype(jnp.int32)])
+
     own = swap(latent[0].T)
     both = jnp.concatenate(
         [
@@ -307,27 +341,32 @@
     )
     both = jnp.moveaxis(both, 1, 0)
     both = lax.all_to_all(both, CTX, 0, 0, tiled=True)
-    both = both.reshape(NQ, HEADS * (DN + DR + DV))
-
-    kept = [own] + [along_z(own, -d) for d in OFFSETS[1:]]
-
-    (qg,) = call(
+    both = both.reshape(NQ, RAW)
+    w_other = in_hbm(turn(latent_up, 1))
+    w_relay = in_hbm(relay(w_other))
+
+    near = {0: own}
+    for d in (-3, 3, -2, 2, -1, 1):
+        near[d] = along_z(own, -d)
+    near[4] = along_z(near[3], -1)
+    kept = [near[d] for d in OFFSETS]
+
+    raw_mine = turn(both, 0)
+    raw_other = turn(both, 1)
+    start = swap(query_start)
+    length = swap(key_lengths)
+    qg_mine, qg_other = call(
         latents_body,
-        [vmem((ROWS, WIDE), BF)],
-        (query_start, key_lengths, both, latent_up),
-        270_000_000,
-        smem=2,
-    )
-    qg_mine = turn(qg, 0)
-    qg_other = turn(qg, 1)
-    (mine_side,) = call(join_body, [vmem((W, NZ * BLK), BF)], kept, 1_000_000)
+        [vmem((ROWS, WIDE), BF)] * 2,
+        (scal, start, length, raw_mine, raw_other, in_hbm(latent_up), w_relay, w_other),
+        540_000_000,
+        (pltpu.VMEM((C, HEADS * (DN + DV)), BF),),
+        smem=3,
+        mib=12,
+    )
+    (mine_side,) = call(join_body, [vmem((W, NZ * BLK), BF)], kept, 1_000_000, mib=6)
     their_side = other_core(mine_side)
 
-    zi = lax.axis_index("z")
-    yi = lax.axis_index("y")
-    ci = lax.axis_index("core")
-    y_own = jnp.where((yi >> 1) == ci, yi, 3 - yi)
-    scal = jnp.stack([zi, y_own, lax.axis_index("x"), ci]).astype(jnp.int32)
     half = vmem((4 * ROWS, NZ * BLK), BF)
     big = pltpu.VMEM((2 * ROWS, KEYS), F32)
     e_mine, e_their, kt, stats = call(
@@ -348,14 +387,18 @@
         1_300_000_000,
     )
     their_keys = other_core(their_keys)
-    (mine_keys,) = call(parts_body, [piece], (qq, e_mine), 1_200_000_000)
-    sums = call(add_body, [vmem((W, BLK), BF)] * NZ, (mine_keys, their_keys), 1_000_000)
+    (mine_keys,) = call(parts_body, [piece], (qq, e_mine), 1_200_000_000, mib=12)
+    sums = call(add_body, [vmem((W, BLK), BF)] * NZ, (mine_keys, their_keys), 1_000_000, mib=8)
     sums, ws = lax.optimization_barrier((sums, ws))
+    sums = dict(zip(OFFSETS, sums))
+    early = along_z(sums[4], -1)
     moved = [sums[0]]
-    for n, d in enumerate(OFFSETS[1:]):
-        moved.append(along_z(sums[n + 1], d))
-    (total,) = call(total_body, [vmem((W, BLK), BF)], moved, 1_000_000)
-    key_grad = swap(total).astype(F32).T
+    for d in (3, -2, 2, -1, 1):
+        moved.append(along_z(sums[d], d))
+    moved.append(along_z((sums[-3].astype(F32) + early.astype(F32)).astype(BF), -3))
+    (total,) = call(total_body, [vmem((W, BLK), BF)], moved, 1_000_000, mib=4)
+    key_grad = swap(total)
+    key_grad = key_grad.astype(F32).T
 
     mine, other = call(
         query_body,
@@ -363,16 +406,18 @@
         (ws, kt, e_mine, e_their),
         2_400_000_000,
     )
-    mine, other = turn(mine, 0), turn(other, 1)
-    qo = (mine.astype(F32) + other.astype(F32)).astype(BF)
+    passed = relay(mine)
+    other = (other.astype(F32) + jnp.where(home, 0.0, passed.astype(F32))).astype(BF)
+    came = turn(other, 1)
     wide = HEADS * (DN + DV)
     gq, keep, send = call(
         tail_body,
         [vmem((NQ, HEADS * (DN + DR)), BF)] + [vmem((C // 2, wide), BF)] * 2,
-        (scal, qo, both, latent_up),
+        (scal, came, mine, both, in_hbm(latent_up)),
         200_000_000,
         (pltpu.VMEM((C, wide), BF),),
         smem=1,
+        mib=12,
     )
     got = other_core(send)
     n = C // 8

time: 179 us -> 194 us (1.084)
  blocking collectives: 0 us -> 26.8 us
  starting transfers between devices: 82.2 us -> 63.8 us
  waiting for transfers between devices: 67.4 us -> 72.9 us
  Pallas kernels: 22.4 us -> 24.7 us
    all_to_all x0 -> x1, blocking collectives: none -> 26.8 us  [step(): both = lax.all_to_all(both, CTX, 0, 0, tiled=True)]
    ppermute x4, waiting for transfers between devices: 26.9 us -> 8.2 us  [turn(): return lax.ppermute(v, ('core', 'y'), turned(flip))]
    ppermute x2 -> x4, waiting for transfers between devices: 3.03 us -> 18.7 us  [swap(): return lax.ppermute(v, ('core', 'y'), swap_pairs())]
    ppermute x0 -> x2, waiting for transfers between devices: none -> 15.1 us  [relay(): return lax.ppermute(v, ('core', 'y'), pairs)]
    all_to_all x1 -> x0, starting transfers between devices: 12.4 us -> none  [step(): both = lax.all_to_all(both, CTX, 0, 0, tiled=True)]
    ppermute x14, starting transfers between devices: 36.8 us -> 25 us  [along_z(): return lax.ppermute(v, 'z', [(i, (i + step) % NZ) for i in range(NZ)])]
    all_to_all x1 -> x0, waiting for transfers between devices: 8.9 us -> none  [step(): both = lax.all_to_all(both, CTX, 0, 0, tiled=True)]
    ppermute x0 -> x2, starting transfers between devices: none -> 3.84 us  [relay(): return lax.ppermute(v, ('core', 'y'), pairs)]
  transfers between devices with their start and end apart: 29 -> 32, of which waited for: 16 -> 16; matrix products, arithmetic and copies ran while one was open for 2% -> 1% of each run, Pallas kernels for 1% -> 4%
where the time goes in v2:
time: 194 us; the launch traced here: 193 us
  waiting for transfers between devices  72.9 us (38%)
  starting transfers between devices  63.8 us (33%)
  blocking collectives  26.8 us (14%)
  Pallas kernels  24.7 us (13%)
  other arithmetic  2.76 us (1%)
    all_to_all x1, blocking collectives, step(): both = lax.all_to_all(both, CTX, 0, 0, tiled=True)  26.8 us
    ppermute x14, starting transfers between devices, along_z(): return lax.ppermute(v, 'z', [(i, (i + step) % NZ) for i in range(NZ)])  25 us
    pallas_call x9, Pallas kernels, call(): pl.pallas_call(body, out_shape=out_shape, in_specs=specs, out_specs=[pl.B...  24.7 us
    ppermute x14, waiting for transfers between devices, along_z(): return lax.ppermute(v, 'z', [(i, (i + step) % NZ) for i in range(NZ)])  23.1 us
    ppermute x4, waiting for transfers between devices, swap(): return lax.ppermute(v, ('core', 'y'), swap_pairs())  18.7 us
    ppermute x2, waiting for transfers between devices, relay(): return lax.ppermute(v, ('core', 'y'), pairs)  15.1 us
    ppermute x4, starting transfers between devices, swap(): return lax.ppermute(v, ('core', 'y'), swap_pairs())  15.1 us
    ppermute x4, starting transfers between devices, turn(): return lax.ppermute(v, ('core', 'y'), turned(flip))  10.1 us
  transfers between devices with their start and end apart: 32, of which 16 were waited for; matrix products, arithmetic and copies ran while one was open for 1% of the time, Pallas kernels for 4%

profile of v2, /device:TPU:1, one launch (start us, length us, event | category | flops | bytes accessed | tf_op | source)
XLA Modules:
  0.0 192.7 jit_solution(640524201009938966)
XLA Ops:
  0.6 4.2 %collective-permute-start.4 = (bf16[512,1024]{1,0:T(8,128)(2,1)}, bf16[512,1024]{1,0:T(8,128)(2,1)}, u32[]{:S(2)}, u32[]{:S(2)}) collective-permute-start(bf16[512,1024]{1,0:T(8,128)(2,1)} %w.1), channel_id=1, source_target_pairs={{0,1},{1,0},{2,33},{3,32},{32,3},{33,2},{34,35},{35,34},{4,5},{5,4... | collective-permute-start | bytes 3145736 | tf_op jit(solution)/shard_map/ppermute | solution.py:60
  4.8 2.1 %collective-permute-start.6 = (bf16[576,128]{1,0:T(8,128)(2,1)}, bf16[576,128]{1,0:T(8,128)(2,1)S(1)}, u32[]{:S(2)}, u32[]{:S(2)}) collective-permute-start(bf16[576,128]{1,0:T(8,128)(2,1)} %bitcast.22), channel_id=1, source_target_pairs={{0,0},{1,1},{2,33},{3,32},{32,3},{33,2},{34,34},{35,35},{4,4},{5,5... | collective-permute-start | bytes 442376 | tf_op jit(solution)/shard_map/ppermute | solution.py:56
  6.9 12.5 %collective-permute-done.6.refs_0_ = bf16[576,128]{1,0:T(8,128)(2,1)S(1)} collective-permute-done((bf16[576,128]{1,0:T(8,128)(2,1)}, bf16[576,128]{1,0:T(8,128)(2,1)S(1)}, u32[]{:S(2)}, u32[]{:S(2)}) %collective-permute-start.6) | collective-permute-done | bytes 147488 | tf_op jit(solution)/shard_map/ppermute | solution.py:56
  19.4 5.6 %collective-permute-start.13 = (bf16[576,128]{1,0:T(8,128)(2,1)S(1)}, bf16[576,128]{1,0:T(8,128)(2,1)S(1)}, u32[]{:S(2)}, u32[]{:S(2)}) collective-permute-start(bf16[576,128]{1,0:T(8,128)(2,1)S(1)} %collective-permute-done.6.refs_0_), channel_id=1, source_target_pairs={{0,28},{4,0},{8,4},{12,8},{16,12},{20,16},{24,20},{28,24},{1,29},{... | collective-permute-start | bytes 442376 | tf_op jit(solution)/shard_map/ppermute | solution.py:81
  25.0 2.1 %collective-permute-start.7 = (bf16[576,128]{1,0:T(8,128)(2,1)S(1)}, bf16[576,128]{1,0:T(8,128)(2,1)S(1)}, u32[]{:S(2)}, u32[]{:S(2)}) collective-permute-start(bf16[576,128]{1,0:T(8,128)(2,1)S(1)} %collective-permute-done.6.refs_0_), channel_id=1, source_target_pairs={{0,20},{4,24},{8,28},{12,0},{16,4},{20,8},{24,12},{28,16},{1,21},{... | collective-permute-start | bytes 442376 | tf_op jit(solution)/shard_map/ppermute | solution.py:81
  27.0 2.0 %collective-permute-start.11 = (bf16[576,128]{1,0:T(8,128)(2,1)S(1)}, bf16[576,128]{1,0:T(8,128)(2,1)S(1)}, u32[]{:S(2)}, u32[]{:S(2)}) collective-permute-start(bf16[576,128]{1,0:T(8,128)(2,1)S(1)} %collective-permute-done.6.refs_0_), channel_id=1, source_target_pairs={{0,24},{4,28},{8,0},{12,4},{16,8},{20,12},{24,16},{28,20},{1,25},{... | collective-permute-start | bytes 442376 | tf_op jit(solution)/shard_map/ppermute | solution.py:81
  29.0 0.7 collective-permute-start.10
  29.7 1.0 collective-permute-done.12.refs_6_
  30.8 2.0 %collective-permute-start.9 = (bf16[576,128]{1,0:T(8,128)(2,1)S(1)}, bf16[576,128]{1,0:T(8,128)(2,1)S(1)}, u32[]{:S(2)}, u32[]{:S(2)}) collective-permute-start(bf16[576,128]{1,0:T(8,128)(2,1)S(1)} %collective-permute-done.6.refs_0_), channel_id=1, source_target_pairs={{0,12},{4,16},{8,20},{12,24},{16,28},{20,0},{24,4},{28,8},{1,13},{... | collective-permute-start | bytes 442376 | tf_op jit(solution)/shard_map/ppermute | solution.py:81
  32.8 1.8 collective-permute-done.7.refs_3_
  34.6 3.5 %collective-permute-start.8 = (bf16[576,128]{1,0:T(8,128)(2,1)S(1)}, bf16[576,128]{1,0:T(8,128)(2,1)S(1)}, u32[]{:S(2)}, u32[]{:S(2)}) collective-permute-start(bf16[576,128]{1,0:T(8,128)(2,1)S(1)} %collective-permute-done.7.refs_3_), channel_id=1, source_target_pairs={{0,28},{4,0},{8,4},{12,8},{16,12},{20,16},{24,20},{28,24},{1,29},{... | collective-permute-start | bytes 442376 | tf_op jit(solution)/shard_map/ppermute | solution.py:81
  38.1 3.3 %collective-permute-done.9.refs_2_ = bf16[576,128]{1,0:T(8,128)(2,1)S(1)} collective-permute-done((bf16[576,128]{1,0:T(8,128)(2,1)S(1)}, bf16[576,128]{1,0:T(8,128)(2,1)S(1)}, u32[]{:S(2)}, u32[]{:S(2)}) %collective-permute-start.9) | collective-permute-done | bytes 147488 | tf_op jit(solution)/shard_map/ppermute | solution.py:81
  41.9 1.9 collective-permute-start.5
  44.0 26.8 %all_to_all.10 = bf16[32,2,1280]{2,1,0:T(2,128)(2,1)S(1)} all-to-all(bf16[32,2,1280]{2,1,0:T(2,128)(2,1)S(1)} %maximum_bitcast_fusion), channel_id=1, replica_groups=mesh['x'=4,'core'=2,'z'=8,'y'=4] {'z','y'}, dimensions={0} | all-to-all | bytes 327680 | tf_op jit(solution)/shard_map/all_to_all | solution.py:343
  71.0 3.6 %collective-permute-start.2 = (bf16[64,1280]{1,0:T(8,128)(2,1)S(1)}, bf16[64,1280]{1,0:T(8,128)(2,1)S(1)}, u32[]{:S(2)}, u32[]{:S(2)}) collective-permute-start(bf16[64,1280]{1,0:T(8,128)(2,1)S(1)} %reshape.35.both), channel_id=1, source_target_pairs={{0,0},{1,1},{2,32},{3,33},{32,2},{33,3},{34,34},{35,35},{4,4},{5,5... | collective-permute-start | bytes 491528 | tf_op jit(solution)/shard_map/ppermute | solution.py:60
  74.6 3.2 %collective-permute-start = (s32[1]{0:T(128)}, s32[1]{0:T(128)}, u32[]{:S(2)}, u32[]{:S(2)}) collective-permute-start(s32[1]{0:T(128)} %param.10), channel_id=1, source_target_pairs={{0,0},{1,1},{2,33},{3,32},{32,3},{33,2},{34,34},{35,35},{4,4},{5,5... | collective-permute-start | bytes 20 | tf_op jit(solution)/shard_map/ppermute | solution.py:56
  77.9 3.1 %collective-permute-done.start = s32[1]{0:T(128)} collective-permute-done((s32[1]{0:T(128)}, s32[1]{0:T(128)}, u32[]{:S(2)}, u32[]{:S(2)}) %collective-permute-start) | collective-permute-done | bytes 36 | tf_op jit(solution)/shard_map/ppermute | solution.py:56
  81.0 3.0 %collective-permute-start.1 = (s32[1]{0:T(128)}, s32[1]{0:T(128)}, u32[]{:S(2)}, u32[]{:S(2)}) collective-permute-start(s32[1]{0:T(128)} %param.11), channel_id=1, source_target_pairs={{0,0},{1,1},{2,33},{3,32},{32,3},{33,2},{34,34},{35,35},{4,4},{5,5... | collective-permute-start | bytes 20 | tf_op jit(solution)/shard_map/ppermute | solution.py:56
  84.0 3.2 %collective-permute-done.1.length = s32[1]{0:T(128)} collective-permute-done((s32[1]{0:T(128)}, s32[1]{0:T(128)}, u32[]{:S(2)}, u32[]{:S(2)}) %collective-permute-start.1) | collective-permute-done | bytes 36 | tf_op jit(solution)/shard_map/ppermute | solution.py:56
  87.2 4.2 %shard_map.85 = (bf16[256,1152]{1,0:T(8,128)(2,1)S(1)}, bf16[256,1152]{1,0:T(8,128)(2,1)S(1)}) custom-call(s32[5]{0:T(128)S(1)} %stack.27.scal.refs_0_, s32[1]{0:T(128)} %collective-permute-done.start, s32[1]{0:T(128)} %collective-permute-done.1.length, bf16[64,1280]{1,0:T(8,128)(2,1)S(1)} %collective-permute-done.2.raw_mine, ...), custom_call_target="tpu_custom_call" | custom-call | flops 540000000 | bytes 4653084 | tf_op jit(solution)/shard_map/pallas_call | solution.py:101
  91.4 9.7 %shard_map.87 = (bf16[1024,1024]{1,0:T(8,128)(2,1)S(1)}, bf16[1024,1024]{1,0:T(8,128)(2,1)S(1)}, bf16[576,2048]{1,0:T(8,128)(2,1)S(1)}, f32[8,512]{1,0:T(8,128)S(1)}) custom-call(s32[5]{0:T(128)S(1)} %stack.27.scal.refs_0_, bf16[256,1152]{1,0:T(8,128)(2,1)S(1)} %get-tuple-element.34.refs_1_.mine, bf16[256,1152]{1,0:T(8,128)(2,1)S(1)} %get-tuple-element.35.refs_2_.other, ...), custom_call_target="tpu_custom_call" | custom-call | flops 2280000000 | bytes 10108948 | tf_op jit(solution)/shard_map/pallas_call | solution.py:101
  101.2 2.6 %collective-permute-done.15.their = f32[8,512]{1,0:T(8,128)S(1)} collective-permute-done((f32[8,512]{1,0:T(8,128)S(1)}, f32[8,512]{1,0:T(8,128)S(1)}, u32[]{:S(2)}, u32[]{:S(2)}) %collective-permute-start.15) | collective-permute-done | bytes 16416 | tf_op jit(solution)/shard_map/ppermute | solution.py:77
  103.8 2.8 %shard_map.88 = (bf16[1024,576]{1,0:T(8,128)(2,1)S(1)}, f32[512,128]{1,0:T(8,128)S(1)}, bf16[8,576,128]{2,1,0:T(8,128)(2,1)S(1)}) custom-call(f32[8,512]{1,0:T(8,128)S(1)} %get-tuple-element.36.st, f32[8,512]{1,0:T(8,128)S(1)} %collective-permute-done.15.their, bf16[256,1152]{1,0:T(8,128)(2,1)S(1)} %get-tuple-element.34.refs_1_.mine, ...), custom_call_target="tpu_custom_call" | custom-call | flops 1300000000 | bytes 5931008 | tf_op jit(solution)/shard_map/pallas_call | solution.py:101
  106.7 1.7 shard_map.89.a
  108.4 1.1 collective-permute-done.16.b
  109.8 3.6 %shard_map.91 = (bf16[256,1152]{1,0:T(8,128)(2,1)S(1)}, bf16[256,1152]{1,0:T(8,128)(2,1)S(1)}) custom-call(f32[512,128]{1,0:T(8,128)S(1)} %get-tuple-element.50.ws, bf16[576,2048]{1,0:T(8,128)(2,1)S(1)} %get-tuple-element.51.kt, bf16[1024,1024]{1,0:T(8,128)(2,1)S(1)} %get-tuple-element.39.ee.e0, bf16[1024,1024]{1,0:T(8,128)(2,1)S(1)} %get-tuple-element.37.ee.e1), custom_call_target="tpu_custom_call" | custom-call | flops 2400000000 | bytes 7995392 | tf_op jit(solution)/shard_map/pallas_call | solution.py:101
  113.4 1.9 collective-permute-start.17
  115.3 15.1 %collective-permute-done.17 = bf16[256,1152]{1,0:T(8,128)(2,1)S(1)} collective-permute-done((bf16[256,1152]{1,0:T(8,128)(2,1)S(1)}, bf16[256,1152]{1,0:T(8,128)(2,1)S(1)}, u32[]{:S(2)}, u32[]{:S(2)}) %collective-permute-start.17) | collective-permute-done | bytes 589856 | tf_op jit(solution)/shard_map/ppermute | solution.py:69
  130.6 2.2 %collective-permute-start.18 = (bf16[256,1152]{1,0:T(8,128)(2,1)S(1)}, bf16[256,1152]{1,0:T(8,128)(2,1)S(1)}, u32[]{:S(2)}, u32[]{:S(2)}) collective-permute-start(bf16[256,1152]{1,0:T(8,128)(2,1)S(1)} %add_convert_fusion), channel_id=1, source_target_pairs={{0,1},{1,0},{2,33},{3,32},{32,3},{33,2},{34,35},{35,34},{4,5},{5,4... | collective-permute-start | bytes 1769480 | tf_op jit(solution)/shard_map/ppermute | solution.py:60
  133.3 8.2 %collective-permute-done.18.came = bf16[256,1152]{1,0:T(8,128)(2,1)S(1)} collective-permute-done((bf16[256,1152]{1,0:T(8,128)(2,1)S(1)}, bf16[256,1152]{1,0:T(8,128)(2,1)S(1)}, u32[]{:S(2)}, u32[]{:S(2)}) %collective-permute-start.18) | collective-permute-done | bytes 589856 | tf_op jit(solution)/shard_map/ppermute | solution.py:60
  141.4 1.9 shard_map.92
  143.4 1.5 collective-permute-start.19
  144.9 3.1 %collective-permute-start.20 = (bf16[576,128]{1,0:T(8,128)(2,1)S(1)}, bf16[576,128]{1,0:T(8,128)(2,1)S(1)}, u32[]{:S(2)}, u32[]{:S(2)}) collective-permute-start(bf16[576,128]{1,0:T(8,128)(2,1)S(1)} %get-tuple-element.57), channel_id=1, source_target_pairs={{0,24},{4,28},{8,0},{12,4},{16,8},{20,12},{24,16},{28,20},{1,25},{... | collective-permute-start | bytes 442376 | tf_op jit(solution)/shard_map/ppermute | solution.py:81
  148.0 2.7 %collective-permute-start.22 = (bf16[576,128]{1,0:T(8,128)(2,1)S(1)}, bf16[576,128]{1,0:T(8,128)(2,1)S(1)}, u32[]{:S(2)}, u32[]{:S(2)}) collective-permute-start(bf16[576,128]{1,0:T(8,128)(2,1)S(1)} %get-tuple-element.59), channel_id=1, source_target_pairs={{0,28},{4,0},{8,4},{12,8},{16,12},{20,16},{24,20},{28,24},{1,29},{... | collective-permute-start | bytes 442376 | tf_op jit(solution)/shard_map/ppermute | solution.py:81
  150.8 8.4 %collective-permute-done.19.refs_1_ = bf16[576,128]{1,0:T(8,128)(2,1)S(1)} collective-permute-done((bf16[576,128]{1,0:T(8,128)(2,1)S(1)}, bf16[576,128]{1,0:T(8,128)(2,1)S(1)}, u32[]{:S(2)}, u32[]{:S(2)}) %collective-permute-start.19) | collective-permute-done | bytes 147488 | tf_op jit(solution)/shard_map/ppermute | solution.py:81
  159.1 1.5 collective-permute-start.25
  160.6 2.8 %collective-permute-done.21.refs_3_ = bf16[576,128]{1,0:T(8,128)(2,1)S(1)} collective-permute-done((bf16[576,128]{1,0:T(8,128)(2,1)S(1)}, bf16[576,128]{1,0:T(8,128)(2,1)S(1)}, u32[]{:S(2)}, u32[]{:S(2)}) %collective-permute-start.21) | collective-permute-done | bytes 147488 | tf_op jit(solution)/shard_map/ppermute | solution.py:81
  163.4 3.4 %collective-permute-done.23.refs_5_ = bf16[576,128]{1,0:T(8,128)(2,1)S(1)} collective-permute-done((bf16[576,128]{1,0:T(8,128)(2,1)S(1)}, bf16[576,128]{1,0:T(8,128)(2,1)S(1)}, u32[]{:S(2)}, u32[]{:S(2)}) %collective-permute-start.23) | collective-permute-done | bytes 147488 | tf_op jit(solution)/shard_map/ppermute | solution.py:81
  166.8 2.4 %collective-permute-done.25.refs_6_ = bf16[576,128]{1,0:T(8,128)(2,1)S(1)} collective-permute-done((bf16[576,128]{1,0:T(8,128)(2,1)S(1)}, bf16[576,128]{1,0:T(8,128)(2,1)S(1)}, u32[]{:S(2)}, u32[]{:S(2)}) %collective-permute-start.25) | collective-permute-done | bytes 147488 | tf_op jit(solution)/shard_map/ppermute | solution.py:81
  169.3 6.8 %collective-permute-start.26 = (bf16[576,128]{1,0:T(8,128)(2,1)S(1)}, bf16[576,128]{1,0:T(8,128)(2,1)S(1)}, u32[]{:S(2)}, u32[]{:S(2)}) collective-permute-start(bf16[576,128]{1,0:T(8,128)(2,1)S(1)} %shard_map.93), channel_id=1, source_target_pairs={{0,0},{1,1},{2,33},{3,32},{32,3},{33,2},{34,34},{35,35},{4,4},{5,5... | collective-permute-start | bytes 442376 | tf_op jit(solution)/shard_map/ppermute | solution.py:56
  176.8 5.1 %all-to-all-start.1 = ((bf16[32,2,768]{2,1,0:T(2,128)(2,1)}), bf16[32,2,768]{2,1,0:T(2,128)(2,1)S(1)}, u32[]{:S(2)}, u32[]{:S(2)}) async-start(bf16[32,2,768]{2,1,0:T(2,128)(2,1)} %reshape.36), calls=%async_computation.1 | async-start | bytes 196608 | tf_op jit(solution)/shard_map/all_to_all | solution.py:430
  182.1 1.3 collective-permute-start.28
  183.4 1.5 collective-permute-start.30
  184.9 1.5 collective-permute-start.29
  186.4 0.7 convert_bitcast_fusion
  187.2 3.9 %all-to-all-done.1 = bf16[32,2,768]{2,1,0:T(2,128)(2,1)S(1)} async-done(((bf16[32,2,768]{2,1,0:T(2,128)(2,1)}), bf16[32,2,768]{2,1,0:T(2,128)(2,1)S(1)}, u32[]{:S(2)}, u32[]{:S(2)}) %all-to-all-start.1) | async-done | bytes 98336 | tf_op jit(solution)/shard_map/all_to_all | solution.py:430
  191.1 0.7 convert_element_type.103
  191.9 0.8 convert_add_fusion
  (40 shorter events, 3.1 us)
Async XLA Ops:
  0.6 41.3 %collective-permute-start.4 = (bf16[512,1024]{1,0:T(8,128)(2,1)}, bf16[512,1024]{1,0:T(8,128)(2,1)}, u32[]{:S(2)}, u32[]{:S(2)}) collective-permute-start(bf16[512,1024]{1,0:T(8,128)(2,1)} %w.1), channel_id=1, source_target_pairs={{0,1},{1,0},{2,33},{3,32},{32,3},{33,2},{34,35},{35,34},{4,5},{5,4... | collective-permute-start | bytes 3145736 | tf_op jit(solution)/shard_map/ppermute | solution.py:60
  4.8 39.0 %copy-start = (bf16[1,2,24576]{2,1,0:T(2,128)(2,1)S(1)}, bf16[1,2,24576]{2,1,0:T(2,128)(2,1)}, u32[]{:S(2)}) copy-start(bf16[1,2,24576]{2,1,0:T(2,128)(2,1)} %param.6) | copy-start | bytes 294916
  4.8 39.0 %copy-start.1 = (bf16[1,2,16384]{2,1,0:T(2,128)(2,1)S(1)}, bf16[1,2,16384]{2,1,0:T(2,128)(2,1)}, u32[]{:S(2)}) copy-start(bf16[1,2,16384]{2,1,0:T(2,128)(2,1)} %param.7) | copy-start | bytes 196612
  4.8 14.6 %collective-permute-start.6 = (bf16[576,128]{1,0:T(8,128)(2,1)}, bf16[576,128]{1,0:T(8,128)(2,1)S(1)}, u32[]{:S(2)}, u32[]{:S(2)}) collective-permute-start(bf16[576,128]{1,0:T(8,128)(2,1)} %bitcast.22), channel_id=1, source_target_pairs={{0,0},{1,1},{2,33},{3,32},{32,3},{33,2},{34,34},{35,35},{4,4},{5,5... | collective-permute-start | bytes 442376 | tf_op jit(solution)/shard_map/ppermute | solution.py:56
  19.4 9.6 %collective-permute-start.13 = (bf16[576,128]{1,0:T(8,128)(2,1)S(1)}, bf16[576,128]{1,0:T(8,128)(2,1)S(1)}, u32[]{:S(2)}, u32[]{:S(2)}) collective-permute-start(bf16[576,128]{1,0:T(8,128)(2,1)S(1)} %collective-permute-done.6.refs_0_), channel_id=1, source_target_pairs={{0,28},{4,0},{8,4},{12,8},{16,12},{20,16},{24,20},{28,24},{1,29},{... | collective-permute-start | bytes 442376 | tf_op jit(solution)/shard_map/ppermute | solution.py:81
  25.0 5.8 %collective-permute-start.12 = (bf16[576,128]{1,0:T(8,128)(2,1)S(1)}, bf16[576,128]{1,0:T(8,128)(2,1)S(1)}, u32[]{:S(2)}, u32[]{:S(2)}) collective-permute-start(bf16[576,128]{1,0:T(8,128)(2,1)S(1)} %collective-permute-done.6.refs_0_), channel_id=1, source_target_pairs={{0,4},{4,8},{8,12},{12,16},{16,20},{20,24},{24,28},{28,0},{1,5},{5... | collective-permute-start | bytes 442376 | tf_op jit(solution)/shard_map/ppermute | solution.py:81
  25.0 9.6 %collective-permute-start.7 = (bf16[576,128]{1,0:T(8,128)(2,1)S(1)}, bf16[576,128]{1,0:T(8,128)(2,1)S(1)}, u32[]{:S(2)}, u32[]{:S(2)}) collective-permute-start(bf16[576,128]{1,0:T(8,128)(2,1)S(1)} %collective-permute-done.6.refs_0_), channel_id=1, source_target_pairs={{0,20},{4,24},{8,28},{12,0},{16,4},{20,8},{24,12},{28,16},{1,21},{... | collective-permute-start | bytes 442376 | tf_op jit(solution)/shard_map/ppermute | solution.py:81
  27.0 11.1 %collective-permute-start.11 = (bf16[576,128]{1,0:T(8,128)(2,1)S(1)}, bf16[576,128]{1,0:T(8,128)(2,1)S(1)}, u32[]{:S(2)}, u32[]{:S(2)}) collective-permute-start(bf16[576,128]{1,0:T(8,128)(2,1)S(1)} %collective-permute-done.6.refs_0_), channel_id=1, source_target_pairs={{0,24},{4,28},{8,0},{12,4},{16,8},{20,12},{24,16},{28,20},{1,25},{... | collective-permute-start | bytes 442376 | tf_op jit(solution)/shard_map/ppermute | solution.py:81
  29.0 9.1 %collective-permute-start.10 = (bf16[576,128]{1,0:T(8,128)(2,1)S(1)}, bf16[576,128]{1,0:T(8,128)(2,1)S(1)}, u32[]{:S(2)}, u32[]{:S(2)}) collective-permute-start(bf16[576,128]{1,0:T(8,128)(2,1)S(1)} %collective-permute-done.6.refs_0_), channel_id=1, source_target_pairs={{0,8},{4,12},{8,16},{12,20},{16,24},{20,28},{24,0},{28,4},{1,9},{5... | collective-permute-start | bytes 442376 | tf_op jit(solution)/shard_map/ppermute | solution.py:81
  30.8 10.7 %collective-permute-start.9 = (bf16[576,128]{1,0:T(8,128)(2,1)S(1)}, bf16[576,128]{1,0:T(8,128)(2,1)S(1)}, u32[]{:S(2)}, u32[]{:S(2)}) collective-permute-start(bf16[576,128]{1,0:T(8,128)(2,1)S(1)} %collective-permute-done.6.refs_0_), channel_id=1, source_target_pairs={{0,12},{4,16},{8,20},{12,24},{16,28},{20,0},{24,4},{28,8},{1,13},{... | collective-permute-start | bytes 442376 | tf_op jit(solution)/shard_map/ppermute | solution.py:81
  34.6 6.8 %collective-permute-start.8 = (bf16[576,128]{1,0:T(8,128)(2,1)S(1)}, bf16[576,128]{1,0:T(8,128)(2,1)S(1)}, u32[]{:S(2)}, u32[]{:S(2)}) collective-permute-start(bf16[576,128]{1,0:T(8,128)(2,1)S(1)} %collective-permute-done.7.refs_3_), channel_id=1, source_target_pairs={{0,28},{4,0},{8,4},{12,8},{16,12},{20,16},{24,20},{28,24},{1,29},{... | collective-permute-start | bytes 442376 | tf_op jit(solution)/shard_map/ppermute | solution.py:81
  41.8 49.6 %collective-permute-start.14 = (bf16[576,1024]{1,0:T(8,128)(2,1)S(1)}, bf16[576,1024]{1,0:T(8,128)(2,1)S(1)}, u32[]{:S(2)}, u32[]{:S(2)}) collective-permute-start(bf16[576,1024]{1,0:T(8,128)(2,1)S(1)} %shard_map.86.refs_3_), channel_id=1, source_target_pairs={{0,32},{32,0},{1,33},{33,1},{2,34},{34,2},{3,35},{35,3},{4,36},{36... | collective-permute-start | bytes 3538952 | tf_op jit(solution)/shard_map/ppermute | solution.py:73
  41.9 45.3 %collective-permute-start.5 = (bf16[512,1024]{1,0:T(8,128)(2,1)}, bf16[512,1024]{1,0:T(8,128)(2,1)}, u32[]{:S(2)}, u32[]{:S(2)}) collective-permute-start(bf16[512,1024]{1,0:T(8,128)(2,1)} %collective-permute-done.4.w_other), channel_id=1, source_target_pairs={{0,0},{1,1},{2,3},{3,2},{32,33},{33,32},{34,34},{35,35},{4,4},{5,5... | collective-permute-start | bytes 3145736 | tf_op jit(solution)/shard_map/ppermute | solution.py:69
  70.9 16.2 %collective-permute-start.3 = (bf16[64,1280]{1,0:T(8,128)(2,1)S(1)}, bf16[64,1280]{1,0:T(8,128)(2,1)S(1)}, u32[]{:S(2)}, u32[]{:S(2)}) collective-permute-start(bf16[64,1280]{1,0:T(8,128)(2,1)S(1)} %reshape.35.both), channel_id=1, source_target_pairs={{0,1},{1,0},{2,33},{3,32},{32,3},{33,2},{34,35},{35,34},{4,5},{5,4... | collective-permute-start | bytes 491528 | tf_op jit(solution)/shard_map/ppermute | solution.py:60
  71.0 16.1 %collective-permute-start.2 = (bf16[64,1280]{1,0:T(8,128)(2,1)S(1)}, bf16[64,1280]{1,0:T(8,128)(2,1)S(1)}, u32[]{:S(2)}, u32[]{:S(2)}) collective-permute-start(bf16[64,1280]{1,0:T(8,128)(2,1)S(1)} %reshape.35.both), channel_id=1, source_target_pairs={{0,0},{1,1},{2,32},{3,33},{32,2},{33,3},{34,34},{35,35},{4,4},{5,5... | collective-permute-start | bytes 491528 | tf_op jit(solution)/shard_map/ppermute | solution.py:60
  74.6 6.3 %collective-permute-start = (s32[1]{0:T(128)}, s32[1]{0:T(128)}, u32[]{:S(2)}, u32[]{:S(2)}) collective-permute-start(s32[1]{0:T(128)} %param.10), channel_id=1, source_target_pairs={{0,0},{1,1},{2,33},{3,32},{32,3},{33,2},{34,34},{35,35},{4,4},{5,5... | collective-permute-start | bytes 20 | tf_op jit(solution)/shard_map/ppermute | solution.py:56
  81.0 6.2 %collective-permute-start.1 = (s32[1]{0:T(128)}, s32[1]{0:T(128)}, u32[]{:S(2)}, u32[]{:S(2)}) collective-permute-start(s32[1]{0:T(128)} %param.11), channel_id=1, source_target_pairs={{0,0},{1,1},{2,33},{3,32},{32,3},{33,2},{34,34},{35,35},{4,4},{5,5... | collective-permute-start | bytes 20 | tf_op jit(solution)/shard_map/ppermute | solution.py:56
  101.1 2.7 %collective-permute-start.15 = (f32[8,512]{1,0:T(8,128)S(1)}, f32[8,512]{1,0:T(8,128)S(1)}, u32[]{:S(2)}, u32[]{:S(2)}) collective-permute-start(f32[8,512]{1,0:T(8,128)S(1)} %get-tuple-element.36.st), channel_id=1, source_target_pairs={{0,1},{1,0},{2,3},{3,2},{4,5},{5,4},{6,7},{7,6},{8,9},{9,8},{10,11... | collective-permute-start | bytes 49160 | tf_op jit(solution)/shard_map/ppermute | solution.py:77
  106.6 2.9 %collective-permute-start.16 = (bf16[8,576,128]{2,1,0:T(8,128)(2,1)S(1)}, bf16[8,576,128]{2,1,0:T(8,128)(2,1)S(1)}, u32[]{:S(2)}, u32[]{:S(2)}) collective-permute-start(bf16[8,576,128]{2,1,0:T(8,128)(2,1)S(1)} %get-tuple-element.40), channel_id=1, source_target_pairs={{0,32},{32,0},{1,33},{33,1},{2,34},{34,2},{3,35},{35,3},{4,36},{36... | collective-permute-start | bytes 3538952 | tf_op jit(solution)/shard_map/ppermute | solution.py:73
  113.4 17.1 %collective-permute-start.17 = (bf16[256,1152]{1,0:T(8,128)(2,1)S(1)}, bf16[256,1152]{1,0:T(8,128)(2,1)S(1)}, u32[]{:S(2)}, u32[]{:S(2)}) collective-permute-start(bf16[256,1152]{1,0:T(8,128)(2,1)S(1)} %get-tuple-element.53.held), channel_id=1, source_target_pairs={{0,0},{1,1},{2,3},{3,2},{32,33},{33,32},{34,34},{35,35},{4,4},{5,5... | collective-permute-start | bytes 1769480 | tf_op jit(solution)/shard_map/ppermute | solution.py:69
  130.6 10.8 %collective-permute-start.18 = (bf16[256,1152]{1,0:T(8,128)(2,1)S(1)}, bf16[256,1152]{1,0:T(8,128)(2,1)S(1)}, u32[]{:S(2)}, u32[]{:S(2)}) collective-permute-start(bf16[256,1152]{1,0:T(8,128)(2,1)S(1)} %add_convert_fusion), channel_id=1, source_target_pairs={{0,1},{1,0},{2,33},{3,32},{32,3},{33,2},{34,35},{35,34},{4,5},{5,4... | collective-permute-start | bytes 1769480 | tf_op jit(solution)/shard_map/ppermute | solution.py:60
  132.8 15.1 %collective-permute-start.24 = (bf16[576,128]{1,0:T(8,128)(2,1)S(1)}, bf16[576,128]{1,0:T(8,128)(2,1)S(1)}, u32[]{:S(2)}, u32[]{:S(2)}) collective-permute-start(bf16[576,128]{1,0:T(8,128)(2,1)S(1)} %get-tuple-element.62), channel_id=1, source_target_pairs={{0,28},{4,0},{8,4},{12,8},{16,12},{20,16},{24,20},{28,24},{1,29},{... | collective-permute-start | bytes 442376 | tf_op jit(solution)/shard_map/ppermute | solution.py:81
  143.3 38.6 %collective-permute-start.27 = (bf16[256,1024]{1,0:T(8,128)(2,1)S(1)}, bf16[256,1024]{1,0:T(8,128)(2,1)S(1)}, u32[]{:S(2)}, u32[]{:S(2)}) collective-permute-start(bf16[256,1024]{1,0:T(8,128)(2,1)S(1)} %get-tuple-element.64), channel_id=1, source_target_pairs={{0,32},{32,0},{1,33},{33,1},{2,34},{34,2},{3,35},{35,3},{4,36},{36... | collective-permute-start | bytes 1572872 | tf_op jit(solution)/shard_map/ppermute | solution.py:73
  143.4 15.7 %collective-permute-start.19 = (bf16[576,128]{1,0:T(8,128)(2,1)S(1)}, bf16[576,128]{1,0:T(8,128)(2,1)S(1)}, u32[]{:S(2)}, u32[]{:S(2)}) collective-permute-start(bf16[576,128]{1,0:T(8,128)(2,1)S(1)} %get-tuple-element.56), channel_id=1, source_target_pairs={{0,12},{4,16},{8,20},{12,24},{16,28},{20,0},{24,4},{28,8},{1,13},{... | collective-permute-start | bytes 442376 | tf_op jit(solution)/shard_map/ppermute | solution.py:81
  144.9 14.2 %collective-permute-start.20 = (bf16[576,128]{1,0:T(8,128)(2,1)S(1)}, bf16[576,128]{1,0:T(8,128)(2,1)S(1)}, u32[]{:S(2)}, u32[]{:S(2)}) collective-permute-start(bf16[576,128]{1,0:T(8,128)(2,1)S(1)} %get-tuple-element.57), channel_id=1, source_target_pairs={{0,24},{4,28},{8,0},{12,4},{16,8},{20,12},{24,16},{28,20},{1,25},{... | collective-permute-start | bytes 442376 | tf_op jit(solution)/shard_map/ppermute | solution.py:81
  148.0 15.4 %collective-permute-start.21 = (bf16[576,128]{1,0:T(8,128)(2,1)S(1)}, bf16[576,128]{1,0:T(8,128)(2,1)S(1)}, u32[]{:S(2)}, u32[]{:S(2)}) collective-permute-start(bf16[576,128]{1,0:T(8,128)(2,1)S(1)} %get-tuple-element.58), channel_id=1, source_target_pairs={{0,8},{4,12},{8,16},{12,20},{16,24},{20,28},{24,0},{28,4},{1,9},{5... | collective-permute-start | bytes 442376 | tf_op jit(solution)/shard_map/ppermute | solution.py:81
  148.0 15.4 %collective-permute-start.22 = (bf16[576,128]{1,0:T(8,128)(2,1)S(1)}, bf16[576,128]{1,0:T(8,128)(2,1)S(1)}, u32[]{:S(2)}, u32[]{:S(2)}) collective-permute-start(bf16[576,128]{1,0:T(8,128)(2,1)S(1)} %get-tuple-element.59), channel_id=1, source_target_pairs={{0,28},{4,0},{8,4},{12,8},{16,12},{20,16},{24,20},{28,24},{1,29},{... | collective-permute-start | bytes 442376 | tf_op jit(solution)/shard_map/ppermute | solution.py:81
  159.1 7.7 %collective-permute-start.23 = (bf16[576,128]{1,0:T(8,128)(2,1)S(1)}, bf16[576,128]{1,0:T(8,128)(2,1)S(1)}, u32[]{:S(2)}, u32[]{:S(2)}) collective-permute-start(bf16[576,128]{1,0:T(8,128)(2,1)S(1)} %get-tuple-element.60), channel_id=1, source_target_pairs={{0,4},{4,8},{8,12},{12,16},{16,20},{20,24},{24,28},{28,0},{1,5},{5... | collective-permute-start | bytes 442376 | tf_op jit(solution)/shard_map/ppermute | solution.py:81
  159.1 10.0 %collective-permute-start.25 = (bf16[576,128]{1,0:T(8,128)(2,1)S(1)}, bf16[576,128]{1,0:T(8,128)(2,1)S(1)}, u32[]{:S(2)}, u32[]{:S(2)}) collective-permute-start(bf16[576,128]{1,0:T(8,128)(2,1)S(1)} %add_convert_fusion.1), channel_id=1, source_target_pairs={{0,20},{4,24},{8,28},{12,0},{16,4},{20,8},{24,12},{28,16},{1,21},{... | collective-permute-start | bytes 442376 | tf_op jit(solution)/shard_map/ppermute | solution.py:81
  169.3 17.1 %collective-permute-start.26 = (bf16[576,128]{1,0:T(8,128)(2,1)S(1)}, bf16[576,128]{1,0:T(8,128)(2,1)S(1)}, u32[]{:S(2)}, u32[]{:S(2)}) collective-permute-start(bf16[576,128]{1,0:T(8,128)(2,1)S(1)} %shard_map.93), channel_id=1, source_target_pairs={{0,0},{1,1},{2,33},{3,32},{32,3},{33,2},{34,34},{35,35},{4,4},{5,5... | collective-permute-start | bytes 442376 | tf_op jit(solution)/shard_map/ppermute | solution.py:56
  176.8 14.2 %all-to-all-start.1 = ((bf16[32,2,768]{2,1,0:T(2,128)(2,1)}), bf16[32,2,768]{2,1,0:T(2,128)(2,1)S(1)}, u32[]{:S(2)}, u32[]{:S(2)}) async-start(bf16[32,2,768]{2,1,0:T(2,128)(2,1)} %reshape.36), calls=%async_computation.1 | async-start | bytes 196608 | tf_op jit(solution)/shard_map/all_to_all | solution.py:430
  182.1 9.7 %collective-permute-start.28 = (bf16[64,1024]{1,0:T(8,128)(2,1)S(1)}, bf16[64,1024]{1,0:T(8,128)(2,1)S(1)}, u32[]{:S(2)}, u32[]{:S(2)}) collective-permute-start(bf16[64,1024]{1,0:T(8,128)(2,1)S(1)} %get-tuple-element.65), channel_id=1, source_target_pairs={{0,64},{64,128},{128,192},{192,0},{1,65},{65,129},{129,193},{193,1... | collective-permute-start | bytes 393224 | tf_op jit(solution)/shard_map/ppermute | solution.py:428
  183.4 8.4 %collective-permute-start.30 = (bf16[64,1024]{1,0:T(8,128)(2,1)S(1)}, bf16[64,1024]{1,0:T(8,128)(2,1)S(1)}, u32[]{:S(2)}, u32[]{:S(2)}) collective-permute-start(bf16[64,1024]{1,0:T(8,128)(2,1)S(1)} %get-tuple-element.66), channel_id=1, source_target_pairs={{0,192},{64,0},{128,64},{192,128},{1,193},{65,1},{129,65},{193,129... | collective-permute-start | bytes 393224 | tf_op jit(solution)/shard_map/ppermute | solution.py:428
  184.9 7.0 %collective-permute-start.29 = (bf16[64,1024]{1,0:T(8,128)(2,1)S(1)}, bf16[64,1024]{1,0:T(8,128)(2,1)S(1)}, u32[]{:S(2)}, u32[]{:S(2)}) collective-permute-start(bf16[64,1024]{1,0:T(8,128)(2,1)S(1)} %get-tuple-element.67), channel_id=1, source_target_pairs={{0,128},{64,192},{128,0},{192,64},{1,129},{65,193},{129,1},{193,65... | collective-permute-start | bytes 393224 | tf_op jit(solution)/shard_map/ppermute | solution.py:428

commit v3 on v1

--- a/solution.py
+++ b/solution.py
@@ -59,6 +59,17 @@
     return lax.ppermute(v, ("core", "y"), turned(flip))
 
 
+def homeward(v, d):
+    pairs = []
+    for c in range(2):
+        for z in range(NZ):
+            for y in range(NY):
+                here = (y >> 1) == c
+                to = (c, y) if here else (1 - c, 3 - y)
+                pairs.append(((c * NZ + z) * NY + y, (to[0] * NZ + (z + d) % NZ) * NY + to[1]))
+    return lax.ppermute(v, ("core", "z", "y"), pairs)
+
+
 def other_core(v):
     return lax.ppermute(v, "core", [(0, 1), (1, 0)])
 
@@ -73,6 +84,10 @@
 
 def dot(a, b, da=1, db=0):
     return lax.dot_general(a, b, (((da,), (db,)), ((), ())), preferred_element_type=F32)
+
+
+def in_hbm(v):
+    return pltpu.with_memory_space_constraint(v, pltpu.HBM)
 
 
 def vmem(shape, dtype):
@@ -211,7 +226,7 @@
     refs[NZ][...] = acc.astype(BF)
 
 
-def first_body(st, their, mine, other, ee, qq, ws, out):
+def row_factors(st, their, ws):
     there = jnp.concatenate([their[:, ROWS:], their[:, :ROWS]], axis=1)
     m, l, rd = st[0:1, :], st[1:2, :], st[2:3, :]
     m2, l2, rd2 = there[0:1, :], there[1:2, :], there[2:3, :]
@@ -220,9 +235,11 @@
     a2 = jnp.exp(m2 - top)
     denom = l * a + l2 * a2
     shift = (rd * l * a + rd2 * l2 * a2) / denom - rd
-    w = a / denom
     row = lax.broadcasted_iota(jnp.int32, (BLK, 2 * ROWS), 0)
-    ws[...] = jnp.transpose(jnp.where(row == 0, w, shift))
+    ws[...] = jnp.transpose(jnp.where(row == 0, a / denom, shift))
+
+
+def first_body(ws, mine, other, ee, qq, out):
     step = 64
     for half, qg in ((0, mine), (1, other)):
 
@@ -249,7 +266,8 @@
     key_parts(qq, ee, out)
 
 
-def query_body(ws, kt, e0, e1, mine, other):
+def query_body(st, their, kt, e0, e1, mine, other, ws):
+    row_factors(st, their, ws)
     for half, out in ((0, mine), (1, other)):
         xs = []
         for top in (0, 2 * ROWS):
@@ -314,13 +332,14 @@
     (qg,) = call(
         latents_body,
         [vmem((ROWS, WIDE), BF)],
-        (query_start, key_lengths, both, latent_up),
+        (query_start, key_lengths, both, in_hbm(latent_up)),
         270_000_000,
         smem=2,
+        mib=12,
     )
     qg_mine = turn(qg, 0)
     qg_other = turn(qg, 1)
-    (mine_side,) = call(join_body, [vmem((W, NZ * BLK), BF)], kept, 1_000_000)
+    (mine_side,) = call(join_body, [vmem((W, NZ * BLK), BF)], kept, 1_000_000, mib=6)
     their_side = other_core(mine_side)
 
     zi = lax.axis_index("z")
@@ -340,39 +359,39 @@
     )
     theirs = pair_y(stats)
 
+    mine, other, ws = call(
+        query_body,
+        [vmem((ROWS, WIDE), BF), vmem((ROWS, WIDE), BF), vmem((2 * ROWS, BLK), F32)],
+        (stats, theirs, kt, e_mine, e_their),
+        2_400_000_000,
+    )
+    mine, other = turn(mine, 0), turn(other, 1)
     piece = vmem((NZ, W, BLK), BF)
-    qq, ws, their_keys = call(
+    qq, their_keys = call(
         first_body,
-        [vmem((4 * ROWS, W), BF), vmem((2 * ROWS, BLK), F32), piece],
-        (stats, theirs, qg_mine, qg_other, e_their),
+        [vmem((4 * ROWS, W), BF), piece],
+        (ws, qg_mine, qg_other, e_their),
         1_300_000_000,
     )
     their_keys = other_core(their_keys)
     (mine_keys,) = call(parts_body, [piece], (qq, e_mine), 1_200_000_000)
-    sums = call(add_body, [vmem((W, BLK), BF)] * NZ, (mine_keys, their_keys), 1_000_000)
-    sums, ws = lax.optimization_barrier((sums, ws))
-    moved = [sums[0]]
-    for n, d in enumerate(OFFSETS[1:]):
-        moved.append(along_z(sums[n + 1], d))
-    (total,) = call(total_body, [vmem((W, BLK), BF)], moved, 1_000_000)
-    key_grad = swap(total).astype(F32).T
-
-    mine, other = call(
-        query_body,
-        [vmem((ROWS, WIDE), BF), vmem((ROWS, WIDE), BF)],
-        (ws, kt, e_mine, e_their),
-        2_400_000_000,
-    )
-    mine, other = turn(mine, 0), turn(other, 1)
+    sums = call(add_body, [vmem((W, BLK), BF)] * NZ, (mine_keys, their_keys), 1_000_000, mib=8)
+    moved = []
+    for n in (1, 2, 3, 4, 5, 0, 6, 7):
+        moved.append(homeward(sums[n], OFFSETS[n]))
+    (total,) = call(total_body, [vmem((W, BLK), BF)], moved, 1_000_000, mib=4)
+    key_grad = total.astype(F32).T
+
     qo = (mine.astype(F32) + other.astype(F32)).astype(BF)
     wide = HEADS * (DN + DV)
     gq, keep, send = call(
         tail_body,
         [vmem((NQ, HEADS * (DN + DR)), BF)] + [vmem((C // 2, wide), BF)] * 2,
-        (scal, qo, both, latent_up),
+        (scal, qo, both, in_hbm(latent_up)),
         200_000_000,
         (pltpu.VMEM((C, wide), BF),),
         smem=1,
+        mib=12,
     )
     got = other_core(send)
     n = C // 8

time: 179 us -> 176 us (0.983)
  waiting for transfers between devices: 67.4 us -> 55.8 us
  Pallas kernels: 22.4 us -> 26.2 us
  local copies, waits for them, and re-layouts: 0.76 us -> 3.11 us
  other arithmetic: 3.43 us -> 5.24 us
    ppermute x0 -> x8, starting transfers between devices: none -> 25 us  [homeward(): return lax.ppermute(v, ('core', 'z', 'y'), pairs)]
    ppermute x14 -> x7, starting transfers between devices: 36.8 us -> 17 us  [along_z(): return lax.ppermute(v, 'z', [(i, (i + step) % NZ) for i in range(NZ)])]
    ppermute x14 -> x7, waiting for transfers between devices: 20.6 us -> 10.5 us  [along_z(): return lax.ppermute(v, 'z', [(i, (i + step) % NZ) for i in range(NZ)])]
    ppermute x2 -> x1, starting transfers between devices: 13 us -> 6.15 us  [swap(): return lax.ppermute(v, ('core', 'y'), swap_pairs())]
    ppermute x4, waiting for transfers between devices: 26.9 us -> 20.5 us  [turn(): return lax.ppermute(v, ('core', 'y'), turned(flip))]
    ppermute x0 -> x8, waiting for transfers between devices: none -> 5.89 us  [homeward(): return lax.ppermute(v, ('core', 'z', 'y'), pairs)]
    all_to_all x1, waiting for transfers between devices: 4.37 us -> 0.01 us  [step(): lax.all_to_all(gq.reshape(ndev, own_q, HEADS * (DN + DR)), CTX, 0, 0, til...]
    pallas_call x9, Pallas kernels: 22.4 us -> 26.2 us  [call(): pl.pallas_call(body, out_shape=out_shape, in_specs=specs, out_specs=[pl.B...]
  transfers between devices with their start and end apart: 29 -> 29, of which waited for: 16 -> 15; matrix products, arithmetic and copies ran while one was open for 2% -> 3% of each run, Pallas kernels for 1% -> 7%
where the time goes in v3:
time: 176 us; the launch traced here: 174 us
  starting transfers between devices  81.9 us (47%)
  waiting for transfers between devices  55.8 us (32%)
  Pallas kernels  26.2 us (15%)
  other arithmetic  5.24 us (3%)
  local copies, waits for them, and re-layouts  3.11 us (2%)
  between operations  2.19 us (1%)
    pallas_call x9, Pallas kernels, call(): pl.pallas_call(body, out_shape=out_shape, in_specs=specs, out_specs=[pl.B...  26.2 us
    ppermute x8, starting transfers between devices, homeward(): return lax.ppermute(v, ('core', 'z', 'y'), pairs)  25 us
    ppermute x4, waiting for transfers between devices, turn(): return lax.ppermute(v, ('core', 'y'), turned(flip))  20.5 us
    ppermute x7, starting transfers between devices, along_z(): return lax.ppermute(v, 'z', [(i, (i + step) % NZ) for i in range(NZ)])  17 us
    all_to_all x1, starting transfers between devices, step(): both = lax.all_to_all(both, CTX, 0, 0, tiled=True)  12.4 us
    ppermute x4, starting transfers between devices, turn(): return lax.ppermute(v, ('core', 'y'), turned(flip))  11.2 us
    ppermute x7, waiting for transfers between devices, along_z(): return lax.ppermute(v, 'z', [(i, (i + step) % NZ) for i in range(NZ)])  10.5 us
    all_to_all x1, waiting for transfers between devices, step(): both = lax.all_to_all(both, CTX, 0, 0, tiled=True)  8.9 us
  transfers between devices with their start and end apart: 29, of which 15 were waited for; matrix products, arithmetic and copies ran while one was open for 3% of the time, Pallas kernels for 7%

profile of v3, /device:TPU:1, one launch (start us, length us, event | category | flops | bytes accessed | tf_op | source)
XLA Modules:
  0.0 174.5 jit_solution(16007108641515988773)
XLA Ops:
  0.7 6.2 %collective-permute-start.2 = (bf16[576,128]{1,0:T(8,128)(2,1)}, bf16[576,128]{1,0:T(8,128)(2,1)S(1)}, u32[]{:S(2)}, u32[]{:S(2)}) collective-permute-start(bf16[576,128]{1,0:T(8,128)(2,1)} %bitcast.21), channel_id=1, source_target_pairs={{0,0},{1,1},{2,33},{3,32},{32,3},{33,2},{34,34},{35,35},{4,4},{5,5... | collective-permute-start | bytes 442376 | tf_op jit(solution)/shard_map/ppermute | solution.py:55
  6.8 3.0 %collective-permute-done.2.refs_0_ = bf16[576,128]{1,0:T(8,128)(2,1)S(1)} collective-permute-done((bf16[576,128]{1,0:T(8,128)(2,1)}, bf16[576,128]{1,0:T(8,128)(2,1)S(1)}, u32[]{:S(2)}, u32[]{:S(2)}) %collective-permute-start.2) | collective-permute-done | bytes 147488 | tf_op jit(solution)/shard_map/ppermute | solution.py:55
  9.8 5.6 %collective-permute-start.9 = (bf16[576,128]{1,0:T(8,128)(2,1)S(1)}, bf16[576,128]{1,0:T(8,128)(2,1)S(1)}, u32[]{:S(2)}, u32[]{:S(2)}) collective-permute-start(bf16[576,128]{1,0:T(8,128)(2,1)S(1)} %collective-permute-done.2.refs_0_), channel_id=1, source_target_pairs={{0,28},{4,0},{8,4},{12,8},{16,12},{20,16},{24,20},{28,24},{1,29},{... | collective-permute-start | bytes 442376 | tf_op jit(solution)/shard_map/ppermute | solution.py:82
  15.4 1.9 %collective-permute-start.7 = (bf16[576,128]{1,0:T(8,128)(2,1)S(1)}, bf16[576,128]{1,0:T(8,128)(2,1)S(1)}, u32[]{:S(2)}, u32[]{:S(2)}) collective-permute-start(bf16[576,128]{1,0:T(8,128)(2,1)S(1)} %collective-permute-done.2.refs_0_), channel_id=1, source_target_pairs={{0,24},{4,28},{8,0},{12,4},{16,8},{20,12},{24,16},{28,20},{1,25},{... | collective-permute-start | bytes 442376 | tf_op jit(solution)/shard_map/ppermute | solution.py:82
  17.8 2.5 %collective-permute-start.5 = (bf16[576,128]{1,0:T(8,128)(2,1)S(1)}, bf16[576,128]{1,0:T(8,128)(2,1)S(1)}, u32[]{:S(2)}, u32[]{:S(2)}) collective-permute-start(bf16[576,128]{1,0:T(8,128)(2,1)S(1)} %collective-permute-done.2.refs_0_), channel_id=1, source_target_pairs={{0,20},{4,24},{8,28},{12,0},{16,4},{20,8},{24,12},{28,16},{1,21},{... | collective-permute-start | bytes 442376 | tf_op jit(solution)/shard_map/ppermute | solution.py:82
  20.3 0.8 collective-permute-done.9.refs_7_
  21.3 1.0 collective-permute-done.8.refs_6_
  22.3 6.3 %collective-permute-start.3 = (bf16[576,128]{1,0:T(8,128)(2,1)S(1)}, bf16[576,128]{1,0:T(8,128)(2,1)S(1)}, u32[]{:S(2)}, u32[]{:S(2)}) collective-permute-start(bf16[576,128]{1,0:T(8,128)(2,1)S(1)} %collective-permute-done.2.refs_0_), channel_id=1, source_target_pairs={{0,16},{4,20},{8,24},{12,28},{16,0},{20,4},{24,8},{28,12},{1,17},{... | collective-permute-start | bytes 442376 | tf_op jit(solution)/shard_map/ppermute | solution.py:82
  28.6 3.8 %collective-permute-done.6.refs_4_ = bf16[576,128]{1,0:T(8,128)(2,1)S(1)} collective-permute-done((bf16[576,128]{1,0:T(8,128)(2,1)S(1)}, bf16[576,128]{1,0:T(8,128)(2,1)S(1)}, u32[]{:S(2)}, u32[]{:S(2)}) %collective-permute-start.6) | collective-permute-done | bytes 147488 | tf_op jit(solution)/shard_map/ppermute | solution.py:82
  32.4 4.8 %collective-permute-done.5.refs_3_ = bf16[576,128]{1,0:T(8,128)(2,1)S(1)} collective-permute-done((bf16[576,128]{1,0:T(8,128)(2,1)S(1)}, bf16[576,128]{1,0:T(8,128)(2,1)S(1)}, u32[]{:S(2)}, u32[]{:S(2)}) %collective-permute-start.5) | collective-permute-done | bytes 147488 | tf_op jit(solution)/shard_map/ppermute | solution.py:82
  37.7 0.8 maximum_bitcast_fusion
  38.6 12.4 %all-to-all-start = ((bf16[32,2,1280]{2,1,0:T(2,128)(2,1)}), bf16[32,2,1280]{2,1,0:T(2,128)(2,1)S(1)}, u32[]{:S(2)}, u32[]{:S(2)}) async-start(bf16[32,2,1280]{2,1,0:T(2,128)(2,1)} %maximum_bitcast_fusion), calls=%async_computation | async-start | bytes 327680 | tf_op jit(solution)/shard_map/all_to_all | solution.py:327
  52.2 8.9 %all-to-all-done = bf16[32,2,1280]{2,1,0:T(2,128)(2,1)S(1)} async-done(((bf16[32,2,1280]{2,1,0:T(2,128)(2,1)}), bf16[32,2,1280]{2,1,0:T(2,128)(2,1)S(1)}, u32[]{:S(2)}, u32[]{:S(2)}) %all-to-all-start) | async-done | bytes 163872 | tf_op jit(solution)/shard_map/all_to_all | solution.py:327
  61.2 1.7 shard_map.85
  62.9 2.9 %collective-permute-start.1 = (bf16[256,1152]{1,0:T(8,128)(2,1)S(1)}, bf16[256,1152]{1,0:T(8,128)(2,1)}, u32[]{:S(2)}, u32[]{:S(2)}) collective-permute-start(bf16[256,1152]{1,0:T(8,128)(2,1)S(1)} %shard_map.85), channel_id=1, source_target_pairs={{0,1},{1,0},{2,33},{3,32},{32,3},{33,2},{34,35},{35,34},{4,5},{5,4... | collective-permute-start | bytes 1769480 | tf_op jit(solution)/shard_map/ppermute | solution.py:59
  65.8 1.9 %collective-permute-start = (bf16[256,1152]{1,0:T(8,128)(2,1)S(1)}, bf16[256,1152]{1,0:T(8,128)(2,1)}, u32[]{:S(2)}, u32[]{:S(2)}) collective-permute-start(bf16[256,1152]{1,0:T(8,128)(2,1)S(1)} %shard_map.85), channel_id=1, source_target_pairs={{0,0},{1,1},{2,32},{3,33},{32,2},{33,3},{34,34},{35,35},{4,4},{5,5... | collective-permute-start | bytes 1769480 | tf_op jit(solution)/shard_map/ppermute | solution.py:59
  67.8 12.2 %collective-permute-done.1.refs_2_.other = bf16[256,1152]{1,0:T(8,128)(2,1)} collective-permute-done((bf16[256,1152]{1,0:T(8,128)(2,1)S(1)}, bf16[256,1152]{1,0:T(8,128)(2,1)}, u32[]{:S(2)}, u32[]{:S(2)}) %collective-permute-start.1) | collective-permute-done | bytes 589856 | tf_op jit(solution)/shard_map/ppermute | solution.py:59
  79.9 1.0 copy-done.3
  81.0 1.3 copy-done.4
  82.2 10.4 %shard_map.87 = (bf16[1024,1024]{1,0:T(8,128)(2,1)S(1)}, bf16[1024,1024]{1,0:T(8,128)(2,1)S(1)}, bf16[576,2048]{1,0:T(8,128)(2,1)S(1)}, f32[8,512]{1,0:T(8,128)S(1)}) custom-call(s32[4]{0:T(128)S(1)} %pad_add_fusion.refs_0_.scal, bf16[256,1152]{1,0:T(8,128)(2,1)} %collective-permute-done.refs_1_.mine, ...), custom_call_target="tpu_custom_call" | custom-call | flops 2280000000 | bytes 10108944 | tf_op jit(solution)/shard_map/pallas_call | solution.py:102
  92.9 2.9 %collective-permute-done.11.their = f32[8,512]{1,0:T(8,128)S(1)} collective-permute-done((f32[8,512]{1,0:T(8,128)S(1)}, f32[8,512]{1,0:T(8,128)S(1)}, u32[]{:S(2)}, u32[]{:S(2)}) %collective-permute-start.11) | collective-permute-done | bytes 16416 | tf_op jit(solution)/shard_map/ppermute | solution.py:78
  95.8 3.5 %shard_map.88 = (bf16[256,1152]{1,0:T(8,128)(2,1)S(1)}, bf16[256,1152]{1,0:T(8,128)(2,1)S(1)}, f32[512,128]{1,0:T(8,128)S(1)}) custom-call(f32[8,512]{1,0:T(8,128)S(1)} %get-tuple-element.23.st, f32[8,512]{1,0:T(8,128)S(1)} %collective-permute-done.11.their, bf16[576,2048]{1,0:T(8,128)(2,1)S(1)} %get-tuple-element.24.kt, ...), custom_call_target="tpu_custom_call" | custom-call | flops 2400000000 | bytes 8028160 | tf_op jit(solution)/shard_map/pallas_call | solution.py:102
  99.4 5.8 %collective-permute-start.12 = (bf16[256,1152]{1,0:T(8,128)(2,1)S(1)}, bf16[256,1152]{1,0:T(8,128)(2,1)S(1)}, u32[]{:S(2)}, u32[]{:S(2)}) collective-permute-start(bf16[256,1152]{1,0:T(8,128)(2,1)S(1)} %get-tuple-element.27), channel_id=1, source_target_pairs={{0,0},{1,1},{2,32},{3,33},{32,2},{33,3},{34,34},{35,35},{4,4},{5,5... | collective-permute-start | bytes 1769480 | tf_op jit(solution)/shard_map/ppermute | solution.py:59
  105.8 4.9 %shard_map.90 = (bf16[1024,576]{1,0:T(8,128)(2,1)S(1)}, bf16[8,576,128]{2,1,0:T(8,128)(2,1)}) custom-call(f32[512,128]{1,0:T(8,128)S(1)} %get-tuple-element.30.ws, bf16[256,1152]{1,0:T(8,128)(2,1)} %collective-permute-done.refs_1_.mine, bf16[256,1152]{1,0:T(8,128)(2,1)} %collective-permute-done.1.refs_2_.other, bf16[1024,1024]{1,0:T(8,128)(2,1)S(1)} %get-tuple-element.26.e1.ee), custom_call_target="tpu_custom_call" | custom-call | flops 1300000000 | bytes 5898240 | tf_op jit(solution)/shard_map/pallas_call | solution.py:102
  110.7 3.2 %collective-permute-done.12 = bf16[256,1152]{1,0:T(8,128)(2,1)S(1)} collective-permute-done((bf16[256,1152]{1,0:T(8,128)(2,1)S(1)}, bf16[256,1152]{1,0:T(8,128)(2,1)S(1)}, u32[]{:S(2)}, u32[]{:S(2)}) %collective-permute-start.12) | collective-permute-done | bytes 589856 | tf_op jit(solution)/shard_map/ppermute | solution.py:59
  113.9 5.1 %collective-permute-done.13 = bf16[256,1152]{1,0:T(8,128)(2,1)S(1)} collective-permute-done((bf16[256,1152]{1,0:T(8,128)(2,1)S(1)}, bf16[256,1152]{1,0:T(8,128)(2,1)S(1)}, u32[]{:S(2)}, u32[]{:S(2)}) %collective-permute-start.13) | collective-permute-done | bytes 589856 | tf_op jit(solution)/shard_map/ppermute | solution.py:59
  119.2 1.9 %shard_map.89 = (bf16[64,768]{1,0:T(8,128)(2,1)S(1)}, bf16[256,1024]{1,0:T(8,128)(2,1)S(1)}, bf16[256,1024]{1,0:T(8,128)(2,1)S(1)}) custom-call(s32[4]{0:T(128)S(1)} %pad_add_fusion.refs_0_.scal, bf16[256,1152]{1,0:T(8,128)(2,1)S(1)} %add_convert_fusion.qo, bf16[64,1280]{1,0:T(8,128)(2,1)S(1)} %reshape.35.both, bf16[512,1024]{1,0:T(8,128)(2,1)} %w.3), custom_call_target="tpu_custom_call" | custom-call | flops 200000000 | bytes 2949136 | tf_op jit(solution)/shard_map/pallas_call | solution.py:102
  121.2 1.9 %collective-permute-done.23 = bf16[256,1024]{1,0:T(8,128)(2,1)S(1)} collective-permute-done((bf16[256,1024]{1,0:T(8,128)(2,1)S(1)}, bf16[256,1024]{1,0:T(8,128)(2,1)S(1)}, u32[]{:S(2)}, u32[]{:S(2)}) %collective-permute-start.23) | collective-permute-done | bytes 524320 | tf_op jit(solution)/shard_map/ppermute | solution.py:74
  123.1 0.9 add_convert_fusion.3
  124.0 1.2 collective-permute-start.24
  125.9 5.6 %all-to-all-start.1 = ((bf16[32,2,768]{2,1,0:T(2,128)(2,1)}), bf16[32,2,768]{2,1,0:T(2,128)(2,1)S(1)}, u32[]{:S(2)}, u32[]{:S(2)}) async-start(bf16[32,2,768]{2,1,0:T(2,128)(2,1)} %reshape.36), calls=%async_computation.1 | async-start | bytes 196608 | tf_op jit(solution)/shard_map/all_to_all | solution.py:404
  131.5 1.7 shard_map.91.a
  133.3 1.6 shard_map.92
  134.9 8.4 %collective-permute-start.15 = (bf16[576,128]{1,0:T(8,128)(2,1)S(1)}, bf16[576,128]{1,0:T(8,128)(2,1)S(1)}, u32[]{:S(2)}, u32[]{:S(2)}) collective-permute-start(bf16[576,128]{1,0:T(8,128)(2,1)S(1)} %get-tuple-element.33), channel_id=1, source_target_pairs={{0,16},{1,17},{2,49},{3,48},{4,20},{5,21},{6,53},{7,52},{8,24},{9,... | collective-permute-start | bytes 442376 | tf_op jit(solution)/shard_map/ppermute | solution.py:70
  143.3 5.7 %collective-permute-start.17 = (bf16[576,128]{1,0:T(8,128)(2,1)S(1)}, bf16[576,128]{1,0:T(8,128)(2,1)S(1)}, u32[]{:S(2)}, u32[]{:S(2)}) collective-permute-start(bf16[576,128]{1,0:T(8,128)(2,1)S(1)} %get-tuple-element.35), channel_id=1, source_target_pairs={{0,12},{1,13},{2,45},{3,44},{4,16},{5,17},{6,49},{7,48},{8,20},{9,... | collective-permute-start | bytes 442376 | tf_op jit(solution)/shard_map/ppermute | solution.py:70
  149.0 1.4 collective-permute-start.26
  150.5 1.5 collective-permute-start.25
  152.0 0.7 convert_element_type.90
  152.7 0.8 collective-permute-done.26
  153.6 1.1 collective-permute-start.18
  154.6 1.4 collective-permute-done.25
  156.1 2.2 %collective-permute-start.19 = (bf16[576,128]{1,0:T(8,128)(2,1)S(1)}, bf16[576,128]{1,0:T(8,128)(2,1)S(1)}, u32[]{:S(2)}, u32[]{:S(2)}) collective-permute-start(bf16[576,128]{1,0:T(8,128)(2,1)S(1)} %get-tuple-element.37), channel_id=1, source_target_pairs={{0,8},{1,9},{2,41},{3,40},{4,12},{5,13},{6,45},{7,44},{8,16},{9,17... | collective-permute-start | bytes 442376 | tf_op jit(solution)/shard_map/ppermute | solution.py:70
  158.3 3.6 %collective-permute-start.20 = (bf16[576,128]{1,0:T(8,128)(2,1)S(1)}, bf16[576,128]{1,0:T(8,128)(2,1)S(1)}, u32[]{:S(2)}, u32[]{:S(2)}) collective-permute-start(bf16[576,128]{1,0:T(8,128)(2,1)S(1)} %get-tuple-element.38), channel_id=1, source_target_pairs={{0,0},{1,1},{2,33},{3,32},{4,4},{5,5},{6,37},{7,36},{8,8},{9,9},{1... | collective-permute-start | bytes 442376 | tf_op jit(solution)/shard_map/ppermute | solution.py:70
  161.9 3.8 %collective-permute-start.21 = (bf16[576,128]{1,0:T(8,128)(2,1)S(1)}, bf16[576,128]{1,0:T(8,128)(2,1)S(1)}, u32[]{:S(2)}, u32[]{:S(2)}) collective-permute-start(bf16[576,128]{1,0:T(8,128)(2,1)S(1)} %get-tuple-element.39), channel_id=1, source_target_pairs={{0,28},{1,29},{2,61},{3,60},{4,0},{5,1},{6,33},{7,32},{8,4},{9,5},... | collective-permute-start | bytes 442376 | tf_op jit(solution)/shard_map/ppermute | solution.py:70
  165.9 1.8 %convert_add_fusion = f32[64,1024]{1,0:T(8,128)} fusion(bf16[64,1024]{1,0:T(8,128)(2,1)S(1)} %collective-permute-done.26, bf16[64,1024]{1,0:T(8,128)(2,1)S(1)} %collective-permute-done.25, bf16[64,1024]{1,0:T(8,128)(2,1)} %collective-permute-done.24, bf16[256,1024]{1,0:T(8,128)(2,1)} %copy-done.5, bf16[256,1024]{1,0:T(8,128)(2,1)} %copy-done.2), kind=kLoop, calls=%fused_computation.2 | loop fusion | flops 589824 | bytes 917504 | tf_op jit(solution)/shard_map/add | solution.py:403
  167.7 1.7 collective-permute-done.20.refs_5_
  169.4 4.2 %collective-permute-done.22.refs_7_ = bf16[576,128]{1,0:T(8,128)(2,1)S(1)} collective-permute-done((bf16[576,128]{1,0:T(8,128)(2,1)S(1)}, bf16[576,128]{1,0:T(8,128)(2,1)S(1)}, u32[]{:S(2)}, u32[]{:S(2)}) %collective-permute-start.22) | collective-permute-done | bytes 147488 | tf_op jit(solution)/shard_map/ppermute | solution.py:70
  173.7 0.7 convert_bitcast_fusion
  (48 shorter events, 3.6 us)
Async XLA Ops:
  0.6 37.1 %copy-start.8 = (bf16[1,2,24576]{2,1,0:T(2,128)(2,1)S(1)}, bf16[1,2,24576]{2,1,0:T(2,128)(2,1)}, u32[]{:S(2)}) copy-start(bf16[1,2,24576]{2,1,0:T(2,128)(2,1)} %param.6) | copy-start | bytes 294916
  0.6 37.1 %copy-start.9 = (bf16[1,2,16384]{2,1,0:T(2,128)(2,1)S(1)}, bf16[1,2,16384]{2,1,0:T(2,128)(2,1)}, u32[]{:S(2)}) copy-start(bf16[1,2,16384]{2,1,0:T(2,128)(2,1)} %param.7) | copy-start | bytes 196612
  0.7 9.2 %collective-permute-start.2 = (bf16[576,128]{1,0:T(8,128)(2,1)}, bf16[576,128]{1,0:T(8,128)(2,1)S(1)}, u32[]{:S(2)}, u32[]{:S(2)}) collective-permute-start(bf16[576,128]{1,0:T(8,128)(2,1)} %bitcast.21), channel_id=1, source_target_pairs={{0,0},{1,1},{2,33},{3,32},{32,3},{33,2},{34,34},{35,35},{4,4},{5,5... | collective-permute-start | bytes 442376 | tf_op jit(solution)/shard_map/ppermute | solution.py:55
  9.8 11.2 %collective-permute-start.9 = (bf16[576,128]{1,0:T(8,128)(2,1)S(1)}, bf16[576,128]{1,0:T(8,128)(2,1)S(1)}, u32[]{:S(2)}, u32[]{:S(2)}) collective-permute-start(bf16[576,128]{1,0:T(8,128)(2,1)S(1)} %collective-permute-done.2.refs_0_), channel_id=1, source_target_pairs={{0,28},{4,0},{8,4},{12,8},{16,12},{20,16},{24,20},{28,24},{1,29},{... | collective-permute-start | bytes 442376 | tf_op jit(solution)/shard_map/ppermute | solution.py:82
  15.4 6.9 %collective-permute-start.8 = (bf16[576,128]{1,0:T(8,128)(2,1)S(1)}, bf16[576,128]{1,0:T(8,128)(2,1)S(1)}, u32[]{:S(2)}, u32[]{:S(2)}) collective-permute-start(bf16[576,128]{1,0:T(8,128)(2,1)S(1)} %collective-permute-done.2.refs_0_), channel_id=1, source_target_pairs={{0,4},{4,8},{8,12},{12,16},{16,20},{20,24},{24,28},{28,0},{1,5},{5... | collective-permute-start | bytes 442376 | tf_op jit(solution)/shard_map/ppermute | solution.py:82
  15.4 13.2 %collective-permute-start.7 = (bf16[576,128]{1,0:T(8,128)(2,1)S(1)}, bf16[576,128]{1,0:T(8,128)(2,1)S(1)}, u32[]{:S(2)}, u32[]{:S(2)}) collective-permute-start(bf16[576,128]{1,0:T(8,128)(2,1)S(1)} %collective-permute-done.2.refs_0_), channel_id=1, source_target_pairs={{0,24},{4,28},{8,0},{12,4},{16,8},{20,12},{24,16},{28,20},{1,25},{... | collective-permute-start | bytes 442376 | tf_op jit(solution)/shard_map/ppermute | solution.py:82
  17.3 15.1 %collective-permute-start.6 = (bf16[576,128]{1,0:T(8,128)(2,1)S(1)}, bf16[576,128]{1,0:T(8,128)(2,1)S(1)}, u32[]{:S(2)}, u32[]{:S(2)}) collective-permute-start(bf16[576,128]{1,0:T(8,128)(2,1)S(1)} %collective-permute-done.2.refs_0_), channel_id=1, source_target_pairs={{0,8},{4,12},{8,16},{12,20},{16,24},{20,28},{24,0},{28,4},{1,9},{5... | collective-permute-start | bytes 442376 | tf_op jit(solution)/shard_map/ppermute | solution.py:82
  17.8 19.5 %collective-permute-start.5 = (bf16[576,128]{1,0:T(8,128)(2,1)S(1)}, bf16[576,128]{1,0:T(8,128)(2,1)S(1)}, u32[]{:S(2)}, u32[]{:S(2)}) collective-permute-start(bf16[576,128]{1,0:T(8,128)(2,1)S(1)} %collective-permute-done.2.refs_0_), channel_id=1, source_target_pairs={{0,20},{4,24},{8,28},{12,0},{16,4},{20,8},{24,12},{28,16},{1,21},{... | collective-permute-start | bytes 442376 | tf_op jit(solution)/shard_map/ppermute | solution.py:82
  21.1 16.2 %collective-permute-start.4 = (bf16[576,128]{1,0:T(8,128)(2,1)S(1)}, bf16[576,128]{1,0:T(8,128)(2,1)S(1)}, u32[]{:S(2)}, u32[]{:S(2)}) collective-permute-start(bf16[576,128]{1,0:T(8,128)(2,1)S(1)} %collective-permute-done.2.refs_0_), channel_id=1, source_target_pairs={{0,12},{4,16},{8,20},{12,24},{16,28},{20,0},{24,4},{28,8},{1,13},{... | collective-permute-start | bytes 442376 | tf_op jit(solution)/shard_map/ppermute | solution.py:82
  22.3 15.0 %collective-permute-start.3 = (bf16[576,128]{1,0:T(8,128)(2,1)S(1)}, bf16[576,128]{1,0:T(8,128)(2,1)S(1)}, u32[]{:S(2)}, u32[]{:S(2)}) collective-permute-start(bf16[576,128]{1,0:T(8,128)(2,1)S(1)} %collective-permute-done.2.refs_0_), channel_id=1, source_target_pairs={{0,16},{4,20},{8,24},{12,28},{16,0},{20,4},{24,8},{28,12},{1,17},{... | collective-permute-start | bytes 442376 | tf_op jit(solution)/shard_map/ppermute | solution.py:82
  37.6 42.3 %collective-permute-start.10 = (bf16[576,1024]{1,0:T(8,128)(2,1)S(1)}, bf16[576,1024]{1,0:T(8,128)(2,1)S(1)}, u32[]{:S(2)}, u32[]{:S(2)}) collective-permute-start(bf16[576,1024]{1,0:T(8,128)(2,1)S(1)} %shard_map.86.refs_3_), channel_id=1, source_target_pairs={{0,32},{32,0},{1,33},{33,1},{2,34},{34,2},{3,35},{35,3},{4,36},{36... | collective-permute-start | bytes 3538952 | tf_op jit(solution)/shard_map/ppermute | solution.py:74
  38.6 22.6 %all-to-all-start = ((bf16[32,2,1280]{2,1,0:T(2,128)(2,1)}), bf16[32,2,1280]{2,1,0:T(2,128)(2,1)S(1)}, u32[]{:S(2)}, u32[]{:S(2)}) async-start(bf16[32,2,1280]{2,1,0:T(2,128)(2,1)} %maximum_bitcast_fusion), calls=%async_computation | async-start | bytes 327680 | tf_op jit(solution)/shard_map/all_to_all | solution.py:327
  62.9 17.0 %collective-permute-start.1 = (bf16[256,1152]{1,0:T(8,128)(2,1)S(1)}, bf16[256,1152]{1,0:T(8,128)(2,1)}, u32[]{:S(2)}, u32[]{:S(2)}) collective-permute-start(bf16[256,1152]{1,0:T(8,128)(2,1)S(1)} %shard_map.85), channel_id=1, source_target_pairs={{0,1},{1,0},{2,33},{3,32},{32,3},{33,2},{34,35},{35,34},{4,5},{5,4... | collective-permute-start | bytes 1769480 | tf_op jit(solution)/shard_map/ppermute | solution.py:59
  65.8 14.2 %collective-permute-start = (bf16[256,1152]{1,0:T(8,128)(2,1)S(1)}, bf16[256,1152]{1,0:T(8,128)(2,1)}, u32[]{:S(2)}, u32[]{:S(2)}) collective-permute-start(bf16[256,1152]{1,0:T(8,128)(2,1)S(1)} %shard_map.85), channel_id=1, source_target_pairs={{0,0},{1,1},{2,32},{3,33},{32,2},{33,3},{34,34},{35,35},{4,4},{5,5... | collective-permute-start | bytes 1769480 | tf_op jit(solution)/shard_map/ppermute | solution.py:59
  79.9 1.0 copy-start.3
  81.0 1.3 copy-start.4
  92.7 3.2 %collective-permute-start.11 = (f32[8,512]{1,0:T(8,128)S(1)}, f32[8,512]{1,0:T(8,128)S(1)}, u32[]{:S(2)}, u32[]{:S(2)}) collective-permute-start(f32[8,512]{1,0:T(8,128)S(1)} %get-tuple-element.23.st), channel_id=1, source_target_pairs={{0,1},{1,0},{2,3},{3,2},{4,5},{5,4},{6,7},{7,6},{8,9},{9,8},{10,11... | collective-permute-start | bytes 49160 | tf_op jit(solution)/shard_map/ppermute | solution.py:78
  99.4 14.6 %collective-permute-start.12 = (bf16[256,1152]{1,0:T(8,128)(2,1)S(1)}, bf16[256,1152]{1,0:T(8,128)(2,1)S(1)}, u32[]{:S(2)}, u32[]{:S(2)}) collective-permute-start(bf16[256,1152]{1,0:T(8,128)(2,1)S(1)} %get-tuple-element.27), channel_id=1, source_target_pairs={{0,0},{1,1},{2,32},{3,33},{32,2},{33,3},{34,34},{35,35},{4,4},{5,5... | collective-permute-start | bytes 1769480 | tf_op jit(solution)/shard_map/ppermute | solution.py:59
  105.1 13.9 %collective-permute-start.13 = (bf16[256,1152]{1,0:T(8,128)(2,1)S(1)}, bf16[256,1152]{1,0:T(8,128)(2,1)S(1)}, u32[]{:S(2)}, u32[]{:S(2)}) collective-permute-start(bf16[256,1152]{1,0:T(8,128)(2,1)S(1)} %get-tuple-element.28), channel_id=1, source_target_pairs={{0,1},{1,0},{2,33},{3,32},{32,3},{33,2},{34,35},{35,34},{4,5},{5,4... | collective-permute-start | bytes 1769480 | tf_op jit(solution)/shard_map/ppermute | solution.py:59
  110.7 10.4 %copy-start = (bf16[1024,576]{1,0:T(8,128)(2,1)}, bf16[1024,576]{1,0:T(8,128)(2,1)S(1)}, u32[]{:S(2)}) copy-start(bf16[1024,576]{1,0:T(8,128)(2,1)S(1)} %get-tuple-element.31.qq) | copy-start | bytes 3538948
  110.7 22.6 %collective-permute-start.14 = (bf16[8,576,128]{2,1,0:T(8,128)(2,1)}, bf16[8,576,128]{2,1,0:T(8,128)(2,1)}, u32[]{:S(2)}, u32[]{:S(2)}) collective-permute-start(bf16[8,576,128]{2,1,0:T(8,128)(2,1)} %get-tuple-element.32), channel_id=1, source_target_pairs={{0,32},{32,0},{1,33},{33,1},{2,34},{34,2},{3,35},{35,3},{4,36},{36... | collective-permute-start | bytes 3538952 | tf_op jit(solution)/shard_map/ppermute | solution.py:74
  121.1 2.0 %copy-start.2 = (bf16[256,1024]{1,0:T(8,128)(2,1)}, bf16[256,1024]{1,0:T(8,128)(2,1)S(1)}, u32[]{:S(2)}) copy-start(bf16[256,1024]{1,0:T(8,128)(2,1)S(1)} %get-tuple-element.41) | copy-start | bytes 1572868
  121.1 10.5 %copy-start.1 = (bf16[1024,576]{1,0:T(8,128)(2,1)S(1)}, bf16[1024,576]{1,0:T(8,128)(2,1)}, u32[]{:S(2)}) copy-start(bf16[1024,576]{1,0:T(8,128)(2,1)} %copy-done) | copy-start | bytes 3538948
  121.1 2.0 %collective-permute-start.23 = (bf16[256,1024]{1,0:T(8,128)(2,1)S(1)}, bf16[256,1024]{1,0:T(8,128)(2,1)S(1)}, u32[]{:S(2)}, u32[]{:S(2)}) collective-permute-start(bf16[256,1024]{1,0:T(8,128)(2,1)S(1)} %get-tuple-element.42), channel_id=1, source_target_pairs={{0,32},{32,0},{1,33},{33,1},{2,34},{34,2},{3,35},{35,3},{4,36},{36... | collective-permute-start | bytes 1572872 | tf_op jit(solution)/shard_map/ppermute | solution.py:74
  123.1 0.9 copy-start.5
  124.0 26.4 %collective-permute-start.24 = (bf16[64,1024]{1,0:T(8,128)(2,1)}, bf16[64,1024]{1,0:T(8,128)(2,1)}, u32[]{:S(2)}, u32[]{:S(2)}) collective-permute-start(bf16[64,1024]{1,0:T(8,128)(2,1)} %get-tuple-element.43), channel_id=1, source_target_pairs={{0,64},{64,128},{128,192},{192,0},{1,65},{65,129},{129,193},{193,1... | collective-permute-start | bytes 393224 | tf_op jit(solution)/shard_map/ppermute | solution.py:402
  125.9 26.1 %all-to-all-start.1 = ((bf16[32,2,768]{2,1,0:T(2,128)(2,1)}), bf16[32,2,768]{2,1,0:T(2,128)(2,1)S(1)}, u32[]{:S(2)}, u32[]{:S(2)}) async-start(bf16[32,2,768]{2,1,0:T(2,128)(2,1)} %reshape.36), calls=%async_computation.1 | async-start | bytes 196608 | tf_op jit(solution)/shard_map/all_to_all | solution.py:404
  133.3 15.7 %copy-start.7 = (bf16[64,1024]{1,0:T(8,128)(2,1)S(1)}, bf16[64,1024]{1,0:T(8,128)(2,1)}, u32[]{:S(2)}) copy-start(bf16[64,1024]{1,0:T(8,128)(2,1)} %get-tuple-element.44) | copy-start | bytes 393220
  133.3 17.2 %copy-start.6 = (bf16[64,1024]{1,0:T(8,128)(2,1)S(1)}, bf16[64,1024]{1,0:T(8,128)(2,1)}, u32[]{:S(2)}) copy-start(bf16[64,1024]{1,0:T(8,128)(2,1)} %get-tuple-element.45) | copy-start | bytes 393220
  134.9 23.4 %collective-permute-start.15 = (bf16[576,128]{1,0:T(8,128)(2,1)S(1)}, bf16[576,128]{1,0:T(8,128)(2,1)S(1)}, u32[]{:S(2)}, u32[]{:S(2)}) collective-permute-start(bf16[576,128]{1,0:T(8,128)(2,1)S(1)} %get-tuple-element.33), channel_id=1, source_target_pairs={{0,16},{1,17},{2,49},{3,48},{4,20},{5,21},{6,53},{7,52},{8,24},{9,... | collective-permute-start | bytes 442376 | tf_op jit(solution)/shard_map/ppermute | solution.py:70
  143.3 18.6 %collective-permute-start.16 = (bf16[576,128]{1,0:T(8,128)(2,1)S(1)}, bf16[576,128]{1,0:T(8,128)(2,1)S(1)}, u32[]{:S(2)}, u32[]{:S(2)}) collective-permute-start(bf16[576,128]{1,0:T(8,128)(2,1)S(1)} %get-tuple-element.34), channel_id=1, source_target_pairs={{0,20},{1,21},{2,53},{3,52},{4,24},{5,25},{6,57},{7,56},{8,28},{9,... | collective-permute-start | bytes 442376 | tf_op jit(solution)/shard_map/ppermute | solution.py:70
  143.3 22.3 %collective-permute-start.17 = (bf16[576,128]{1,0:T(8,128)(2,1)S(1)}, bf16[576,128]{1,0:T(8,128)(2,1)S(1)}, u32[]{:S(2)}, u32[]{:S(2)}) collective-permute-start(bf16[576,128]{1,0:T(8,128)(2,1)S(1)} %get-tuple-element.35), channel_id=1, source_target_pairs={{0,12},{1,13},{2,45},{3,44},{4,16},{5,17},{6,49},{7,48},{8,20},{9,... | collective-permute-start | bytes 442376 | tf_op jit(solution)/shard_map/ppermute | solution.py:70
  149.0 4.6 %collective-permute-start.26 = (bf16[64,1024]{1,0:T(8,128)(2,1)S(1)}, bf16[64,1024]{1,0:T(8,128)(2,1)S(1)}, u32[]{:S(2)}, u32[]{:S(2)}) collective-permute-start(bf16[64,1024]{1,0:T(8,128)(2,1)S(1)} %copy-done.7), channel_id=1, source_target_pairs={{0,192},{64,0},{128,64},{192,128},{1,193},{65,1},{129,65},{193,129... | collective-permute-start | bytes 393224 | tf_op jit(solution)/shard_map/ppermute | solution.py:402
  150.5 5.6 %collective-permute-start.25 = (bf16[64,1024]{1,0:T(8,128)(2,1)S(1)}, bf16[64,1024]{1,0:T(8,128)(2,1)S(1)}, u32[]{:S(2)}, u32[]{:S(2)}) collective-permute-start(bf16[64,1024]{1,0:T(8,128)(2,1)S(1)} %copy-done.6), channel_id=1, source_target_pairs={{0,128},{64,192},{128,0},{192,64},{1,129},{65,193},{129,1},{193,65... | collective-permute-start | bytes 393224 | tf_op jit(solution)/shard_map/ppermute | solution.py:402
  153.6 14.1 %collective-permute-start.18 = (bf16[576,128]{1,0:T(8,128)(2,1)S(1)}, bf16[576,128]{1,0:T(8,128)(2,1)S(1)}, u32[]{:S(2)}, u32[]{:S(2)}) collective-permute-start(bf16[576,128]{1,0:T(8,128)(2,1)S(1)} %get-tuple-element.36), channel_id=1, source_target_pairs={{0,24},{1,25},{2,57},{3,56},{4,28},{5,29},{6,61},{7,60},{8,0},{9,1... | collective-permute-start | bytes 442376 | tf_op jit(solution)/shard_map/ppermute | solution.py:70
  156.1 11.6 %collective-permute-start.19 = (bf16[576,128]{1,0:T(8,128)(2,1)S(1)}, bf16[576,128]{1,0:T(8,128)(2,1)S(1)}, u32[]{:S(2)}, u32[]{:S(2)}) collective-permute-start(bf16[576,128]{1,0:T(8,128)(2,1)S(1)} %get-tuple-element.37), channel_id=1, source_target_pairs={{0,8},{1,9},{2,41},{3,40},{4,12},{5,13},{6,45},{7,44},{8,16},{9,17... | collective-permute-start | bytes 442376 | tf_op jit(solution)/shard_map/ppermute | solution.py:70
  158.3 11.1 %collective-permute-start.20 = (bf16[576,128]{1,0:T(8,128)(2,1)S(1)}, bf16[576,128]{1,0:T(8,128)(2,1)S(1)}, u32[]{:S(2)}, u32[]{:S(2)}) collective-permute-start(bf16[576,128]{1,0:T(8,128)(2,1)S(1)} %get-tuple-element.38), channel_id=1, source_target_pairs={{0,0},{1,1},{2,33},{3,32},{4,4},{5,5},{6,37},{7,36},{8,8},{9,9},{1... | collective-permute-start | bytes 442376 | tf_op jit(solution)/shard_map/ppermute | solution.py:70
  161.9 7.5 %collective-permute-start.21 = (bf16[576,128]{1,0:T(8,128)(2,1)S(1)}, bf16[576,128]{1,0:T(8,128)(2,1)S(1)}, u32[]{:S(2)}, u32[]{:S(2)}) collective-permute-start(bf16[576,128]{1,0:T(8,128)(2,1)S(1)} %get-tuple-element.39), channel_id=1, source_target_pairs={{0,28},{1,29},{2,61},{3,60},{4,0},{5,1},{6,33},{7,32},{8,4},{9,5},... | collective-permute-start | bytes 442376 | tf_op jit(solution)/shard_map/ppermute | solution.py:70
  165.7 7.9 %collective-permute-start.22 = (bf16[576,128]{1,0:T(8,128)(2,1)S(1)}, bf16[576,128]{1,0:T(8,128)(2,1)S(1)}, u32[]{:S(2)}, u32[]{:S(2)}) collective-permute-start(bf16[576,128]{1,0:T(8,128)(2,1)S(1)} %get-tuple-element.40), channel_id=1, source_target_pairs={{0,4},{1,5},{2,37},{3,36},{4,8},{5,9},{6,41},{7,40},{8,12},{9,13},... | collective-permute-start | bytes 442376 | tf_op jit(solution)/shard_map/ppermute | solution.py:70

commit v4 on v3

--- a/solution.py
+++ b/solution.py
@@ -40,19 +40,6 @@
             v, w = y >> 1, y & 1
             pairs.append((c * NY + y, v * NY + 2 * c + (w ^ flip)))
     return pairs
-
-
-def swap_pairs():
-    pairs = []
-    for c in range(2):
-        for y in range(NY):
-            home = (y >> 1) == c
-            pairs.append((c * NY + y, c * NY + y if home else (1 - c) * NY + 3 - y))
-    return pairs
-
-
-def swap(v):
-    return lax.ppermute(v, ("core", "y"), swap_pairs())
 
 
 def turn(v, flip):
@@ -219,13 +206,6 @@
         outs[k][...] = (a[k].astype(F32) + b[k].astype(F32)).astype(BF)
 
 
-def total_body(*refs):
-    acc = refs[0][...].astype(F32)
-    for k in range(1, NZ):
-        acc = acc + refs[k][...].astype(F32)
-    refs[NZ][...] = acc.astype(BF)
-
-
 def row_factors(st, their, ws):
     there = jnp.concatenate([their[:, ROWS:], their[:, :ROWS]], axis=1)
     m, l, rd = st[0:1, :], st[1:2, :], st[2:3, :]
@@ -311,11 +291,15 @@
         send[slot, :] = terms[pl.ds(pl.multiple_of(base + (1 - c) * n, n), n), :]
 
 
+def plus(a, b):
+    return (a.astype(F32) + b.astype(F32)).astype(BF)
+
+
 def step(queries, grad_out, latent, latent_up, query_start, key_lengths):
     ndev = NZ * NY
     own_q = queries.shape[1]
 
-    own = swap(latent[0].T)
+    own = latent[0].T
     both = jnp.concatenate(
         [
             queries.reshape(own_q, ndev, HEADS * (DN + DR)),
@@ -327,7 +311,13 @@
     both = lax.all_to_all(both, CTX, 0, 0, tiled=True)
     both = both.reshape(NQ, HEADS * (DN + DR + DV))
 
-    kept = [own] + [along_z(own, -d) for d in OFFSETS[1:]]
+    near = {0: homeward(own, 0)}
+    near[-1], near[1] = homeward(own, 1), homeward(own, -1)
+    for j in (2, 3):
+        near[-j] = along_z(near[1 - j], 1)
+        near[j] = along_z(near[j - 1], -1)
+    near[4] = along_z(near[-3], 1)
+    kept = [near[d] for d in OFFSETS]
 
     (qg,) = call(
         latents_body,
@@ -376,18 +366,28 @@
     their_keys = other_core(their_keys)
     (mine_keys,) = call(parts_body, [piece], (qq, e_mine), 1_200_000_000)
     sums = call(add_body, [vmem((W, BLK), BF)] * NZ, (mine_keys, their_keys), 1_000_000, mib=8)
-    moved = []
-    for n in (1, 2, 3, 4, 5, 0, 6, 7):
-        moved.append(homeward(sums[n], OFFSETS[n]))
-    (total,) = call(total_body, [vmem((W, BLK), BF)], moved, 1_000_000, mib=4)
-    key_grad = total.astype(F32).T
+    part = dict(zip(OFFSETS, sums))
+    f = along_z(part[4], 1)
+    b = along_z(part[-3], -1)
+    stay = homeward(part[0], 0)
+    f = plus(part[3], f)
+    b = plus(part[-2], b)
+    f = along_z(f, 1)
+    b = along_z(b, -1)
+    f = plus(part[2], f)
+    b = plus(part[-1], b)
+    f = along_z(f, 1)
+    b = homeward(b, -1)
+    f = plus(part[1], f)
+    f = homeward(f, 1)
+    key_grad = (stay.astype(F32) + b.astype(F32) + f.astype(F32)).T
 
     qo = (mine.astype(F32) + other.astype(F32)).astype(BF)
     wide = HEADS * (DN + DV)
     gq, keep, send = call(
         tail_body,
         [vmem((NQ, HEADS * (DN + DR)), BF)] + [vmem((C // 2, wide), BF)] * 2,
-        (scal, qo, both, in_hbm(latent_up)),
+        (scal, qo, both, latent_up),
         200_000_000,
         (pltpu.VMEM((C, wide), BF),),
         smem=1,

time: 176 us -> 180 us (1.023)
  waiting for transfers between devices: 55.8 us -> 75.3 us
  starting transfers between devices: 81.9 us -> 63.7 us
  local copies, waits for them, and re-layouts: 3.11 us -> 6.47 us
    ppermute x7 -> x10, waiting for transfers between devices: 10.5 us -> 25.7 us  [along_z(): return lax.ppermute(v, 'z', [(i, (i + step) % NZ) for i in range(NZ)])]
    ppermute x7 -> x10, starting transfers between devices: 17 us -> 10.3 us  [along_z(): return lax.ppermute(v, 'z', [(i, (i + step) % NZ) for i in range(NZ)])]
    all_to_all x1, waiting for transfers between devices: 0.01 us -> 6.17 us  [step(): lax.all_to_all(gq.reshape(ndev, own_q, HEADS * (DN + DR)), CTX, 0, 0, til...]
    ppermute x1 -> x0, starting transfers between devices: 6.15 us -> none  [swap(): return lax.ppermute(v, ('core', 'y'), swap_pairs())]
    ppermute x8 -> x6, waiting for transfers between devices: 5.89 us -> 11.3 us  [homeward(): return lax.ppermute(v, ('core', 'z', 'y'), pairs)]
    all_to_all x1, starting transfers between devices: 12.4 us -> 8.77 us  [step(): both = lax.all_to_all(both, CTX, 0, 0, tiled=True)]
    unnamed x20 -> x22, local copies, waits for them, and re-layouts: 2.35 us -> 5.72 us
    ppermute x1 -> x0, waiting for transfers between devices: 3.02 us -> none  [swap(): return lax.ppermute(v, ('core', 'y'), swap_pairs())]
  transfers between devices with their start and end apart: 29 -> 29, of which waited for: 15 -> 17; matrix products, arithmetic and copies ran while one was open for 3% -> 3% of each run, Pallas kernels for 7% -> 7%
where the time goes in v4:
time: 180 us
  waiting for transfers between devices  75.3 us (42%)
  starting transfers between devices  63.7 us (35%)
  Pallas kernels  26.2 us (15%)
  local copies, waits for them, and re-layouts  6.47 us (4%)
  other arithmetic  5.6 us (3%)
  between operations  2.17 us (1%)
    pallas_call x8, Pallas kernels, call(): pl.pallas_call(body, out_shape=out_shape, in_specs=specs, out_specs=[pl.B...  26.2 us
    ppermute x10, waiting for transfers between devices, along_z(): return lax.ppermute(v, 'z', [(i, (i + step) % NZ) for i in range(NZ)])  25.7 us
    ppermute x6, starting transfers between devices, homeward(): return lax.ppermute(v, ('core', 'z', 'y'), pairs)  22.1 us
    ppermute x4, waiting for transfers between devices, turn(): return lax.ppermute(v, ('core', 'y'), turned(flip))  20.5 us
    ppermute x4, starting transfers between devices, turn(): return lax.ppermute(v, ('core', 'y'), turned(flip))  11.3 us
    ppermute x6, waiting for transfers between devices, homeward(): return lax.ppermute(v, ('core', 'z', 'y'), pairs)  11.3 us
    ppermute x10, starting transfers between devices, along_z(): return lax.ppermute(v, 'z', [(i, (i + step) % NZ) for i in range(NZ)])  10.3 us
    all_to_all x1, waiting for transfers between devices, step(): both = lax.all_to_all(both, CTX, 0, 0, tiled=True)  8.94 us
  transfers between devices with their start and end apart: 29, of which 17 were waited for; matrix products, arithmetic and copies ran while one was open for 3% of the time, Pallas kernels for 7%

profile of v4, /device:TPU:1, one launch (start us, length us, event | category | flops | bytes accessed | tf_op | source)
XLA Modules:
  0.0 179.5 jit_solution(1190245553919286005)
XLA Ops:
  0.7 5.5 %collective-permute-start.3 = (bf16[576,128]{1,0:T(8,128)(2,1)}, bf16[576,128]{1,0:T(8,128)(2,1)S(1)}, u32[]{:S(2)}, u32[]{:S(2)}) collective-permute-start(bf16[576,128]{1,0:T(8,128)(2,1)} %bitcast.21), channel_id=1, source_target_pairs={{0,4},{1,5},{2,37},{3,36},{4,8},{5,9},{6,41},{7,40},{8,12},{9,13},... | collective-permute-start | bytes 442376 | tf_op jit(solution)/shard_map/ppermute | solution.py:57
  6.2 4.0 %collective-permute-start.7 = (bf16[576,128]{1,0:T(8,128)(2,1)}, bf16[576,128]{1,0:T(8,128)(2,1)S(1)}, u32[]{:S(2)}, u32[]{:S(2)}) collective-permute-start(bf16[576,128]{1,0:T(8,128)(2,1)} %bitcast.22), channel_id=1, source_target_pairs={{0,28},{1,29},{2,61},{3,60},{4,0},{5,1},{6,33},{7,32},{8,4},{9,5},... | collective-permute-start | bytes 442376 | tf_op jit(solution)/shard_map/ppermute | solution.py:57
  10.2 4.4 %collective-permute-done.3.refs_6_ = bf16[576,128]{1,0:T(8,128)(2,1)S(1)} collective-permute-done((bf16[576,128]{1,0:T(8,128)(2,1)}, bf16[576,128]{1,0:T(8,128)(2,1)S(1)}, u32[]{:S(2)}, u32[]{:S(2)}) %collective-permute-start.3) | collective-permute-done | bytes 147488 | tf_op jit(solution)/shard_map/ppermute | solution.py:57
  14.7 2.7 %collective-permute-start.8 = (bf16[576,128]{1,0:T(8,128)(2,1)S(1)}, bf16[576,128]{1,0:T(8,128)(2,1)S(1)}, u32[]{:S(2)}, u32[]{:S(2)}) collective-permute-start(bf16[576,128]{1,0:T(8,128)(2,1)S(1)} %collective-permute-done.7.refs_7_), channel_id=1, source_target_pairs={{0,28},{4,0},{8,4},{12,8},{16,12},{20,16},{24,20},{28,24},{1,29},{... | collective-permute-start | bytes 442376 | tf_op jit(solution)/shard_map/ppermute | solution.py:69
  17.3 2.5 %collective-permute-done.4.refs_4_ = bf16[576,128]{1,0:T(8,128)(2,1)S(1)} collective-permute-done((bf16[576,128]{1,0:T(8,128)(2,1)S(1)}, bf16[576,128]{1,0:T(8,128)(2,1)S(1)}, u32[]{:S(2)}, u32[]{:S(2)}) %collective-permute-start.4) | collective-permute-done | bytes 147488 | tf_op jit(solution)/shard_map/ppermute | solution.py:69
  19.9 3.0 %collective-permute-start.2 = (bf16[576,128]{1,0:T(8,128)(2,1)}, bf16[576,128]{1,0:T(8,128)(2,1)S(1)}, u32[]{:S(2)}, u32[]{:S(2)}) collective-permute-start(bf16[576,128]{1,0:T(8,128)(2,1)} %bitcast.23), channel_id=1, source_target_pairs={{0,0},{1,1},{2,33},{3,32},{4,4},{5,5},{6,37},{7,36},{8,8},{9,9},{1... | collective-permute-start | bytes 442376 | tf_op jit(solution)/shard_map/ppermute | solution.py:57
  22.9 3.0 %collective-permute-start.9 = (bf16[576,128]{1,0:T(8,128)(2,1)S(1)}, bf16[576,128]{1,0:T(8,128)(2,1)S(1)}, u32[]{:S(2)}, u32[]{:S(2)}) collective-permute-start(bf16[576,128]{1,0:T(8,128)(2,1)S(1)} %collective-permute-done.8.refs_5_), channel_id=1, source_target_pairs={{0,28},{4,0},{8,4},{12,8},{16,12},{20,16},{24,20},{28,24},{1,29},{... | collective-permute-start | bytes 442376 | tf_op jit(solution)/shard_map/ppermute | solution.py:69
  25.9 1.8 %collective-permute-done.2.refs_0_ = bf16[576,128]{1,0:T(8,128)(2,1)S(1)} collective-permute-done((bf16[576,128]{1,0:T(8,128)(2,1)}, bf16[576,128]{1,0:T(8,128)(2,1)S(1)}, u32[]{:S(2)}, u32[]{:S(2)}) %collective-permute-start.2) | collective-permute-done | bytes 147488 | tf_op jit(solution)/shard_map/ppermute | solution.py:57
  28.0 4.7 %collective-permute-done.6.refs_1_ = bf16[576,128]{1,0:T(8,128)(2,1)S(1)} collective-permute-done((bf16[576,128]{1,0:T(8,128)(2,1)S(1)}, bf16[576,128]{1,0:T(8,128)(2,1)S(1)}, u32[]{:S(2)}, u32[]{:S(2)}) %collective-permute-start.6) | collective-permute-done | bytes 147488 | tf_op jit(solution)/shard_map/ppermute | solution.py:69
  34.7 8.8 %all-to-all-start = ((bf16[32,2,1280]{2,1,0:T(2,128)(2,1)}), bf16[32,2,1280]{2,1,0:T(2,128)(2,1)S(1)}, u32[]{:S(2)}, u32[]{:S(2)}) async-start(bf16[32,2,1280]{2,1,0:T(2,128)(2,1)} %maximum_bitcast_fusion), calls=%async_computation | async-start | bytes 327680 | tf_op jit(solution)/shard_map/all_to_all | solution.py:311
  44.7 8.9 %all-to-all-done = bf16[32,2,1280]{2,1,0:T(2,128)(2,1)S(1)} async-done(((bf16[32,2,1280]{2,1,0:T(2,128)(2,1)}), bf16[32,2,1280]{2,1,0:T(2,128)(2,1)S(1)}, u32[]{:S(2)}, u32[]{:S(2)}) %all-to-all-start) | async-done | bytes 163872 | tf_op jit(solution)/shard_map/all_to_all | solution.py:311
  53.7 1.7 shard_map.85
  55.5 2.8 %collective-permute-start.1 = (bf16[256,1152]{1,0:T(8,128)(2,1)S(1)}, bf16[256,1152]{1,0:T(8,128)(2,1)}, u32[]{:S(2)}, u32[]{:S(2)}) collective-permute-start(bf16[256,1152]{1,0:T(8,128)(2,1)S(1)} %shard_map.85), channel_id=1, source_target_pairs={{0,1},{1,0},{2,33},{3,32},{32,3},{33,2},{34,35},{35,34},{4,5},{5,4... | collective-permute-start | bytes 1769480 | tf_op jit(solution)/shard_map/ppermute | solution.py:46
  58.3 1.9 %collective-permute-start = (bf16[256,1152]{1,0:T(8,128)(2,1)S(1)}, bf16[256,1152]{1,0:T(8,128)(2,1)}, u32[]{:S(2)}, u32[]{:S(2)}) collective-permute-start(bf16[256,1152]{1,0:T(8,128)(2,1)S(1)} %shard_map.85), channel_id=1, source_target_pairs={{0,0},{1,1},{2,32},{3,33},{32,2},{33,3},{34,34},{35,35},{4,4},{5,5... | collective-permute-start | bytes 1769480 | tf_op jit(solution)/shard_map/ppermute | solution.py:46
  60.3 12.2 %collective-permute-done.1.refs_2_.other = bf16[256,1152]{1,0:T(8,128)(2,1)} collective-permute-done((bf16[256,1152]{1,0:T(8,128)(2,1)S(1)}, bf16[256,1152]{1,0:T(8,128)(2,1)}, u32[]{:S(2)}, u32[]{:S(2)}) %collective-permute-start.1) | collective-permute-done | bytes 589856 | tf_op jit(solution)/shard_map/ppermute | solution.py:46
  72.5 1.0 copy-done.7
  73.5 1.3 copy-done.4
  74.8 1.3 copy-done.8
  76.1 10.5 %shard_map.87 = (bf16[1024,1024]{1,0:T(8,128)(2,1)S(1)}, bf16[1024,1024]{1,0:T(8,128)(2,1)S(1)}, bf16[576,2048]{1,0:T(8,128)(2,1)S(1)}, f32[8,512]{1,0:T(8,128)S(1)}) custom-call(s32[4]{0:T(128)S(1)} %pad_add_fusion.refs_0_.scal, bf16[256,1152]{1,0:T(8,128)(2,1)} %collective-permute-done.refs_1_.mine, ...), custom_call_target="tpu_custom_call" | custom-call | flops 2280000000 | bytes 10108944 | tf_op jit(solution)/shard_map/pallas_call | solution.py:89
  86.8 2.8 %collective-permute-done.11.their = f32[8,512]{1,0:T(8,128)S(1)} collective-permute-done((f32[8,512]{1,0:T(8,128)S(1)}, f32[8,512]{1,0:T(8,128)S(1)}, u32[]{:S(2)}, u32[]{:S(2)}) %collective-permute-start.11) | collective-permute-done | bytes 16416 | tf_op jit(solution)/shard_map/ppermute | solution.py:65
  89.6 3.6 %shard_map.88 = (bf16[256,1152]{1,0:T(8,128)(2,1)S(1)}, bf16[256,1152]{1,0:T(8,128)(2,1)S(1)}, f32[512,128]{1,0:T(8,128)S(1)}) custom-call(f32[8,512]{1,0:T(8,128)S(1)} %get-tuple-element.23.st, f32[8,512]{1,0:T(8,128)S(1)} %collective-permute-done.11.their, bf16[576,2048]{1,0:T(8,128)(2,1)S(1)} %get-tuple-element.24.kt, ...), custom_call_target="tpu_custom_call" | custom-call | flops 2400000000 | bytes 8028160 | tf_op jit(solution)/shard_map/pallas_call | solution.py:89
  93.2 5.9 %collective-permute-start.12 = (bf16[256,1152]{1,0:T(8,128)(2,1)S(1)}, bf16[256,1152]{1,0:T(8,128)(2,1)S(1)}, u32[]{:S(2)}, u32[]{:S(2)}) collective-permute-start(bf16[256,1152]{1,0:T(8,128)(2,1)S(1)} %get-tuple-element.27), channel_id=1, source_target_pairs={{0,0},{1,1},{2,32},{3,33},{32,2},{33,3},{34,34},{35,35},{4,4},{5,5... | collective-permute-start | bytes 1769480 | tf_op jit(solution)/shard_map/ppermute | solution.py:46
  99.7 4.9 %shard_map.90 = (bf16[1024,576]{1,0:T(8,128)(2,1)S(1)}, bf16[8,576,128]{2,1,0:T(8,128)(2,1)}) custom-call(f32[512,128]{1,0:T(8,128)S(1)} %get-tuple-element.30.ws, bf16[256,1152]{1,0:T(8,128)(2,1)} %collective-permute-done.refs_1_.mine, bf16[256,1152]{1,0:T(8,128)(2,1)} %collective-permute-done.1.refs_2_.other, bf16[1024,1024]{1,0:T(8,128)(2,1)S(1)} %get-tuple-element.26.e1.ee), custom_call_target="tpu_custom_call" | custom-call | flops 1300000000 | bytes 5898240 | tf_op jit(solution)/shard_map/pallas_call | solution.py:89
  104.6 3.1 %collective-permute-done.12 = bf16[256,1152]{1,0:T(8,128)(2,1)S(1)} collective-permute-done((bf16[256,1152]{1,0:T(8,128)(2,1)S(1)}, bf16[256,1152]{1,0:T(8,128)(2,1)S(1)}, u32[]{:S(2)}, u32[]{:S(2)}) %collective-permute-start.12) | collective-permute-done | bytes 589856 | tf_op jit(solution)/shard_map/ppermute | solution.py:46
  107.7 5.2 %collective-permute-done.13 = bf16[256,1152]{1,0:T(8,128)(2,1)S(1)} collective-permute-done((bf16[256,1152]{1,0:T(8,128)(2,1)S(1)}, bf16[256,1152]{1,0:T(8,128)(2,1)S(1)}, u32[]{:S(2)}, u32[]{:S(2)}) %collective-permute-start.13) | collective-permute-done | bytes 589856 | tf_op jit(solution)/shard_map/ppermute | solution.py:46
  113.1 2.0 %shard_map.89 = (bf16[64,768]{1,0:T(8,128)(2,1)S(1)}, bf16[256,1024]{1,0:T(8,128)(2,1)S(1)}, bf16[256,1024]{1,0:T(8,128)(2,1)}) custom-call(s32[4]{0:T(128)S(1)} %pad_add_fusion.refs_0_.scal, bf16[256,1152]{1,0:T(8,128)(2,1)S(1)} %add_convert_fusion.qo, bf16[64,1280]{1,0:T(8,128)(2,1)S(1)} %reshape.35.both, bf16[512,1024]{1,0:T(8,128)(2,1)S(1)} %copy-done), custom_call_target="tpu_custom_call" | custom-call | flops 200000000 | bytes 2949136 | tf_op jit(solution)/shard_map/pallas_call | solution.py:89
  115.0 0.8 copy-done.5
  116.6 6.0 %all-to-all-start.1 = ((bf16[32,2,768]{2,1,0:T(2,128)(2,1)}), bf16[32,2,768]{2,1,0:T(2,128)(2,1)S(1)}, u32[]{:S(2)}, u32[]{:S(2)}) async-start(bf16[32,2,768]{2,1,0:T(2,128)(2,1)} %reshape.36), calls=%async_computation.1 | async-start | bytes 196608 | tf_op jit(solution)/shard_map/all_to_all | solution.py:404
  122.6 1.3 copy-done.2
  123.9 1.7 shard_map.91.a
  125.6 6.2 %all-to-all-done.1 = bf16[32,2,768]{2,1,0:T(2,128)(2,1)S(1)} async-done(((bf16[32,2,768]{2,1,0:T(2,128)(2,1)}), bf16[32,2,768]{2,1,0:T(2,128)(2,1)S(1)}, u32[]{:S(2)}, u32[]{:S(2)}) %all-to-all-start.1) | async-done | bytes 98336 | tf_op jit(solution)/shard_map/all_to_all | solution.py:404
  132.5 1.6 shard_map.92
  134.7 1.2 add_convert_fusion.8
  135.8 1.3 collective-permute-start.24
  137.1 1.5 collective-permute-start.26
  138.6 1.5 collective-permute-start.25
  140.1 5.5 %collective-permute-start.15 = (bf16[576,128]{1,0:T(8,128)(2,1)S(1)}, bf16[576,128]{1,0:T(8,128)(2,1)S(1)}, u32[]{:S(2)}, u32[]{:S(2)}) collective-permute-start(bf16[576,128]{1,0:T(8,128)(2,1)S(1)} %get-tuple-element.33), channel_id=1, source_target_pairs={{0,0},{1,1},{2,33},{3,32},{4,4},{5,5},{6,37},{7,36},{8,8},{9,9},{1... | collective-permute-start | bytes 442376 | tf_op jit(solution)/shard_map/ppermute | solution.py:57
  145.7 2.3 %collective-permute-start.16 = (bf16[576,128]{1,0:T(8,128)(2,1)S(1)}, bf16[576,128]{1,0:T(8,128)(2,1)S(1)}, u32[]{:S(2)}, u32[]{:S(2)}) collective-permute-start(bf16[576,128]{1,0:T(8,128)(2,1)S(1)} %get-tuple-element.36), channel_id=1, source_target_pairs={{0,28},{4,0},{8,4},{12,8},{16,12},{20,16},{24,20},{28,24},{1,29},{... | collective-permute-start | bytes 442376 | tf_op jit(solution)/shard_map/ppermute | solution.py:69
  148.1 2.1 %collective-permute-done.16 = bf16[576,128]{1,0:T(8,128)(2,1)S(1)} collective-permute-done((bf16[576,128]{1,0:T(8,128)(2,1)S(1)}, bf16[576,128]{1,0:T(8,128)(2,1)S(1)}, u32[]{:S(2)}, u32[]{:S(2)}) %collective-permute-start.16) | collective-permute-done | bytes 147488 | tf_op jit(solution)/shard_map/ppermute | solution.py:69
  150.2 6.2 %collective-permute-done.20 = bf16[576,128]{1,0:T(8,128)(2,1)S(1)} collective-permute-done((bf16[576,128]{1,0:T(8,128)(2,1)S(1)}, bf16[576,128]{1,0:T(8,128)(2,1)S(1)}, u32[]{:S(2)}, u32[]{:S(2)}) %collective-permute-start.20) | collective-permute-done | bytes 147488 | tf_op jit(solution)/shard_map/ppermute | solution.py:69
  156.4 1.7 collective-permute-start.17
  158.2 3.9 %collective-permute-done.17 = bf16[576,128]{1,0:T(8,128)(2,1)S(1)} collective-permute-done((bf16[576,128]{1,0:T(8,128)(2,1)S(1)}, bf16[576,128]{1,0:T(8,128)(2,1)S(1)}, u32[]{:S(2)}, u32[]{:S(2)}) %collective-permute-start.17) | collective-permute-done | bytes 147488 | tf_op jit(solution)/shard_map/ppermute | solution.py:69
  162.1 5.9 %collective-permute-done.21 = bf16[576,128]{1,0:T(8,128)(2,1)S(1)} collective-permute-done((bf16[576,128]{1,0:T(8,128)(2,1)S(1)}, bf16[576,128]{1,0:T(8,128)(2,1)S(1)}, u32[]{:S(2)}, u32[]{:S(2)}) %collective-permute-start.21) | collective-permute-done | bytes 147488 | tf_op jit(solution)/shard_map/ppermute | solution.py:69
  168.1 2.7 %collective-permute-start.18 = (bf16[576,128]{1,0:T(8,128)(2,1)S(1)}, bf16[576,128]{1,0:T(8,128)(2,1)S(1)}, u32[]{:S(2)}, u32[]{:S(2)}) collective-permute-start(bf16[576,128]{1,0:T(8,128)(2,1)S(1)} %add_convert_fusion.4), channel_id=1, source_target_pairs={{0,28},{1,29},{2,61},{3,60},{4,0},{5,1},{6,33},{7,32},{8,4},{9,5},... | collective-permute-start | bytes 442376 | tf_op jit(solution)/shard_map/ppermute | solution.py:57
  170.8 1.2 collective-permute-start.22
  172.0 1.7 convert_add_fusion
  173.7 1.0 collective-permute-done.18
  174.7 4.0 %collective-permute-done.22 = bf16[576,128]{1,0:T(8,128)(2,1)S(1)} collective-permute-done((bf16[576,128]{1,0:T(8,128)(2,1)S(1)}, bf16[576,128]{1,0:T(8,128)(2,1)S(1)}, u32[]{:S(2)}, u32[]{:S(2)}) %collective-permute-start.22) | collective-permute-done | bytes 147488 | tf_op jit(solution)/shard_map/ppermute | solution.py:57
  (54 shorter events, 6.4 us)
Async XLA Ops:
  0.6 33.2 %copy-start.9 = (bf16[1,2,24576]{2,1,0:T(2,128)(2,1)S(1)}, bf16[1,2,24576]{2,1,0:T(2,128)(2,1)}, u32[]{:S(2)}) copy-start(bf16[1,2,24576]{2,1,0:T(2,128)(2,1)} %param.6) | copy-start | bytes 294916
  0.6 33.2 %copy-start.10 = (bf16[1,2,16384]{2,1,0:T(2,128)(2,1)S(1)}, bf16[1,2,16384]{2,1,0:T(2,128)(2,1)}, u32[]{:S(2)}) copy-start(bf16[1,2,16384]{2,1,0:T(2,128)(2,1)} %param.7) | copy-start | bytes 196612
  0.7 14.0 %collective-permute-start.3 = (bf16[576,128]{1,0:T(8,128)(2,1)}, bf16[576,128]{1,0:T(8,128)(2,1)S(1)}, u32[]{:S(2)}, u32[]{:S(2)}) collective-permute-start(bf16[576,128]{1,0:T(8,128)(2,1)} %bitcast.21), channel_id=1, source_target_pairs={{0,4},{1,5},{2,37},{3,36},{4,8},{5,9},{6,41},{7,40},{8,12},{9,13},... | collective-permute-start | bytes 442376 | tf_op jit(solution)/shard_map/ppermute | solution.py:57
  6.2 8.5 %collective-permute-start.7 = (bf16[576,128]{1,0:T(8,128)(2,1)}, bf16[576,128]{1,0:T(8,128)(2,1)S(1)}, u32[]{:S(2)}, u32[]{:S(2)}) collective-permute-start(bf16[576,128]{1,0:T(8,128)(2,1)} %bitcast.22), channel_id=1, source_target_pairs={{0,28},{1,29},{2,61},{3,60},{4,0},{5,1},{6,33},{7,32},{8,4},{9,5},... | collective-permute-start | bytes 442376 | tf_op jit(solution)/shard_map/ppermute | solution.py:57
  14.7 5.2 %collective-permute-start.4 = (bf16[576,128]{1,0:T(8,128)(2,1)S(1)}, bf16[576,128]{1,0:T(8,128)(2,1)S(1)}, u32[]{:S(2)}, u32[]{:S(2)}) collective-permute-start(bf16[576,128]{1,0:T(8,128)(2,1)S(1)} %collective-permute-done.3.refs_6_), channel_id=1, source_target_pairs={{0,4},{4,8},{8,12},{12,16},{16,20},{20,24},{24,28},{28,0},{1,5},{5... | collective-permute-start | bytes 442376 | tf_op jit(solution)/shard_map/ppermute | solution.py:69
  14.7 8.2 %collective-permute-start.8 = (bf16[576,128]{1,0:T(8,128)(2,1)S(1)}, bf16[576,128]{1,0:T(8,128)(2,1)S(1)}, u32[]{:S(2)}, u32[]{:S(2)}) collective-permute-start(bf16[576,128]{1,0:T(8,128)(2,1)S(1)} %collective-permute-done.7.refs_7_), channel_id=1, source_target_pairs={{0,28},{4,0},{8,4},{12,8},{16,12},{20,16},{24,20},{28,24},{1,29},{... | collective-permute-start | bytes 442376 | tf_op jit(solution)/shard_map/ppermute | solution.py:69
  19.9 6.1 %collective-permute-start.5 = (bf16[576,128]{1,0:T(8,128)(2,1)S(1)}, bf16[576,128]{1,0:T(8,128)(2,1)S(1)}, u32[]{:S(2)}, u32[]{:S(2)}) collective-permute-start(bf16[576,128]{1,0:T(8,128)(2,1)S(1)} %collective-permute-done.4.refs_4_), channel_id=1, source_target_pairs={{0,4},{4,8},{8,12},{12,16},{16,20},{20,24},{24,28},{28,0},{1,5},{5... | collective-permute-start | bytes 442376 | tf_op jit(solution)/shard_map/ppermute | solution.py:69
  19.9 7.9 %collective-permute-start.2 = (bf16[576,128]{1,0:T(8,128)(2,1)}, bf16[576,128]{1,0:T(8,128)(2,1)S(1)}, u32[]{:S(2)}, u32[]{:S(2)}) collective-permute-start(bf16[576,128]{1,0:T(8,128)(2,1)} %bitcast.23), channel_id=1, source_target_pairs={{0,0},{1,1},{2,33},{3,32},{4,4},{5,5},{6,37},{7,36},{8,8},{9,9},{1... | collective-permute-start | bytes 442376 | tf_op jit(solution)/shard_map/ppermute | solution.py:57
  22.9 5.1 %collective-permute-start.9 = (bf16[576,128]{1,0:T(8,128)(2,1)S(1)}, bf16[576,128]{1,0:T(8,128)(2,1)S(1)}, u32[]{:S(2)}, u32[]{:S(2)}) collective-permute-start(bf16[576,128]{1,0:T(8,128)(2,1)S(1)} %collective-permute-done.8.refs_5_), channel_id=1, source_target_pairs={{0,28},{4,0},{8,4},{12,8},{16,12},{20,16},{24,20},{28,24},{1,29},{... | collective-permute-start | bytes 442376 | tf_op jit(solution)/shard_map/ppermute | solution.py:69
  25.9 6.8 %collective-permute-start.6 = (bf16[576,128]{1,0:T(8,128)(2,1)S(1)}, bf16[576,128]{1,0:T(8,128)(2,1)S(1)}, u32[]{:S(2)}, u32[]{:S(2)}) collective-permute-start(bf16[576,128]{1,0:T(8,128)(2,1)S(1)} %collective-permute-done.5.refs_2_), channel_id=1, source_target_pairs={{0,4},{4,8},{8,12},{12,16},{16,20},{20,24},{24,28},{28,0},{1,5},{5... | collective-permute-start | bytes 442376 | tf_op jit(solution)/shard_map/ppermute | solution.py:69
  33.1 22.3 %copy-start.3 = (bf16[576,1024]{1,0:T(8,128)(2,1)}, bf16[576,1024]{1,0:T(8,128)(2,1)S(1)}, u32[]{:S(2)}) copy-start(bf16[576,1024]{1,0:T(8,128)(2,1)S(1)} %shard_map.86.refs_3_) | copy-start | bytes 3538948
  33.1 39.4 %collective-permute-start.10 = (bf16[576,1024]{1,0:T(8,128)(2,1)S(1)}, bf16[576,1024]{1,0:T(8,128)(2,1)S(1)}, u32[]{:S(2)}, u32[]{:S(2)}) collective-permute-start(bf16[576,1024]{1,0:T(8,128)(2,1)S(1)} %shard_map.86.refs_3_), channel_id=1, source_target_pairs={{0,32},{32,0},{1,33},{33,1},{2,34},{34,2},{3,35},{35,3},{4,36},{36... | collective-permute-start | bytes 3538952 | tf_op jit(solution)/shard_map/ppermute | solution.py:61
  34.7 19.0 %all-to-all-start = ((bf16[32,2,1280]{2,1,0:T(2,128)(2,1)}), bf16[32,2,1280]{2,1,0:T(2,128)(2,1)S(1)}, u32[]{:S(2)}, u32[]{:S(2)}) async-start(bf16[32,2,1280]{2,1,0:T(2,128)(2,1)} %maximum_bitcast_fusion), calls=%async_computation | async-start | bytes 327680 | tf_op jit(solution)/shard_map/all_to_all | solution.py:311
  55.5 17.0 %collective-permute-start.1 = (bf16[256,1152]{1,0:T(8,128)(2,1)S(1)}, bf16[256,1152]{1,0:T(8,128)(2,1)}, u32[]{:S(2)}, u32[]{:S(2)}) collective-permute-start(bf16[256,1152]{1,0:T(8,128)(2,1)S(1)} %shard_map.85), channel_id=1, source_target_pairs={{0,1},{1,0},{2,33},{3,32},{32,3},{33,2},{34,35},{35,34},{4,5},{5,4... | collective-permute-start | bytes 1769480 | tf_op jit(solution)/shard_map/ppermute | solution.py:46
  58.3 14.2 %collective-permute-start = (bf16[256,1152]{1,0:T(8,128)(2,1)S(1)}, bf16[256,1152]{1,0:T(8,128)(2,1)}, u32[]{:S(2)}, u32[]{:S(2)}) collective-permute-start(bf16[256,1152]{1,0:T(8,128)(2,1)S(1)} %shard_map.85), channel_id=1, source_target_pairs={{0,0},{1,1},{2,32},{3,33},{32,2},{33,3},{34,34},{35,35},{4,4},{5,5... | collective-permute-start | bytes 1769480 | tf_op jit(solution)/shard_map/ppermute | solution.py:46
  72.5 1.0 copy-start.7
  73.5 1.3 copy-start.4
  74.8 1.3 copy-start.8
  86.6 3.0 %collective-permute-start.11 = (f32[8,512]{1,0:T(8,128)S(1)}, f32[8,512]{1,0:T(8,128)S(1)}, u32[]{:S(2)}, u32[]{:S(2)}) collective-permute-start(f32[8,512]{1,0:T(8,128)S(1)} %get-tuple-element.23.st), channel_id=1, source_target_pairs={{0,1},{1,0},{2,3},{3,2},{4,5},{5,4},{6,7},{7,6},{8,9},{9,8},{10,11... | collective-permute-start | bytes 49160 | tf_op jit(solution)/shard_map/ppermute | solution.py:65
  93.2 14.6 %collective-permute-start.12 = (bf16[256,1152]{1,0:T(8,128)(2,1)S(1)}, bf16[256,1152]{1,0:T(8,128)(2,1)S(1)}, u32[]{:S(2)}, u32[]{:S(2)}) collective-permute-start(bf16[256,1152]{1,0:T(8,128)(2,1)S(1)} %get-tuple-element.27), channel_id=1, source_target_pairs={{0,0},{1,1},{2,32},{3,33},{32,2},{33,3},{34,34},{35,35},{4,4},{5,5... | collective-permute-start | bytes 1769480 | tf_op jit(solution)/shard_map/ppermute | solution.py:46
  99.1 13.9 %collective-permute-start.13 = (bf16[256,1152]{1,0:T(8,128)(2,1)S(1)}, bf16[256,1152]{1,0:T(8,128)(2,1)S(1)}, u32[]{:S(2)}, u32[]{:S(2)}) collective-permute-start(bf16[256,1152]{1,0:T(8,128)(2,1)S(1)} %get-tuple-element.28), channel_id=1, source_target_pairs={{0,1},{1,0},{2,33},{3,32},{32,3},{33,2},{34,35},{35,34},{4,5},{5,4... | collective-permute-start | bytes 1769480 | tf_op jit(solution)/shard_map/ppermute | solution.py:46
  104.6 10.5 %copy-start.1 = (bf16[1024,576]{1,0:T(8,128)(2,1)}, bf16[1024,576]{1,0:T(8,128)(2,1)S(1)}, u32[]{:S(2)}) copy-start(bf16[1024,576]{1,0:T(8,128)(2,1)S(1)} %get-tuple-element.31.qq) | copy-start | bytes 3538948
  104.6 8.5 %copy-start = (bf16[512,1024]{1,0:T(8,128)(2,1)S(1)}, bf16[512,1024]{1,0:T(8,128)(2,1)}, u32[]{:S(2)}) copy-start(bf16[512,1024]{1,0:T(8,128)(2,1)} %w.3) | copy-start | bytes 3145732
  104.6 27.9 %collective-permute-start.14 = (bf16[8,576,128]{2,1,0:T(8,128)(2,1)}, bf16[8,576,128]{2,1,0:T(8,128)(2,1)}, u32[]{:S(2)}, u32[]{:S(2)}) collective-permute-start(bf16[8,576,128]{2,1,0:T(8,128)(2,1)} %get-tuple-element.32), channel_id=1, source_target_pairs={{0,32},{32,0},{1,33},{33,1},{2,34},{34,2},{3,35},{35,3},{4,36},{36... | collective-permute-start | bytes 3538952 | tf_op jit(solution)/shard_map/ppermute | solution.py:61
  115.0 0.8 copy-start.5
  115.9 18.8 %collective-permute-start.23 = (bf16[256,1024]{1,0:T(8,128)(2,1)}, bf16[256,1024]{1,0:T(8,128)(2,1)}, u32[]{:S(2)}, u32[]{:S(2)}) collective-permute-start(bf16[256,1024]{1,0:T(8,128)(2,1)} %get-tuple-element.42), channel_id=1, source_target_pairs={{0,32},{32,0},{1,33},{33,1},{2,34},{34,2},{3,35},{35,3},{4,36},{36... | collective-permute-start | bytes 1572872 | tf_op jit(solution)/shard_map/ppermute | solution.py:61
  116.6 15.2 %all-to-all-start.1 = ((bf16[32,2,768]{2,1,0:T(2,128)(2,1)}), bf16[32,2,768]{2,1,0:T(2,128)(2,1)S(1)}, u32[]{:S(2)}, u32[]{:S(2)}) async-start(bf16[32,2,768]{2,1,0:T(2,128)(2,1)} %reshape.36), calls=%async_computation.1 | async-start | bytes 196608 | tf_op jit(solution)/shard_map/all_to_all | solution.py:404
  122.5 1.3 copy-start.2
  132.5 2.2 %copy-start.6 = (bf16[256,1024]{1,0:T(8,128)(2,1)S(1)}, bf16[256,1024]{1,0:T(8,128)(2,1)}, u32[]{:S(2)}) copy-start(bf16[256,1024]{1,0:T(8,128)(2,1)} %copy-done.5) | copy-start | bytes 1572868
  134.1 11.6 %collective-permute-start.19 = (bf16[576,128]{1,0:T(8,128)(2,1)S(1)}, bf16[576,128]{1,0:T(8,128)(2,1)S(1)}, u32[]{:S(2)}, u32[]{:S(2)}) collective-permute-start(bf16[576,128]{1,0:T(8,128)(2,1)S(1)} %get-tuple-element.40), channel_id=1, source_target_pairs={{0,4},{4,8},{8,12},{12,16},{16,20},{20,24},{24,28},{28,0},{1,5},{5... | collective-permute-start | bytes 442376 | tf_op jit(solution)/shard_map/ppermute | solution.py:69
  135.8 35.0 %collective-permute-start.24 = (bf16[64,1024]{1,0:T(8,128)(2,1)S(1)}, bf16[64,1024]{1,0:T(8,128)(2,1)S(1)}, u32[]{:S(2)}, u32[]{:S(2)}) collective-permute-start(bf16[64,1024]{1,0:T(8,128)(2,1)S(1)} %get-tuple-element.43), channel_id=1, source_target_pairs={{0,64},{64,128},{128,192},{192,0},{1,65},{65,129},{129,193},{193,1... | collective-permute-start | bytes 393224 | tf_op jit(solution)/shard_map/ppermute | solution.py:402
  137.1 34.9 %collective-permute-start.26 = (bf16[64,1024]{1,0:T(8,128)(2,1)S(1)}, bf16[64,1024]{1,0:T(8,128)(2,1)S(1)}, u32[]{:S(2)}, u32[]{:S(2)}) collective-permute-start(bf16[64,1024]{1,0:T(8,128)(2,1)S(1)} %get-tuple-element.44), channel_id=1, source_target_pairs={{0,192},{64,0},{128,64},{192,128},{1,193},{65,1},{129,65},{193,129... | collective-permute-start | bytes 393224 | tf_op jit(solution)/shard_map/ppermute | solution.py:402
  138.6 33.5 %collective-permute-start.25 = (bf16[64,1024]{1,0:T(8,128)(2,1)S(1)}, bf16[64,1024]{1,0:T(8,128)(2,1)S(1)}, u32[]{:S(2)}, u32[]{:S(2)}) collective-permute-start(bf16[64,1024]{1,0:T(8,128)(2,1)S(1)} %get-tuple-element.45), channel_id=1, source_target_pairs={{0,128},{64,192},{128,0},{192,64},{1,129},{65,193},{129,1},{193,65... | collective-permute-start | bytes 393224 | tf_op jit(solution)/shard_map/ppermute | solution.py:402
  140.1 33.6 %collective-permute-start.15 = (bf16[576,128]{1,0:T(8,128)(2,1)S(1)}, bf16[576,128]{1,0:T(8,128)(2,1)S(1)}, u32[]{:S(2)}, u32[]{:S(2)}) collective-permute-start(bf16[576,128]{1,0:T(8,128)(2,1)S(1)} %get-tuple-element.33), channel_id=1, source_target_pairs={{0,0},{1,1},{2,33},{3,32},{4,4},{5,5},{6,37},{7,36},{8,8},{9,9},{1... | collective-permute-start | bytes 442376 | tf_op jit(solution)/shard_map/ppermute | solution.py:57
  145.7 4.4 %collective-permute-start.16 = (bf16[576,128]{1,0:T(8,128)(2,1)S(1)}, bf16[576,128]{1,0:T(8,128)(2,1)S(1)}, u32[]{:S(2)}, u32[]{:S(2)}) collective-permute-start(bf16[576,128]{1,0:T(8,128)(2,1)S(1)} %get-tuple-element.36), channel_id=1, source_target_pairs={{0,28},{4,0},{8,4},{12,8},{16,12},{20,16},{24,20},{28,24},{1,29},{... | collective-permute-start | bytes 442376 | tf_op jit(solution)/shard_map/ppermute | solution.py:69
  150.1 6.3 %collective-permute-start.20 = (bf16[576,128]{1,0:T(8,128)(2,1)S(1)}, bf16[576,128]{1,0:T(8,128)(2,1)S(1)}, u32[]{:S(2)}, u32[]{:S(2)}) collective-permute-start(bf16[576,128]{1,0:T(8,128)(2,1)S(1)} %add_convert_fusion.3), channel_id=1, source_target_pairs={{0,4},{4,8},{8,12},{12,16},{16,20},{20,24},{24,28},{28,0},{1,5},{5... | collective-permute-start | bytes 442376 | tf_op jit(solution)/shard_map/ppermute | solution.py:69
  156.4 5.6 %collective-permute-start.17 = (bf16[576,128]{1,0:T(8,128)(2,1)S(1)}, bf16[576,128]{1,0:T(8,128)(2,1)S(1)}, u32[]{:S(2)}, u32[]{:S(2)}) collective-permute-start(bf16[576,128]{1,0:T(8,128)(2,1)S(1)} %add_convert_fusion.5), channel_id=1, source_target_pairs={{0,28},{4,0},{8,4},{12,8},{16,12},{20,16},{24,20},{28,24},{1,29},{... | collective-permute-start | bytes 442376 | tf_op jit(solution)/shard_map/ppermute | solution.py:69
  162.1 6.0 %collective-permute-start.21 = (bf16[576,128]{1,0:T(8,128)(2,1)S(1)}, bf16[576,128]{1,0:T(8,128)(2,1)S(1)}, u32[]{:S(2)}, u32[]{:S(2)}) collective-permute-start(bf16[576,128]{1,0:T(8,128)(2,1)S(1)} %add_convert_fusion.2), channel_id=1, source_target_pairs={{0,4},{4,8},{8,12},{12,16},{16,20},{20,24},{24,28},{28,0},{1,5},{5... | collective-permute-start | bytes 442376 | tf_op jit(solution)/shard_map/ppermute | solution.py:69
  168.1 6.7 %collective-permute-start.18 = (bf16[576,128]{1,0:T(8,128)(2,1)S(1)}, bf16[576,128]{1,0:T(8,128)(2,1)S(1)}, u32[]{:S(2)}, u32[]{:S(2)}) collective-permute-start(bf16[576,128]{1,0:T(8,128)(2,1)S(1)} %add_convert_fusion.4), channel_id=1, source_target_pairs={{0,28},{1,29},{2,61},{3,60},{4,0},{5,1},{6,33},{7,32},{8,4},{9,5},... | collective-permute-start | bytes 442376 | tf_op jit(solution)/shard_map/ppermute | solution.py:57
  170.8 8.0 %collective-permute-start.22 = (bf16[576,128]{1,0:T(8,128)(2,1)S(1)}, bf16[576,128]{1,0:T(8,128)(2,1)S(1)}, u32[]{:S(2)}, u32[]{:S(2)}) collective-permute-start(bf16[576,128]{1,0:T(8,128)(2,1)S(1)} %add_convert_fusion.1), channel_id=1, source_target_pairs={{0,4},{1,5},{2,37},{3,36},{4,8},{5,9},{6,41},{7,40},{8,12},{9,13},... | collective-permute-start | bytes 442376 | tf_op jit(solution)/shard_map/ppermute | solution.py:57

commit v5 on v4

--- a/solution.py
+++ b/solution.py
@@ -147,8 +147,24 @@
         g = qg[:, :C]
         for t in range(KEYS // TILE):
             cols = slice(t * TILE, (t + 1) * TILE)
-            s_ref[rows, cols] = dot(q, kt[:, cols])
+            raw = dot(q, kt[:, cols])
             gp_ref[rows, cols] = dot(g, kt[:C, cols])
+            inside = [above + base[2 * t + n] >= 0 for n in range(2)]
+            gap = [ahead + base[2 * t + n] for n in range(2)]
+            for j in range(NQ // 8):
+                ok = [inside[n] & (gap[n] <= 8 * j) for n in range(2)]
+                for h in range(HEADS):
+                    r = slice(h * NQ + 8 * j, h * NQ + 8 * j + 8)
+                    at = slice(half * ROWS + r.start, half * ROWS + r.stop)
+                    v = [
+                        jnp.where(ok[n], raw[r, n * BLK : (n + 1) * BLK], NEG_FILL)
+                        for n in range(2)
+                    ]
+                    for n in range(2):
+                        b = 2 * t + n
+                        s_ref[at, b * BLK : (b + 1) * BLK] = v[n]
+                    top = jnp.maximum(v[0], v[1])
+                    wide[at, :] = top if t == 0 else jnp.maximum(wide[at, :], top)
     chunk = NQ
 
     @pl.loop(0, 2 * ROWS // chunk)
@@ -156,24 +172,13 @@
         r0 = pl.multiple_of(i * chunk, chunk)
         here = pl.ds(r0, chunk)
         below = pl.ds(pl.multiple_of(2 * ROWS + r0, chunk), chunk)
-        peak = [None] * (chunk // 8)
-        for b in range(16):
-            cols = slice(b * BLK, (b + 1) * BLK)
-            inside = above + base[b] >= 0
-            gap = ahead + base[b]
-            for k in range(chunk // 8):
-                r = pl.ds(pl.multiple_of(r0 + 8 * k, 8), 8)
-                ok = inside & (gap <= 8 * k)
-                v = jnp.where(ok, s_ref[r, cols] * SCALE, NEG_FILL)
-                s_ref[r, cols] = v
-                peak[k] = v if peak[k] is None else jnp.maximum(peak[k], v)
-        m = jnp.max(jnp.concatenate(peak, axis=0), axis=1, keepdims=True)
+        m = jnp.max(wide[here, :], axis=1, keepdims=True)
         safe = jnp.broadcast_to(jnp.maximum(m, 0.1 * NEG_FILL), (chunk, BLK))
         total = None
         rsum = None
         for b in range(16):
             cols = slice(b * BLK, (b + 1) * BLK)
-            e = jnp.exp(s_ref[here, cols] - safe)
+            e = jnp.exp2((s_ref[here, cols] - safe) * (SCALE * math.log2(math.e)))
             s_ref[here, cols] = e
             p = e * gp_ref[here, cols]
             total = e if total is None else total + e
@@ -189,7 +194,7 @@
             out[here, oc] = (e * (gp_ref[here, cols] - rdb)).astype(BF)
             out[below, oc] = e.astype(BF)
         col = lax.broadcasted_iota(jnp.int32, (chunk, BLK), 1)
-        wide[here, :] = jnp.where(col == 0, m, jnp.where(col == 1, l, rd))
+        wide[here, :] = jnp.where(col == 0, m * SCALE, jnp.where(col == 1, l, rd))
 
     stats[...] = jnp.transpose(wide[...])[0:8, :]
 

time: 180 us -> 177 us (0.983)
  Pallas kernels: 26.2 us -> 23.2 us
    pallas_call x8, Pallas kernels: 26.2 us -> 23.2 us  [call(): pl.pallas_call(body, out_shape=out_shape, in_specs=specs, out_specs=[pl.B...]
where the time goes in v5:
time: 177 us
  waiting for transfers between devices  75.4 us (43%)
  starting transfers between devices  63.7 us (36%)
  Pallas kernels  23.2 us (13%)
  local copies, waits for them, and re-layouts  6.47 us (4%)
  other arithmetic  5.6 us (3%)
  between operations  2.17 us (1%)
    ppermute x10, waiting for transfers between devices, along_z(): return lax.ppermute(v, 'z', [(i, (i + step) % NZ) for i in range(NZ)])  25.7 us
    pallas_call x8, Pallas kernels, call(): pl.pallas_call(body, out_shape=out_shape, in_specs=specs, out_specs=[pl.B...  23.2 us
    ppermute x6, starting transfers between devices, homeward(): return lax.ppermute(v, ('core', 'z', 'y'), pairs)  22.1 us
    ppermute x4, waiting for transfers between devices, turn(): return lax.ppermute(v, ('core', 'y'), turned(flip))  20.5 us
    ppermute x4, starting transfers between devices, turn(): return lax.ppermute(v, ('core', 'y'), turned(flip))  11.3 us
    ppermute x6, waiting for transfers between devices, homeward(): return lax.ppermute(v, ('core', 'z', 'y'), pairs)  11.3 us
    ppermute x10, starting transfers between devices, along_z(): return lax.ppermute(v, 'z', [(i, (i + step) % NZ) for i in range(NZ)])  10.3 us
    all_to_all x1, waiting for transfers between devices, step(): both = lax.all_to_all(both, CTX, 0, 0, tiled=True)  8.94 us
  transfers between devices with their start and end apart: 29, of which 17 were waited for; matrix products, arithmetic and copies ran while one was open for 3% of the time, Pallas kernels for 7%

profile of v5, /device:TPU:1, one launch (start us, length us, event | category | flops | bytes accessed | tf_op | source)
XLA Modules:
  0.0 176.5 jit_solution(587553835597793672)
XLA Ops:
  0.7 5.5 %collective-permute-start.3 = (bf16[576,128]{1,0:T(8,128)(2,1)}, bf16[576,128]{1,0:T(8,128)(2,1)S(1)}, u32[]{:S(2)}, u32[]{:S(2)}) collective-permute-start(bf16[576,128]{1,0:T(8,128)(2,1)} %bitcast.21), channel_id=1, source_target_pairs={{0,4},{1,5},{2,37},{3,36},{4,8},{5,9},{6,41},{7,40},{8,12},{9,13},... | collective-permute-start | bytes 442376 | tf_op jit(solution)/shard_map/ppermute | solution.py:57
  6.2 4.0 %collective-permute-start.7 = (bf16[576,128]{1,0:T(8,128)(2,1)}, bf16[576,128]{1,0:T(8,128)(2,1)S(1)}, u32[]{:S(2)}, u32[]{:S(2)}) collective-permute-start(bf16[576,128]{1,0:T(8,128)(2,1)} %bitcast.22), channel_id=1, source_target_pairs={{0,28},{1,29},{2,61},{3,60},{4,0},{5,1},{6,33},{7,32},{8,4},{9,5},... | collective-permute-start | bytes 442376 | tf_op jit(solution)/shard_map/ppermute | solution.py:57
  10.2 4.4 %collective-permute-done.3.refs_6_ = bf16[576,128]{1,0:T(8,128)(2,1)S(1)} collective-permute-done((bf16[576,128]{1,0:T(8,128)(2,1)}, bf16[576,128]{1,0:T(8,128)(2,1)S(1)}, u32[]{:S(2)}, u32[]{:S(2)}) %collective-permute-start.3) | collective-permute-done | bytes 147488 | tf_op jit(solution)/shard_map/ppermute | solution.py:57
  14.7 2.7 %collective-permute-start.8 = (bf16[576,128]{1,0:T(8,128)(2,1)S(1)}, bf16[576,128]{1,0:T(8,128)(2,1)S(1)}, u32[]{:S(2)}, u32[]{:S(2)}) collective-permute-start(bf16[576,128]{1,0:T(8,128)(2,1)S(1)} %collective-permute-done.7.refs_7_), channel_id=1, source_target_pairs={{0,28},{4,0},{8,4},{12,8},{16,12},{20,16},{24,20},{28,24},{1,29},{... | collective-permute-start | bytes 442376 | tf_op jit(solution)/shard_map/ppermute | solution.py:69
  17.3 2.5 %collective-permute-done.4.refs_4_ = bf16[576,128]{1,0:T(8,128)(2,1)S(1)} collective-permute-done((bf16[576,128]{1,0:T(8,128)(2,1)S(1)}, bf16[576,128]{1,0:T(8,128)(2,1)S(1)}, u32[]{:S(2)}, u32[]{:S(2)}) %collective-permute-start.4) | collective-permute-done | bytes 147488 | tf_op jit(solution)/shard_map/ppermute | solution.py:69
  19.9 3.0 %collective-permute-start.2 = (bf16[576,128]{1,0:T(8,128)(2,1)}, bf16[576,128]{1,0:T(8,128)(2,1)S(1)}, u32[]{:S(2)}, u32[]{:S(2)}) collective-permute-start(bf16[576,128]{1,0:T(8,128)(2,1)} %bitcast.23), channel_id=1, source_target_pairs={{0,0},{1,1},{2,33},{3,32},{4,4},{5,5},{6,37},{7,36},{8,8},{9,9},{1... | collective-permute-start | bytes 442376 | tf_op jit(solution)/shard_map/ppermute | solution.py:57
  22.9 3.0 %collective-permute-start.9 = (bf16[576,128]{1,0:T(8,128)(2,1)S(1)}, bf16[576,128]{1,0:T(8,128)(2,1)S(1)}, u32[]{:S(2)}, u32[]{:S(2)}) collective-permute-start(bf16[576,128]{1,0:T(8,128)(2,1)S(1)} %collective-permute-done.8.refs_5_), channel_id=1, source_target_pairs={{0,28},{4,0},{8,4},{12,8},{16,12},{20,16},{24,20},{28,24},{1,29},{... | collective-permute-start | bytes 442376 | tf_op jit(solution)/shard_map/ppermute | solution.py:69
  25.9 1.8 %collective-permute-done.2.refs_0_ = bf16[576,128]{1,0:T(8,128)(2,1)S(1)} collective-permute-done((bf16[576,128]{1,0:T(8,128)(2,1)}, bf16[576,128]{1,0:T(8,128)(2,1)S(1)}, u32[]{:S(2)}, u32[]{:S(2)}) %collective-permute-start.2) | collective-permute-done | bytes 147488 | tf_op jit(solution)/shard_map/ppermute | solution.py:57
  28.0 4.7 %collective-permute-done.6.refs_1_ = bf16[576,128]{1,0:T(8,128)(2,1)S(1)} collective-permute-done((bf16[576,128]{1,0:T(8,128)(2,1)S(1)}, bf16[576,128]{1,0:T(8,128)(2,1)S(1)}, u32[]{:S(2)}, u32[]{:S(2)}) %collective-permute-start.6) | collective-permute-done | bytes 147488 | tf_op jit(solution)/shard_map/ppermute | solution.py:69
  34.7 8.8 %all-to-all-start = ((bf16[32,2,1280]{2,1,0:T(2,128)(2,1)}), bf16[32,2,1280]{2,1,0:T(2,128)(2,1)S(1)}, u32[]{:S(2)}, u32[]{:S(2)}) async-start(bf16[32,2,1280]{2,1,0:T(2,128)(2,1)} %maximum_bitcast_fusion), calls=%async_computation | async-start | bytes 327680 | tf_op jit(solution)/shard_map/all_to_all | solution.py:316
  44.7 8.9 %all-to-all-done = bf16[32,2,1280]{2,1,0:T(2,128)(2,1)S(1)} async-done(((bf16[32,2,1280]{2,1,0:T(2,128)(2,1)}), bf16[32,2,1280]{2,1,0:T(2,128)(2,1)S(1)}, u32[]{:S(2)}, u32[]{:S(2)}) %all-to-all-start) | async-done | bytes 163872 | tf_op jit(solution)/shard_map/all_to_all | solution.py:316
  53.7 1.7 shard_map.85
  55.5 2.8 %collective-permute-start.1 = (bf16[256,1152]{1,0:T(8,128)(2,1)S(1)}, bf16[256,1152]{1,0:T(8,128)(2,1)}, u32[]{:S(2)}, u32[]{:S(2)}) collective-permute-start(bf16[256,1152]{1,0:T(8,128)(2,1)S(1)} %shard_map.85), channel_id=1, source_target_pairs={{0,1},{1,0},{2,33},{3,32},{32,3},{33,2},{34,35},{35,34},{4,5},{5,4... | collective-permute-start | bytes 1769480 | tf_op jit(solution)/shard_map/ppermute | solution.py:46
  58.3 1.9 %collective-permute-start = (bf16[256,1152]{1,0:T(8,128)(2,1)S(1)}, bf16[256,1152]{1,0:T(8,128)(2,1)}, u32[]{:S(2)}, u32[]{:S(2)}) collective-permute-start(bf16[256,1152]{1,0:T(8,128)(2,1)S(1)} %shard_map.85), channel_id=1, source_target_pairs={{0,0},{1,1},{2,32},{3,33},{32,2},{33,3},{34,34},{35,35},{4,4},{5,5... | collective-permute-start | bytes 1769480 | tf_op jit(solution)/shard_map/ppermute | solution.py:46
  60.3 12.2 %collective-permute-done.1.refs_2_.other = bf16[256,1152]{1,0:T(8,128)(2,1)} collective-permute-done((bf16[256,1152]{1,0:T(8,128)(2,1)S(1)}, bf16[256,1152]{1,0:T(8,128)(2,1)}, u32[]{:S(2)}, u32[]{:S(2)}) %collective-permute-start.1) | collective-permute-done | bytes 589856 | tf_op jit(solution)/shard_map/ppermute | solution.py:46
  72.5 1.0 copy-done.7
  73.5 1.3 copy-done.4
  74.8 1.3 copy-done.8
  76.1 7.5 %shard_map.87 = (bf16[1024,1024]{1,0:T(8,128)(2,1)S(1)}, bf16[1024,1024]{1,0:T(8,128)(2,1)S(1)}, bf16[576,2048]{1,0:T(8,128)(2,1)S(1)}, f32[8,512]{1,0:T(8,128)S(1)}) custom-call(s32[4]{0:T(128)S(1)} %pad_add_fusion.refs_0_.scal, bf16[256,1152]{1,0:T(8,128)(2,1)} %collective-permute-done.refs_1_.mine, ...), custom_call_target="tpu_custom_call" | custom-call | flops 2280000000 | bytes 10108944 | tf_op jit(solution)/shard_map/pallas_call | solution.py:89
  83.8 2.8 %collective-permute-done.11.their = f32[8,512]{1,0:T(8,128)S(1)} collective-permute-done((f32[8,512]{1,0:T(8,128)S(1)}, f32[8,512]{1,0:T(8,128)S(1)}, u32[]{:S(2)}, u32[]{:S(2)}) %collective-permute-start.11) | collective-permute-done | bytes 16416 | tf_op jit(solution)/shard_map/ppermute | solution.py:65
  86.6 3.6 %shard_map.88 = (bf16[256,1152]{1,0:T(8,128)(2,1)S(1)}, bf16[256,1152]{1,0:T(8,128)(2,1)S(1)}, f32[512,128]{1,0:T(8,128)S(1)}) custom-call(f32[8,512]{1,0:T(8,128)S(1)} %get-tuple-element.23.st, f32[8,512]{1,0:T(8,128)S(1)} %collective-permute-done.11.their, bf16[576,2048]{1,0:T(8,128)(2,1)S(1)} %get-tuple-element.24.kt, ...), custom_call_target="tpu_custom_call" | custom-call | flops 2400000000 | bytes 8028160 | tf_op jit(solution)/shard_map/pallas_call | solution.py:89
  90.1 5.9 %collective-permute-start.12 = (bf16[256,1152]{1,0:T(8,128)(2,1)S(1)}, bf16[256,1152]{1,0:T(8,128)(2,1)S(1)}, u32[]{:S(2)}, u32[]{:S(2)}) collective-permute-start(bf16[256,1152]{1,0:T(8,128)(2,1)S(1)} %get-tuple-element.27), channel_id=1, source_target_pairs={{0,0},{1,1},{2,32},{3,33},{32,2},{33,3},{34,34},{35,35},{4,4},{5,5... | collective-permute-start | bytes 1769480 | tf_op jit(solution)/shard_map/ppermute | solution.py:46
  96.7 4.9 %shard_map.90 = (bf16[1024,576]{1,0:T(8,128)(2,1)S(1)}, bf16[8,576,128]{2,1,0:T(8,128)(2,1)}) custom-call(f32[512,128]{1,0:T(8,128)S(1)} %get-tuple-element.30.ws, bf16[256,1152]{1,0:T(8,128)(2,1)} %collective-permute-done.refs_1_.mine, bf16[256,1152]{1,0:T(8,128)(2,1)} %collective-permute-done.1.refs_2_.other, bf16[1024,1024]{1,0:T(8,128)(2,1)S(1)} %get-tuple-element.26.e1.ee), custom_call_target="tpu_custom_call" | custom-call | flops 1300000000 | bytes 5898240 | tf_op jit(solution)/shard_map/pallas_call | solution.py:89
  101.6 3.1 %collective-permute-done.12 = bf16[256,1152]{1,0:T(8,128)(2,1)S(1)} collective-permute-done((bf16[256,1152]{1,0:T(8,128)(2,1)S(1)}, bf16[256,1152]{1,0:T(8,128)(2,1)S(1)}, u32[]{:S(2)}, u32[]{:S(2)}) %collective-permute-start.12) | collective-permute-done | bytes 589856 | tf_op jit(solution)/shard_map/ppermute | solution.py:46
  104.7 5.2 %collective-permute-done.13 = bf16[256,1152]{1,0:T(8,128)(2,1)S(1)} collective-permute-done((bf16[256,1152]{1,0:T(8,128)(2,1)S(1)}, bf16[256,1152]{1,0:T(8,128)(2,1)S(1)}, u32[]{:S(2)}, u32[]{:S(2)}) %collective-permute-start.13) | collective-permute-done | bytes 589856 | tf_op jit(solution)/shard_map/ppermute | solution.py:46
  110.1 2.0 %shard_map.89 = (bf16[64,768]{1,0:T(8,128)(2,1)S(1)}, bf16[256,1024]{1,0:T(8,128)(2,1)S(1)}, bf16[256,1024]{1,0:T(8,128)(2,1)}) custom-call(s32[4]{0:T(128)S(1)} %pad_add_fusion.refs_0_.scal, bf16[256,1152]{1,0:T(8,128)(2,1)S(1)} %add_convert_fusion.qo, bf16[64,1280]{1,0:T(8,128)(2,1)S(1)} %reshape.35.both, bf16[512,1024]{1,0:T(8,128)(2,1)S(1)} %copy-done), custom_call_target="tpu_custom_call" | custom-call | flops 200000000 | bytes 2949136 | tf_op jit(solution)/shard_map/pallas_call | solution.py:89
  112.0 0.8 copy-done.5
  113.5 6.0 %all-to-all-start.1 = ((bf16[32,2,768]{2,1,0:T(2,128)(2,1)}), bf16[32,2,768]{2,1,0:T(2,128)(2,1)S(1)}, u32[]{:S(2)}, u32[]{:S(2)}) async-start(bf16[32,2,768]{2,1,0:T(2,128)(2,1)} %reshape.36), calls=%async_computation.1 | async-start | bytes 196608 | tf_op jit(solution)/shard_map/all_to_all | solution.py:409
  119.5 1.3 copy-done.2
  120.9 1.7 shard_map.91.a
  122.6 6.2 %all-to-all-done.1 = bf16[32,2,768]{2,1,0:T(2,128)(2,1)S(1)} async-done(((bf16[32,2,768]{2,1,0:T(2,128)(2,1)}), bf16[32,2,768]{2,1,0:T(2,128)(2,1)S(1)}, u32[]{:S(2)}, u32[]{:S(2)}) %all-to-all-start.1) | async-done | bytes 98336 | tf_op jit(solution)/shard_map/all_to_all | solution.py:409
  129.5 1.6 shard_map.92
  131.7 1.2 add_convert_fusion.8
  132.8 1.3 collective-permute-start.24
  134.1 1.5 collective-permute-start.26
  135.6 1.5 collective-permute-start.25
  137.1 5.5 %collective-permute-start.15 = (bf16[576,128]{1,0:T(8,128)(2,1)S(1)}, bf16[576,128]{1,0:T(8,128)(2,1)S(1)}, u32[]{:S(2)}, u32[]{:S(2)}) collective-permute-start(bf16[576,128]{1,0:T(8,128)(2,1)S(1)} %get-tuple-element.33), channel_id=1, source_target_pairs={{0,0},{1,1},{2,33},{3,32},{4,4},{5,5},{6,37},{7,36},{8,8},{9,9},{1... | collective-permute-start | bytes 442376 | tf_op jit(solution)/shard_map/ppermute | solution.py:57
  142.7 2.3 %collective-permute-start.16 = (bf16[576,128]{1,0:T(8,128)(2,1)S(1)}, bf16[576,128]{1,0:T(8,128)(2,1)S(1)}, u32[]{:S(2)}, u32[]{:S(2)}) collective-permute-start(bf16[576,128]{1,0:T(8,128)(2,1)S(1)} %get-tuple-element.36), channel_id=1, source_target_pairs={{0,28},{4,0},{8,4},{12,8},{16,12},{20,16},{24,20},{28,24},{1,29},{... | collective-permute-start | bytes 442376 | tf_op jit(solution)/shard_map/ppermute | solution.py:69
  145.1 2.1 %collective-permute-done.16 = bf16[576,128]{1,0:T(8,128)(2,1)S(1)} collective-permute-done((bf16[576,128]{1,0:T(8,128)(2,1)S(1)}, bf16[576,128]{1,0:T(8,128)(2,1)S(1)}, u32[]{:S(2)}, u32[]{:S(2)}) %collective-permute-start.16) | collective-permute-done | bytes 147488 | tf_op jit(solution)/shard_map/ppermute | solution.py:69
  147.2 6.2 %collective-permute-done.20 = bf16[576,128]{1,0:T(8,128)(2,1)S(1)} collective-permute-done((bf16[576,128]{1,0:T(8,128)(2,1)S(1)}, bf16[576,128]{1,0:T(8,128)(2,1)S(1)}, u32[]{:S(2)}, u32[]{:S(2)}) %collective-permute-start.20) | collective-permute-done | bytes 147488 | tf_op jit(solution)/shard_map/ppermute | solution.py:69
  153.4 1.7 collective-permute-start.17
  155.2 3.9 %collective-permute-done.17 = bf16[576,128]{1,0:T(8,128)(2,1)S(1)} collective-permute-done((bf16[576,128]{1,0:T(8,128)(2,1)S(1)}, bf16[576,128]{1,0:T(8,128)(2,1)S(1)}, u32[]{:S(2)}, u32[]{:S(2)}) %collective-permute-start.17) | collective-permute-done | bytes 147488 | tf_op jit(solution)/shard_map/ppermute | solution.py:69
  159.1 5.9 %collective-permute-done.21 = bf16[576,128]{1,0:T(8,128)(2,1)S(1)} collective-permute-done((bf16[576,128]{1,0:T(8,128)(2,1)S(1)}, bf16[576,128]{1,0:T(8,128)(2,1)S(1)}, u32[]{:S(2)}, u32[]{:S(2)}) %collective-permute-start.21) | collective-permute-done | bytes 147488 | tf_op jit(solution)/shard_map/ppermute | solution.py:69
  165.0 2.7 %collective-permute-start.18 = (bf16[576,128]{1,0:T(8,128)(2,1)S(1)}, bf16[576,128]{1,0:T(8,128)(2,1)S(1)}, u32[]{:S(2)}, u32[]{:S(2)}) collective-permute-start(bf16[576,128]{1,0:T(8,128)(2,1)S(1)} %add_convert_fusion.4), channel_id=1, source_target_pairs={{0,28},{1,29},{2,61},{3,60},{4,0},{5,1},{6,33},{7,32},{8,4},{9,5},... | collective-permute-start | bytes 442376 | tf_op jit(solution)/shard_map/ppermute | solution.py:57
  167.8 1.2 collective-permute-start.22
  169.0 1.7 convert_add_fusion
  170.7 1.0 collective-permute-done.18
  171.7 4.0 %collective-permute-done.22 = bf16[576,128]{1,0:T(8,128)(2,1)S(1)} collective-permute-done((bf16[576,128]{1,0:T(8,128)(2,1)S(1)}, bf16[576,128]{1,0:T(8,128)(2,1)S(1)}, u32[]{:S(2)}, u32[]{:S(2)}) %collective-permute-start.22) | collective-permute-done | bytes 147488 | tf_op jit(solution)/shard_map/ppermute | solution.py:57
  (54 shorter events, 6.4 us)
Async XLA Ops:
  0.6 33.2 %copy-start.9 = (bf16[1,2,24576]{2,1,0:T(2,128)(2,1)S(1)}, bf16[1,2,24576]{2,1,0:T(2,128)(2,1)}, u32[]{:S(2)}) copy-start(bf16[1,2,24576]{2,1,0:T(2,128)(2,1)} %param.6) | copy-start | bytes 294916
  0.6 33.2 %copy-start.10 = (bf16[1,2,16384]{2,1,0:T(2,128)(2,1)S(1)}, bf16[1,2,16384]{2,1,0:T(2,128)(2,1)}, u32[]{:S(2)}) copy-start(bf16[1,2,16384]{2,1,0:T(2,128)(2,1)} %param.7) | copy-start | bytes 196612
  0.7 14.0 %collective-permute-start.3 = (bf16[576,128]{1,0:T(8,128)(2,1)}, bf16[576,128]{1,0:T(8,128)(2,1)S(1)}, u32[]{:S(2)}, u32[]{:S(2)}) collective-permute-start(bf16[576,128]{1,0:T(8,128)(2,1)} %bitcast.21), channel_id=1, source_target_pairs={{0,4},{1,5},{2,37},{3,36},{4,8},{5,9},{6,41},{7,40},{8,12},{9,13},... | collective-permute-start | bytes 442376 | tf_op jit(solution)/shard_map/ppermute | solution.py:57
  6.2 8.5 %collective-permute-start.7 = (bf16[576,128]{1,0:T(8,128)(2,1)}, bf16[576,128]{1,0:T(8,128)(2,1)S(1)}, u32[]{:S(2)}, u32[]{:S(2)}) collective-permute-start(bf16[576,128]{1,0:T(8,128)(2,1)} %bitcast.22), channel_id=1, source_target_pairs={{0,28},{1,29},{2,61},{3,60},{4,0},{5,1},{6,33},{7,32},{8,4},{9,5},... | collective-permute-start | bytes 442376 | tf_op jit(solution)/shard_map/ppermute | solution.py:57
  14.7 5.2 %collective-permute-start.4 = (bf16[576,128]{1,0:T(8,128)(2,1)S(1)}, bf16[576,128]{1,0:T(8,128)(2,1)S(1)}, u32[]{:S(2)}, u32[]{:S(2)}) collective-permute-start(bf16[576,128]{1,0:T(8,128)(2,1)S(1)} %collective-permute-done.3.refs_6_), channel_id=1, source_target_pairs={{0,4},{4,8},{8,12},{12,16},{16,20},{20,24},{24,28},{28,0},{1,5},{5... | collective-permute-start | bytes 442376 | tf_op jit(solution)/shard_map/ppermute | solution.py:69
  14.7 8.2 %collective-permute-start.8 = (bf16[576,128]{1,0:T(8,128)(2,1)S(1)}, bf16[576,128]{1,0:T(8,128)(2,1)S(1)}, u32[]{:S(2)}, u32[]{:S(2)}) collective-permute-start(bf16[576,128]{1,0:T(8,128)(2,1)S(1)} %collective-permute-done.7.refs_7_), channel_id=1, source_target_pairs={{0,28},{4,0},{8,4},{12,8},{16,12},{20,16},{24,20},{28,24},{1,29},{... | collective-permute-start | bytes 442376 | tf_op jit(solution)/shard_map/ppermute | solution.py:69
  19.9 6.1 %collective-permute-start.5 = (bf16[576,128]{1,0:T(8,128)(2,1)S(1)}, bf16[576,128]{1,0:T(8,128)(2,1)S(1)}, u32[]{:S(2)}, u32[]{:S(2)}) collective-permute-start(bf16[576,128]{1,0:T(8,128)(2,1)S(1)} %collective-permute-done.4.refs_4_), channel_id=1, source_target_pairs={{0,4},{4,8},{8,12},{12,16},{16,20},{20,24},{24,28},{28,0},{1,5},{5... | collective-permute-start | bytes 442376 | tf_op jit(solution)/shard_map/ppermute | solution.py:69
  19.9 7.9 %collective-permute-start.2 = (bf16[576,128]{1,0:T(8,128)(2,1)}, bf16[576,128]{1,0:T(8,128)(2,1)S(1)}, u32[]{:S(2)}, u32[]{:S(2)}) collective-permute-start(bf16[576,128]{1,0:T(8,128)(2,1)} %bitcast.23), channel_id=1, source_target_pairs={{0,0},{1,1},{2,33},{3,32},{4,4},{5,5},{6,37},{7,36},{8,8},{9,9},{1... | collective-permute-start | bytes 442376 | tf_op jit(solution)/shard_map/ppermute | solution.py:57
  22.9 5.1 %collective-permute-start.9 = (bf16[576,128]{1,0:T(8,128)(2,1)S(1)}, bf16[576,128]{1,0:T(8,128)(2,1)S(1)}, u32[]{:S(2)}, u32[]{:S(2)}) collective-permute-start(bf16[576,128]{1,0:T(8,128)(2,1)S(1)} %collective-permute-done.8.refs_5_), channel_id=1, source_target_pairs={{0,28},{4,0},{8,4},{12,8},{16,12},{20,16},{24,20},{28,24},{1,29},{... | collective-permute-start | bytes 442376 | tf_op jit(solution)/shard_map/ppermute | solution.py:69
  25.9 6.8 %collective-permute-start.6 = (bf16[576,128]{1,0:T(8,128)(2,1)S(1)}, bf16[576,128]{1,0:T(8,128)(2,1)S(1)}, u32[]{:S(2)}, u32[]{:S(2)}) collective-permute-start(bf16[576,128]{1,0:T(8,128)(2,1)S(1)} %collective-permute-done.5.refs_2_), channel_id=1, source_target_pairs={{0,4},{4,8},{8,12},{12,16},{16,20},{20,24},{24,28},{28,0},{1,5},{5... | collective-permute-start | bytes 442376 | tf_op jit(solution)/shard_map/ppermute | solution.py:69
  33.1 22.3 %copy-start.3 = (bf16[576,1024]{1,0:T(8,128)(2,1)}, bf16[576,1024]{1,0:T(8,128)(2,1)S(1)}, u32[]{:S(2)}) copy-start(bf16[576,1024]{1,0:T(8,128)(2,1)S(1)} %shard_map.86.refs_3_) | copy-start | bytes 3538948
  33.1 39.4 %collective-permute-start.10 = (bf16[576,1024]{1,0:T(8,128)(2,1)S(1)}, bf16[576,1024]{1,0:T(8,128)(2,1)S(1)}, u32[]{:S(2)}, u32[]{:S(2)}) collective-permute-start(bf16[576,1024]{1,0:T(8,128)(2,1)S(1)} %shard_map.86.refs_3_), channel_id=1, source_target_pairs={{0,32},{32,0},{1,33},{33,1},{2,34},{34,2},{3,35},{35,3},{4,36},{36... | collective-permute-start | bytes 3538952 | tf_op jit(solution)/shard_map/ppermute | solution.py:61
  34.7 19.0 %all-to-all-start = ((bf16[32,2,1280]{2,1,0:T(2,128)(2,1)}), bf16[32,2,1280]{2,1,0:T(2,128)(2,1)S(1)}, u32[]{:S(2)}, u32[]{:S(2)}) async-start(bf16[32,2,1280]{2,1,0:T(2,128)(2,1)} %maximum_bitcast_fusion), calls=%async_computation | async-start | bytes 327680 | tf_op jit(solution)/shard_map/all_to_all | solution.py:316
  55.5 17.0 %collective-permute-start.1 = (bf16[256,1152]{1,0:T(8,128)(2,1)S(1)}, bf16[256,1152]{1,0:T(8,128)(2,1)}, u32[]{:S(2)}, u32[]{:S(2)}) collective-permute-start(bf16[256,1152]{1,0:T(8,128)(2,1)S(1)} %shard_map.85), channel_id=1, source_target_pairs={{0,1},{1,0},{2,33},{3,32},{32,3},{33,2},{34,35},{35,34},{4,5},{5,4... | collective-permute-start | bytes 1769480 | tf_op jit(solution)/shard_map/ppermute | solution.py:46
  58.3 14.2 %collective-permute-start = (bf16[256,1152]{1,0:T(8,128)(2,1)S(1)}, bf16[256,1152]{1,0:T(8,128)(2,1)}, u32[]{:S(2)}, u32[]{:S(2)}) collective-permute-start(bf16[256,1152]{1,0:T(8,128)(2,1)S(1)} %shard_map.85), channel_id=1, source_target_pairs={{0,0},{1,1},{2,32},{3,33},{32,2},{33,3},{34,34},{35,35},{4,4},{5,5... | collective-permute-start | bytes 1769480 | tf_op jit(solution)/shard_map/ppermute | solution.py:46
  72.5 1.0 copy-start.7
  73.5 1.3 copy-start.4
  74.8 1.3 copy-start.8
  83.5 3.0 %collective-permute-start.11 = (f32[8,512]{1,0:T(8,128)S(1)}, f32[8,512]{1,0:T(8,128)S(1)}, u32[]{:S(2)}, u32[]{:S(2)}) collective-permute-start(f32[8,512]{1,0:T(8,128)S(1)} %get-tuple-element.23.st), channel_id=1, source_target_pairs={{0,1},{1,0},{2,3},{3,2},{4,5},{5,4},{6,7},{7,6},{8,9},{9,8},{10,11... | collective-permute-start | bytes 49160 | tf_op jit(solution)/shard_map/ppermute | solution.py:65
  90.1 14.6 %collective-permute-start.12 = (bf16[256,1152]{1,0:T(8,128)(2,1)S(1)}, bf16[256,1152]{1,0:T(8,128)(2,1)S(1)}, u32[]{:S(2)}, u32[]{:S(2)}) collective-permute-start(bf16[256,1152]{1,0:T(8,128)(2,1)S(1)} %get-tuple-element.27), channel_id=1, source_target_pairs={{0,0},{1,1},{2,32},{3,33},{32,2},{33,3},{34,34},{35,35},{4,4},{5,5... | collective-permute-start | bytes 1769480 | tf_op jit(solution)/shard_map/ppermute | solution.py:46
  96.1 13.9 %collective-permute-start.13 = (bf16[256,1152]{1,0:T(8,128)(2,1)S(1)}, bf16[256,1152]{1,0:T(8,128)(2,1)S(1)}, u32[]{:S(2)}, u32[]{:S(2)}) collective-permute-start(bf16[256,1152]{1,0:T(8,128)(2,1)S(1)} %get-tuple-element.28), channel_id=1, source_target_pairs={{0,1},{1,0},{2,33},{3,32},{32,3},{33,2},{34,35},{35,34},{4,5},{5,4... | collective-permute-start | bytes 1769480 | tf_op jit(solution)/shard_map/ppermute | solution.py:46
  101.6 10.5 %copy-start.1 = (bf16[1024,576]{1,0:T(8,128)(2,1)}, bf16[1024,576]{1,0:T(8,128)(2,1)S(1)}, u32[]{:S(2)}) copy-start(bf16[1024,576]{1,0:T(8,128)(2,1)S(1)} %get-tuple-element.31.qq) | copy-start | bytes 3538948
  101.6 8.5 %copy-start = (bf16[512,1024]{1,0:T(8,128)(2,1)S(1)}, bf16[512,1024]{1,0:T(8,128)(2,1)}, u32[]{:S(2)}) copy-start(bf16[512,1024]{1,0:T(8,128)(2,1)} %w.3) | copy-start | bytes 3145732
  101.6 27.9 %collective-permute-start.14 = (bf16[8,576,128]{2,1,0:T(8,128)(2,1)}, bf16[8,576,128]{2,1,0:T(8,128)(2,1)}, u32[]{:S(2)}, u32[]{:S(2)}) collective-permute-start(bf16[8,576,128]{2,1,0:T(8,128)(2,1)} %get-tuple-element.32), channel_id=1, source_target_pairs={{0,32},{32,0},{1,33},{33,1},{2,34},{34,2},{3,35},{35,3},{4,36},{36... | collective-permute-start | bytes 3538952 | tf_op jit(solution)/shard_map/ppermute | solution.py:61
  112.0 0.8 copy-start.5
  112.9 18.8 %collective-permute-start.23 = (bf16[256,1024]{1,0:T(8,128)(2,1)}, bf16[256,1024]{1,0:T(8,128)(2,1)}, u32[]{:S(2)}, u32[]{:S(2)}) collective-permute-start(bf16[256,1024]{1,0:T(8,128)(2,1)} %get-tuple-element.42), channel_id=1, source_target_pairs={{0,32},{32,0},{1,33},{33,1},{2,34},{34,2},{3,35},{35,3},{4,36},{36... | collective-permute-start | bytes 1572872 | tf_op jit(solution)/shard_map/ppermute | solution.py:61
  113.5 15.2 %all-to-all-start.1 = ((bf16[32,2,768]{2,1,0:T(2,128)(2,1)}), bf16[32,2,768]{2,1,0:T(2,128)(2,1)S(1)}, u32[]{:S(2)}, u32[]{:S(2)}) async-start(bf16[32,2,768]{2,1,0:T(2,128)(2,1)} %reshape.36), calls=%async_computation.1 | async-start | bytes 196608 | tf_op jit(solution)/shard_map/all_to_all | solution.py:409
  119.5 1.3 copy-start.2
  129.5 2.2 %copy-start.6 = (bf16[256,1024]{1,0:T(8,128)(2,1)S(1)}, bf16[256,1024]{1,0:T(8,128)(2,1)}, u32[]{:S(2)}) copy-start(bf16[256,1024]{1,0:T(8,128)(2,1)} %copy-done.5) | copy-start | bytes 1572868
  131.1 11.6 %collective-permute-start.19 = (bf16[576,128]{1,0:T(8,128)(2,1)S(1)}, bf16[576,128]{1,0:T(8,128)(2,1)S(1)}, u32[]{:S(2)}, u32[]{:S(2)}) collective-permute-start(bf16[576,128]{1,0:T(8,128)(2,1)S(1)} %get-tuple-element.40), channel_id=1, source_target_pairs={{0,4},{4,8},{8,12},{12,16},{16,20},{20,24},{24,28},{28,0},{1,5},{5... | collective-permute-start | bytes 442376 | tf_op jit(solution)/shard_map/ppermute | solution.py:69
  132.8 35.0 %collective-permute-start.24 = (bf16[64,1024]{1,0:T(8,128)(2,1)S(1)}, bf16[64,1024]{1,0:T(8,128)(2,1)S(1)}, u32[]{:S(2)}, u32[]{:S(2)}) collective-permute-start(bf16[64,1024]{1,0:T(8,128)(2,1)S(1)} %get-tuple-element.43), channel_id=1, source_target_pairs={{0,64},{64,128},{128,192},{192,0},{1,65},{65,129},{129,193},{193,1... | collective-permute-start | bytes 393224 | tf_op jit(solution)/shard_map/ppermute | solution.py:407
  134.1 34.9 %collective-permute-start.26 = (bf16[64,1024]{1,0:T(8,128)(2,1)S(1)}, bf16[64,1024]{1,0:T(8,128)(2,1)S(1)}, u32[]{:S(2)}, u32[]{:S(2)}) collective-permute-start(bf16[64,1024]{1,0:T(8,128)(2,1)S(1)} %get-tuple-element.44), channel_id=1, source_target_pairs={{0,192},{64,0},{128,64},{192,128},{1,193},{65,1},{129,65},{193,129... | collective-permute-start | bytes 393224 | tf_op jit(solution)/shard_map/ppermute | solution.py:407
  135.6 33.5 %collective-permute-start.25 = (bf16[64,1024]{1,0:T(8,128)(2,1)S(1)}, bf16[64,1024]{1,0:T(8,128)(2,1)S(1)}, u32[]{:S(2)}, u32[]{:S(2)}) collective-permute-start(bf16[64,1024]{1,0:T(8,128)(2,1)S(1)} %get-tuple-element.45), channel_id=1, source_target_pairs={{0,128},{64,192},{128,0},{192,64},{1,129},{65,193},{129,1},{193,65... | collective-permute-start | bytes 393224 | tf_op jit(solution)/shard_map/ppermute | solution.py:407
  137.1 33.6 %collective-permute-start.15 = (bf16[576,128]{1,0:T(8,128)(2,1)S(1)}, bf16[576,128]{1,0:T(8,128)(2,1)S(1)}, u32[]{:S(2)}, u32[]{:S(2)}) collective-permute-start(bf16[576,128]{1,0:T(8,128)(2,1)S(1)} %get-tuple-element.33), channel_id=1, source_target_pairs={{0,0},{1,1},{2,33},{3,32},{4,4},{5,5},{6,37},{7,36},{8,8},{9,9},{1... | collective-permute-start | bytes 442376 | tf_op jit(solution)/shard_map/ppermute | solution.py:57
  142.7 4.4 %collective-permute-start.16 = (bf16[576,128]{1,0:T(8,128)(2,1)S(1)}, bf16[576,128]{1,0:T(8,128)(2,1)S(1)}, u32[]{:S(2)}, u32[]{:S(2)}) collective-permute-start(bf16[576,128]{1,0:T(8,128)(2,1)S(1)} %get-tuple-element.36), channel_id=1, source_target_pairs={{0,28},{4,0},{8,4},{12,8},{16,12},{20,16},{24,20},{28,24},{1,29},{... | collective-permute-start | bytes 442376 | tf_op jit(solution)/shard_map/ppermute | solution.py:69
  147.1 6.3 %collective-permute-start.20 = (bf16[576,128]{1,0:T(8,128)(2,1)S(1)}, bf16[576,128]{1,0:T(8,128)(2,1)S(1)}, u32[]{:S(2)}, u32[]{:S(2)}) collective-permute-start(bf16[576,128]{1,0:T(8,128)(2,1)S(1)} %add_convert_fusion.3), channel_id=1, source_target_pairs={{0,4},{4,8},{8,12},{12,16},{16,20},{20,24},{24,28},{28,0},{1,5},{5... | collective-permute-start | bytes 442376 | tf_op jit(solution)/shard_map/ppermute | solution.py:69
  153.4 5.6 %collective-permute-start.17 = (bf16[576,128]{1,0:T(8,128)(2,1)S(1)}, bf16[576,128]{1,0:T(8,128)(2,1)S(1)}, u32[]{:S(2)}, u32[]{:S(2)}) collective-permute-start(bf16[576,128]{1,0:T(8,128)(2,1)S(1)} %add_convert_fusion.5), channel_id=1, source_target_pairs={{0,28},{4,0},{8,4},{12,8},{16,12},{20,16},{24,20},{28,24},{1,29},{... | collective-permute-start | bytes 442376 | tf_op jit(solution)/shard_map/ppermute | solution.py:69
  159.0 6.0 %collective-permute-start.21 = (bf16[576,128]{1,0:T(8,128)(2,1)S(1)}, bf16[576,128]{1,0:T(8,128)(2,1)S(1)}, u32[]{:S(2)}, u32[]{:S(2)}) collective-permute-start(bf16[576,128]{1,0:T(8,128)(2,1)S(1)} %add_convert_fusion.2), channel_id=1, source_target_pairs={{0,4},{4,8},{8,12},{12,16},{16,20},{20,24},{24,28},{28,0},{1,5},{5... | collective-permute-start | bytes 442376 | tf_op jit(solution)/shard_map/ppermute | solution.py:69
  165.0 6.7 %collective-permute-start.18 = (bf16[576,128]{1,0:T(8,128)(2,1)S(1)}, bf16[576,128]{1,0:T(8,128)(2,1)S(1)}, u32[]{:S(2)}, u32[]{:S(2)}) collective-permute-start(bf16[576,128]{1,0:T(8,128)(2,1)S(1)} %add_convert_fusion.4), channel_id=1, source_target_pairs={{0,28},{1,29},{2,61},{3,60},{4,0},{5,1},{6,33},{7,32},{8,4},{9,5},... | collective-permute-start | bytes 442376 | tf_op jit(solution)/shard_map/ppermute | solution.py:57
  167.8 8.0 %collective-permute-start.22 = (bf16[576,128]{1,0:T(8,128)(2,1)S(1)}, bf16[576,128]{1,0:T(8,128)(2,1)S(1)}, u32[]{:S(2)}, u32[]{:S(2)}) collective-permute-start(bf16[576,128]{1,0:T(8,128)(2,1)S(1)} %add_convert_fusion.1), channel_id=1, source_target_pairs={{0,4},{1,5},{2,37},{3,36},{4,8},{5,9},{6,41},{7,40},{8,12},{9,13},... | collective-permute-start | bytes 442376 | tf_op jit(solution)/shard_map/ppermute | solution.py:57

commit v6 on v5

--- a/solution.py
+++ b/solution.py
@@ -224,7 +224,8 @@
     ws[...] = jnp.transpose(jnp.where(row == 0, a / denom, shift))
 
 
-def first_body(ws, mine, other, ee, qq, out):
+def first_body(st, their, mine, other, ee, qq, out, ws):
+    row_factors(st, their, ws)
     step = 64
     for half, qg in ((0, mine), (1, other)):
 
@@ -251,8 +252,7 @@
     key_parts(qq, ee, out)
 
 
-def query_body(st, their, kt, e0, e1, mine, other, ws):
-    row_factors(st, their, ws)
+def query_body(ws, kt, e0, e1, mine, other):
     for half, out in ((0, mine), (1, other)):
         xs = []
         for top in (0, 2 * ROWS):
@@ -354,21 +354,21 @@
     )
     theirs = pair_y(stats)
 
-    mine, other, ws = call(
+    piece = vmem((NZ, W, BLK), BF)
+    qq, their_keys, ws = call(
+        first_body,
+        [vmem((4 * ROWS, W), BF), piece, vmem((2 * ROWS, BLK), F32)],
+        (stats, theirs, qg_mine, qg_other, e_their),
+        1_300_000_000,
+    )
+    their_keys = other_core(their_keys)
+    mine, other = call(
         query_body,
-        [vmem((ROWS, WIDE), BF), vmem((ROWS, WIDE), BF), vmem((2 * ROWS, BLK), F32)],
-        (stats, theirs, kt, e_mine, e_their),
+        [vmem((ROWS, WIDE), BF), vmem((ROWS, WIDE), BF)],
+        (ws, kt, e_mine, e_their),
         2_400_000_000,
     )
     mine, other = turn(mine, 0), turn(other, 1)
-    piece = vmem((NZ, W, BLK), BF)
-    qq, their_keys = call(
-        first_body,
-        [vmem((4 * ROWS, W), BF), piece],
-        (ws, qg_mine, qg_other, e_their),
-        1_300_000_000,
-    )
-    their_keys = other_core(their_keys)
     (mine_keys,) = call(parts_body, [piece], (qq, e_mine), 1_200_000_000)
     sums = call(add_body, [vmem((W, BLK), BF)] * NZ, (mine_keys, their_keys), 1_000_000, mib=8)
     part = dict(zip(OFFSETS, sums))

time: 177 us -> 183 us (1.034)
  waiting for transfers between devices: 75.4 us -> 80.2 us
    ppermute x4, waiting for transfers between devices: 20.5 us -> 25.4 us  [turn(): return lax.ppermute(v, ('core', 'y'), turned(flip))]
  transfers between devices with their start and end apart: 29 -> 29, of which waited for: 17 -> 17; matrix products, arithmetic and copies ran while one was open for 3% -> 3% of each run, Pallas kernels for 7% -> 4%
where the time goes in v6:
time: 183 us
  waiting for transfers between devices  80.2 us (44%)
  starting transfers between devices  63.7 us (35%)
  Pallas kernels  23.3 us (13%)
  local copies, waits for them, and re-layouts  7.58 us (4%)
  other arithmetic  5.6 us (3%)
  between operations  2.18 us (1%)
    ppermute x10, waiting for transfers between devices, along_z(): return lax.ppermute(v, 'z', [(i, (i + step) % NZ) for i in range(NZ)])  25.7 us
    ppermute x4, waiting for transfers between devices, turn(): return lax.ppermute(v, ('core', 'y'), turned(flip))  25.4 us
    pallas_call x8, Pallas kernels, call(): pl.pallas_call(body, out_shape=out_shape, in_specs=specs, out_specs=[pl.B...  23.3 us
    ppermute x6, starting transfers between devices, homeward(): return lax.ppermute(v, ('core', 'z', 'y'), pairs)  22.1 us
    ppermute x6, waiting for transfers between devices, homeward(): return lax.ppermute(v, ('core', 'z', 'y'), pairs)  11.3 us
    ppermute x4, starting transfers between devices, turn(): return lax.ppermute(v, ('core', 'y'), turned(flip))  11.2 us
    ppermute x10, starting transfers between devices, along_z(): return lax.ppermute(v, 'z', [(i, (i + step) % NZ) for i in range(NZ)])  10.3 us
    all_to_all x1, waiting for transfers between devices, step(): both = lax.all_to_all(both, CTX, 0, 0, tiled=True)  8.94 us
  transfers between devices with their start and end apart: 29, of which 17 were waited for; matrix products, arithmetic and copies ran while one was open for 3% of the time, Pallas kernels for 4%

profile of v6, /device:TPU:1, one launch (start us, length us, event | category | flops | bytes accessed | tf_op | source)
XLA Modules:
  0.0 182.5 jit_solution(10132031000368405668)
XLA Ops:
  0.7 5.5 %collective-permute-start.3 = (bf16[576,128]{1,0:T(8,128)(2,1)}, bf16[576,128]{1,0:T(8,128)(2,1)S(1)}, u32[]{:S(2)}, u32[]{:S(2)}) collective-permute-start(bf16[576,128]{1,0:T(8,128)(2,1)} %bitcast.21), channel_id=1, source_target_pairs={{0,4},{1,5},{2,37},{3,36},{4,8},{5,9},{6,41},{7,40},{8,12},{9,13},... | collective-permute-start | bytes 442376 | tf_op jit(solution)/shard_map/ppermute | solution.py:57
  6.2 4.0 %collective-permute-start.7 = (bf16[576,128]{1,0:T(8,128)(2,1)}, bf16[576,128]{1,0:T(8,128)(2,1)S(1)}, u32[]{:S(2)}, u32[]{:S(2)}) collective-permute-start(bf16[576,128]{1,0:T(8,128)(2,1)} %bitcast.22), channel_id=1, source_target_pairs={{0,28},{1,29},{2,61},{3,60},{4,0},{5,1},{6,33},{7,32},{8,4},{9,5},... | collective-permute-start | bytes 442376 | tf_op jit(solution)/shard_map/ppermute | solution.py:57
  10.2 4.4 %collective-permute-done.3.refs_6_ = bf16[576,128]{1,0:T(8,128)(2,1)S(1)} collective-permute-done((bf16[576,128]{1,0:T(8,128)(2,1)}, bf16[576,128]{1,0:T(8,128)(2,1)S(1)}, u32[]{:S(2)}, u32[]{:S(2)}) %collective-permute-start.3) | collective-permute-done | bytes 147488 | tf_op jit(solution)/shard_map/ppermute | solution.py:57
  14.7 2.7 %collective-permute-start.8 = (bf16[576,128]{1,0:T(8,128)(2,1)S(1)}, bf16[576,128]{1,0:T(8,128)(2,1)S(1)}, u32[]{:S(2)}, u32[]{:S(2)}) collective-permute-start(bf16[576,128]{1,0:T(8,128)(2,1)S(1)} %collective-permute-done.7.refs_7_), channel_id=1, source_target_pairs={{0,28},{4,0},{8,4},{12,8},{16,12},{20,16},{24,20},{28,24},{1,29},{... | collective-permute-start | bytes 442376 | tf_op jit(solution)/shard_map/ppermute | solution.py:69
  17.3 2.5 %collective-permute-done.4.refs_4_ = bf16[576,128]{1,0:T(8,128)(2,1)S(1)} collective-permute-done((bf16[576,128]{1,0:T(8,128)(2,1)S(1)}, bf16[576,128]{1,0:T(8,128)(2,1)S(1)}, u32[]{:S(2)}, u32[]{:S(2)}) %collective-permute-start.4) | collective-permute-done | bytes 147488 | tf_op jit(solution)/shard_map/ppermute | solution.py:69
  19.9 3.0 %collective-permute-start.2 = (bf16[576,128]{1,0:T(8,128)(2,1)}, bf16[576,128]{1,0:T(8,128)(2,1)S(1)}, u32[]{:S(2)}, u32[]{:S(2)}) collective-permute-start(bf16[576,128]{1,0:T(8,128)(2,1)} %bitcast.23), channel_id=1, source_target_pairs={{0,0},{1,1},{2,33},{3,32},{4,4},{5,5},{6,37},{7,36},{8,8},{9,9},{1... | collective-permute-start | bytes 442376 | tf_op jit(solution)/shard_map/ppermute | solution.py:57
  22.9 3.0 %collective-permute-start.9 = (bf16[576,128]{1,0:T(8,128)(2,1)S(1)}, bf16[576,128]{1,0:T(8,128)(2,1)S(1)}, u32[]{:S(2)}, u32[]{:S(2)}) collective-permute-start(bf16[576,128]{1,0:T(8,128)(2,1)S(1)} %collective-permute-done.8.refs_5_), channel_id=1, source_target_pairs={{0,28},{4,0},{8,4},{12,8},{16,12},{20,16},{24,20},{28,24},{1,29},{... | collective-permute-start | bytes 442376 | tf_op jit(solution)/shard_map/ppermute | solution.py:69
  25.9 1.8 collective-permute-done.2.refs_0_
  28.0 4.7 %collective-permute-done.6.refs_1_ = bf16[576,128]{1,0:T(8,128)(2,1)S(1)} collective-permute-done((bf16[576,128]{1,0:T(8,128)(2,1)S(1)}, bf16[576,128]{1,0:T(8,128)(2,1)S(1)}, u32[]{:S(2)}, u32[]{:S(2)}) %collective-permute-start.6) | collective-permute-done | bytes 147488 | tf_op jit(solution)/shard_map/ppermute | solution.py:69
  34.7 8.8 %all-to-all-start = ((bf16[32,2,1280]{2,1,0:T(2,128)(2,1)}), bf16[32,2,1280]{2,1,0:T(2,128)(2,1)S(1)}, u32[]{:S(2)}, u32[]{:S(2)}) async-start(bf16[32,2,1280]{2,1,0:T(2,128)(2,1)} %maximum_bitcast_fusion), calls=%async_computation | async-start | bytes 327680 | tf_op jit(solution)/shard_map/all_to_all | solution.py:316
  44.7 8.9 %all-to-all-done = bf16[32,2,1280]{2,1,0:T(2,128)(2,1)S(1)} async-done(((bf16[32,2,1280]{2,1,0:T(2,128)(2,1)}), bf16[32,2,1280]{2,1,0:T(2,128)(2,1)S(1)}, u32[]{:S(2)}, u32[]{:S(2)}) %all-to-all-start) | async-done | bytes 163872 | tf_op jit(solution)/shard_map/all_to_all | solution.py:316
  53.7 1.7 shard_map.85
  55.5 2.8 %collective-permute-start.1 = (bf16[256,1152]{1,0:T(8,128)(2,1)S(1)}, bf16[256,1152]{1,0:T(8,128)(2,1)}, u32[]{:S(2)}, u32[]{:S(2)}) collective-permute-start(bf16[256,1152]{1,0:T(8,128)(2,1)S(1)} %shard_map.85), channel_id=1, source_target_pairs={{0,1},{1,0},{2,33},{3,32},{32,3},{33,2},{34,35},{35,34},{4,5},{5,4... | collective-permute-start | bytes 1769480 | tf_op jit(solution)/shard_map/ppermute | solution.py:46
  58.3 1.9 %collective-permute-start = (bf16[256,1152]{1,0:T(8,128)(2,1)S(1)}, bf16[256,1152]{1,0:T(8,128)(2,1)}, u32[]{:S(2)}, u32[]{:S(2)}) collective-permute-start(bf16[256,1152]{1,0:T(8,128)(2,1)S(1)} %shard_map.85), channel_id=1, source_target_pairs={{0,0},{1,1},{2,32},{3,33},{32,2},{33,3},{34,34},{35,35},{4,4},{5,5... | collective-permute-start | bytes 1769480 | tf_op jit(solution)/shard_map/ppermute | solution.py:46
  60.3 12.2 %collective-permute-done.1.refs_2_.other = bf16[256,1152]{1,0:T(8,128)(2,1)} collective-permute-done((bf16[256,1152]{1,0:T(8,128)(2,1)S(1)}, bf16[256,1152]{1,0:T(8,128)(2,1)}, u32[]{:S(2)}, u32[]{:S(2)}) %collective-permute-start.1) | collective-permute-done | bytes 589856 | tf_op jit(solution)/shard_map/ppermute | solution.py:46
  72.5 1.0 copy-done.7
  73.5 1.3 copy-done.4
  74.8 1.3 copy-done.8
  76.1 7.5 %shard_map.87 = (bf16[1024,1024]{1,0:T(8,128)(2,1)S(1)}, bf16[1024,1024]{1,0:T(8,128)(2,1)S(1)}, bf16[576,2048]{1,0:T(8,128)(2,1)S(1)}, f32[8,512]{1,0:T(8,128)S(1)}) custom-call(s32[4]{0:T(128)S(1)} %pad_add_fusion.refs_0_.scal, bf16[256,1152]{1,0:T(8,128)(2,1)} %collective-permute-done.refs_1_.mine, ...), custom_call_target="tpu_custom_call" | custom-call | flops 2280000000 | bytes 10108944 | tf_op jit(solution)/shard_map/pallas_call | solution.py:89
  83.8 2.8 %collective-permute-done.11.their = f32[8,512]{1,0:T(8,128)S(1)} collective-permute-done((f32[8,512]{1,0:T(8,128)S(1)}, f32[8,512]{1,0:T(8,128)S(1)}, u32[]{:S(2)}, u32[]{:S(2)}) %collective-permute-start.11) | collective-permute-done | bytes 16416 | tf_op jit(solution)/shard_map/ppermute | solution.py:65
  86.6 5.0 %shard_map.88 = (bf16[1024,576]{1,0:T(8,128)(2,1)S(1)}, bf16[8,576,128]{2,1,0:T(8,128)(2,1)}, f32[512,128]{1,0:T(8,128)S(1)}) custom-call(f32[8,512]{1,0:T(8,128)S(1)} %get-tuple-element.23.st, f32[8,512]{1,0:T(8,128)S(1)} %collective-permute-done.11.their, bf16[256,1152]{1,0:T(8,128)(2,1)} %collective-permute-done.refs_1_.mine, ...), custom_call_target="tpu_custom_call" | custom-call | flops 1300000000 | bytes 5931008 | tf_op jit(solution)/shard_map/pallas_call | solution.py:89
  91.6 1.1 copy-done.1
  92.7 3.5 %shard_map.89 = (bf16[256,1152]{1,0:T(8,128)(2,1)S(1)}, bf16[256,1152]{1,0:T(8,128)(2,1)S(1)}) custom-call(f32[512,128]{1,0:T(8,128)S(1)} %get-tuple-element.25.ws, bf16[576,2048]{1,0:T(8,128)(2,1)S(1)} %get-tuple-element.26.kt, bf16[1024,1024]{1,0:T(8,128)(2,1)S(1)} %get-tuple-element.27.e0.ee, bf16[1024,1024]{1,0:T(8,128)(2,1)S(1)} %get-tuple-element.24.ee.e1), custom_call_target="tpu_custom_call" | custom-call | flops 2400000000 | bytes 7995392 | tf_op jit(solution)/shard_map/pallas_call | solution.py:89
  96.2 5.8 %collective-permute-start.12 = (bf16[256,1152]{1,0:T(8,128)(2,1)S(1)}, bf16[256,1152]{1,0:T(8,128)(2,1)S(1)}, u32[]{:S(2)}, u32[]{:S(2)}) collective-permute-start(bf16[256,1152]{1,0:T(8,128)(2,1)S(1)} %get-tuple-element.28), channel_id=1, source_target_pairs={{0,0},{1,1},{2,32},{3,33},{32,2},{33,3},{34,34},{35,35},{4,4},{5,5... | collective-permute-start | bytes 1769480 | tf_op jit(solution)/shard_map/ppermute | solution.py:46
  102.7 8.2 %collective-permute-done.12 = bf16[256,1152]{1,0:T(8,128)(2,1)S(1)} collective-permute-done((bf16[256,1152]{1,0:T(8,128)(2,1)S(1)}, bf16[256,1152]{1,0:T(8,128)(2,1)S(1)}, u32[]{:S(2)}, u32[]{:S(2)}) %collective-permute-start.12) | collective-permute-done | bytes 589856 | tf_op jit(solution)/shard_map/ppermute | solution.py:46
  110.9 5.0 %collective-permute-done.13 = bf16[256,1152]{1,0:T(8,128)(2,1)S(1)} collective-permute-done((bf16[256,1152]{1,0:T(8,128)(2,1)S(1)}, bf16[256,1152]{1,0:T(8,128)(2,1)S(1)}, u32[]{:S(2)}, u32[]{:S(2)}) %collective-permute-start.13) | collective-permute-done | bytes 589856 | tf_op jit(solution)/shard_map/ppermute | solution.py:46
  116.1 2.0 %shard_map.90 = (bf16[64,768]{1,0:T(8,128)(2,1)S(1)}, bf16[256,1024]{1,0:T(8,128)(2,1)S(1)}, bf16[256,1024]{1,0:T(8,128)(2,1)}) custom-call(s32[4]{0:T(128)S(1)} %pad_add_fusion.refs_0_.scal, bf16[256,1152]{1,0:T(8,128)(2,1)S(1)} %add_convert_fusion.qo, bf16[64,1280]{1,0:T(8,128)(2,1)S(1)} %reshape.35.both, bf16[512,1024]{1,0:T(8,128)(2,1)S(1)} %copy-done), custom_call_target="tpu_custom_call" | custom-call | flops 200000000 | bytes 2949136 | tf_op jit(solution)/shard_map/pallas_call | solution.py:89
  119.6 6.0 %all-to-all-start.1 = ((bf16[32,2,768]{2,1,0:T(2,128)(2,1)}), bf16[32,2,768]{2,1,0:T(2,128)(2,1)S(1)}, u32[]{:S(2)}, u32[]{:S(2)}) async-start(bf16[32,2,768]{2,1,0:T(2,128)(2,1)} %reshape.36), calls=%async_computation.1 | async-start | bytes 196608 | tf_op jit(solution)/shard_map/all_to_all | solution.py:409
  125.6 1.3 copy-done.2
  126.9 1.7 shard_map.91.a
  128.6 6.2 %all-to-all-done.1 = bf16[32,2,768]{2,1,0:T(2,128)(2,1)S(1)} async-done(((bf16[32,2,768]{2,1,0:T(2,128)(2,1)}), bf16[32,2,768]{2,1,0:T(2,128)(2,1)S(1)}, u32[]{:S(2)}, u32[]{:S(2)}) %all-to-all-start.1) | async-done | bytes 98336 | tf_op jit(solution)/shard_map/all_to_all | solution.py:409
  135.5 1.6 shard_map.92
  137.7 1.2 add_convert_fusion.8
  138.8 1.3 collective-permute-start.24
  140.1 1.6 collective-permute-start.26
  141.7 1.4 collective-permute-start.25
  143.1 5.5 %collective-permute-start.15 = (bf16[576,128]{1,0:T(8,128)(2,1)S(1)}, bf16[576,128]{1,0:T(8,128)(2,1)S(1)}, u32[]{:S(2)}, u32[]{:S(2)}) collective-permute-start(bf16[576,128]{1,0:T(8,128)(2,1)S(1)} %get-tuple-element.33), channel_id=1, source_target_pairs={{0,0},{1,1},{2,33},{3,32},{4,4},{5,5},{6,37},{7,36},{8,8},{9,9},{1... | collective-permute-start | bytes 442376 | tf_op jit(solution)/shard_map/ppermute | solution.py:57
  148.7 2.3 %collective-permute-start.16 = (bf16[576,128]{1,0:T(8,128)(2,1)S(1)}, bf16[576,128]{1,0:T(8,128)(2,1)S(1)}, u32[]{:S(2)}, u32[]{:S(2)}) collective-permute-start(bf16[576,128]{1,0:T(8,128)(2,1)S(1)} %get-tuple-element.36), channel_id=1, source_target_pairs={{0,28},{4,0},{8,4},{12,8},{16,12},{20,16},{24,20},{28,24},{1,29},{... | collective-permute-start | bytes 442376 | tf_op jit(solution)/shard_map/ppermute | solution.py:69
  151.1 2.1 %collective-permute-done.16 = bf16[576,128]{1,0:T(8,128)(2,1)S(1)} collective-permute-done((bf16[576,128]{1,0:T(8,128)(2,1)S(1)}, bf16[576,128]{1,0:T(8,128)(2,1)S(1)}, u32[]{:S(2)}, u32[]{:S(2)}) %collective-permute-start.16) | collective-permute-done | bytes 147488 | tf_op jit(solution)/shard_map/ppermute | solution.py:69
  153.2 6.2 %collective-permute-done.20 = bf16[576,128]{1,0:T(8,128)(2,1)S(1)} collective-permute-done((bf16[576,128]{1,0:T(8,128)(2,1)S(1)}, bf16[576,128]{1,0:T(8,128)(2,1)S(1)}, u32[]{:S(2)}, u32[]{:S(2)}) %collective-permute-start.20) | collective-permute-done | bytes 147488 | tf_op jit(solution)/shard_map/ppermute | solution.py:69
  159.4 1.7 collective-permute-start.17
  161.2 3.9 %collective-permute-done.17 = bf16[576,128]{1,0:T(8,128)(2,1)S(1)} collective-permute-done((bf16[576,128]{1,0:T(8,128)(2,1)S(1)}, bf16[576,128]{1,0:T(8,128)(2,1)S(1)}, u32[]{:S(2)}, u32[]{:S(2)}) %collective-permute-start.17) | collective-permute-done | bytes 147488 | tf_op jit(solution)/shard_map/ppermute | solution.py:69
  165.1 5.9 %collective-permute-done.21 = bf16[576,128]{1,0:T(8,128)(2,1)S(1)} collective-permute-done((bf16[576,128]{1,0:T(8,128)(2,1)S(1)}, bf16[576,128]{1,0:T(8,128)(2,1)S(1)}, u32[]{:S(2)}, u32[]{:S(2)}) %collective-permute-start.21) | collective-permute-done | bytes 147488 | tf_op jit(solution)/shard_map/ppermute | solution.py:69
  171.1 2.7 %collective-permute-start.18 = (bf16[576,128]{1,0:T(8,128)(2,1)S(1)}, bf16[576,128]{1,0:T(8,128)(2,1)S(1)}, u32[]{:S(2)}, u32[]{:S(2)}) collective-permute-start(bf16[576,128]{1,0:T(8,128)(2,1)S(1)} %add_convert_fusion.4), channel_id=1, source_target_pairs={{0,28},{1,29},{2,61},{3,60},{4,0},{5,1},{6,33},{7,32},{8,4},{9,5},... | collective-permute-start | bytes 442376 | tf_op jit(solution)/shard_map/ppermute | solution.py:57
  173.8 1.2 collective-permute-start.22
  175.1 1.7 convert_add_fusion
  176.8 1.0 collective-permute-done.18
  177.7 4.0 %collective-permute-done.22 = bf16[576,128]{1,0:T(8,128)(2,1)S(1)} collective-permute-done((bf16[576,128]{1,0:T(8,128)(2,1)S(1)}, bf16[576,128]{1,0:T(8,128)(2,1)S(1)}, u32[]{:S(2)}, u32[]{:S(2)}) %collective-permute-start.22) | collective-permute-done | bytes 147488 | tf_op jit(solution)/shard_map/ppermute | solution.py:57
  (54 shorter events, 7.2 us)
Async XLA Ops:
  0.6 33.2 %copy-start.9 = (bf16[1,2,24576]{2,1,0:T(2,128)(2,1)S(1)}, bf16[1,2,24576]{2,1,0:T(2,128)(2,1)}, u32[]{:S(2)}) copy-start(bf16[1,2,24576]{2,1,0:T(2,128)(2,1)} %param.6) | copy-start | bytes 294916
  0.6 33.2 %copy-start.10 = (bf16[1,2,16384]{2,1,0:T(2,128)(2,1)S(1)}, bf16[1,2,16384]{2,1,0:T(2,128)(2,1)}, u32[]{:S(2)}) copy-start(bf16[1,2,16384]{2,1,0:T(2,128)(2,1)} %param.7) | copy-start | bytes 196612
  0.7 14.0 %collective-permute-start.3 = (bf16[576,128]{1,0:T(8,128)(2,1)}, bf16[576,128]{1,0:T(8,128)(2,1)S(1)}, u32[]{:S(2)}, u32[]{:S(2)}) collective-permute-start(bf16[576,128]{1,0:T(8,128)(2,1)} %bitcast.21), channel_id=1, source_target_pairs={{0,4},{1,5},{2,37},{3,36},{4,8},{5,9},{6,41},{7,40},{8,12},{9,13},... | collective-permute-start | bytes 442376 | tf_op jit(solution)/shard_map/ppermute | solution.py:57
  6.2 8.5 %collective-permute-start.7 = (bf16[576,128]{1,0:T(8,128)(2,1)}, bf16[576,128]{1,0:T(8,128)(2,1)S(1)}, u32[]{:S(2)}, u32[]{:S(2)}) collective-permute-start(bf16[576,128]{1,0:T(8,128)(2,1)} %bitcast.22), channel_id=1, source_target_pairs={{0,28},{1,29},{2,61},{3,60},{4,0},{5,1},{6,33},{7,32},{8,4},{9,5},... | collective-permute-start | bytes 442376 | tf_op jit(solution)/shard_map/ppermute | solution.py:57
  14.7 5.2 %collective-permute-start.4 = (bf16[576,128]{1,0:T(8,128)(2,1)S(1)}, bf16[576,128]{1,0:T(8,128)(2,1)S(1)}, u32[]{:S(2)}, u32[]{:S(2)}) collective-permute-start(bf16[576,128]{1,0:T(8,128)(2,1)S(1)} %collective-permute-done.3.refs_6_), channel_id=1, source_target_pairs={{0,4},{4,8},{8,12},{12,16},{16,20},{20,24},{24,28},{28,0},{1,5},{5... | collective-permute-start | bytes 442376 | tf_op jit(solution)/shard_map/ppermute | solution.py:69
  14.7 8.2 %collective-permute-start.8 = (bf16[576,128]{1,0:T(8,128)(2,1)S(1)}, bf16[576,128]{1,0:T(8,128)(2,1)S(1)}, u32[]{:S(2)}, u32[]{:S(2)}) collective-permute-start(bf16[576,128]{1,0:T(8,128)(2,1)S(1)} %collective-permute-done.7.refs_7_), channel_id=1, source_target_pairs={{0,28},{4,0},{8,4},{12,8},{16,12},{20,16},{24,20},{28,24},{1,29},{... | collective-permute-start | bytes 442376 | tf_op jit(solution)/shard_map/ppermute | solution.py:69
  19.9 6.1 %collective-permute-start.5 = (bf16[576,128]{1,0:T(8,128)(2,1)S(1)}, bf16[576,128]{1,0:T(8,128)(2,1)S(1)}, u32[]{:S(2)}, u32[]{:S(2)}) collective-permute-start(bf16[576,128]{1,0:T(8,128)(2,1)S(1)} %collective-permute-done.4.refs_4_), channel_id=1, source_target_pairs={{0,4},{4,8},{8,12},{12,16},{16,20},{20,24},{24,28},{28,0},{1,5},{5... | collective-permute-start | bytes 442376 | tf_op jit(solution)/shard_map/ppermute | solution.py:69
  19.9 7.9 %collective-permute-start.2 = (bf16[576,128]{1,0:T(8,128)(2,1)}, bf16[576,128]{1,0:T(8,128)(2,1)S(1)}, u32[]{:S(2)}, u32[]{:S(2)}) collective-permute-start(bf16[576,128]{1,0:T(8,128)(2,1)} %bitcast.23), channel_id=1, source_target_pairs={{0,0},{1,1},{2,33},{3,32},{4,4},{5,5},{6,37},{7,36},{8,8},{9,9},{1... | collective-permute-start | bytes 442376 | tf_op jit(solution)/shard_map/ppermute | solution.py:57
  22.9 5.1 %collective-permute-start.9 = (bf16[576,128]{1,0:T(8,128)(2,1)S(1)}, bf16[576,128]{1,0:T(8,128)(2,1)S(1)}, u32[]{:S(2)}, u32[]{:S(2)}) collective-permute-start(bf16[576,128]{1,0:T(8,128)(2,1)S(1)} %collective-permute-done.8.refs_5_), channel_id=1, source_target_pairs={{0,28},{4,0},{8,4},{12,8},{16,12},{20,16},{24,20},{28,24},{1,29},{... | collective-permute-start | bytes 442376 | tf_op jit(solution)/shard_map/ppermute | solution.py:69
  25.9 6.8 %collective-permute-start.6 = (bf16[576,128]{1,0:T(8,128)(2,1)S(1)}, bf16[576,128]{1,0:T(8,128)(2,1)S(1)}, u32[]{:S(2)}, u32[]{:S(2)}) collective-permute-start(bf16[576,128]{1,0:T(8,128)(2,1)S(1)} %collective-permute-done.5.refs_2_), channel_id=1, source_target_pairs={{0,4},{4,8},{8,12},{12,16},{16,20},{20,24},{24,28},{28,0},{1,5},{5... | collective-permute-start | bytes 442376 | tf_op jit(solution)/shard_map/ppermute | solution.py:69
  33.1 22.3 %copy-start.3 = (bf16[576,1024]{1,0:T(8,128)(2,1)}, bf16[576,1024]{1,0:T(8,128)(2,1)S(1)}, u32[]{:S(2)}) copy-start(bf16[576,1024]{1,0:T(8,128)(2,1)S(1)} %shard_map.86.refs_3_) | copy-start | bytes 3538948
  33.1 39.4 %collective-permute-start.10 = (bf16[576,1024]{1,0:T(8,128)(2,1)S(1)}, bf16[576,1024]{1,0:T(8,128)(2,1)S(1)}, u32[]{:S(2)}, u32[]{:S(2)}) collective-permute-start(bf16[576,1024]{1,0:T(8,128)(2,1)S(1)} %shard_map.86.refs_3_), channel_id=1, source_target_pairs={{0,32},{32,0},{1,33},{33,1},{2,34},{34,2},{3,35},{35,3},{4,36},{36... | collective-permute-start | bytes 3538952 | tf_op jit(solution)/shard_map/ppermute | solution.py:61
  34.7 19.0 %all-to-all-start = ((bf16[32,2,1280]{2,1,0:T(2,128)(2,1)}), bf16[32,2,1280]{2,1,0:T(2,128)(2,1)S(1)}, u32[]{:S(2)}, u32[]{:S(2)}) async-start(bf16[32,2,1280]{2,1,0:T(2,128)(2,1)} %maximum_bitcast_fusion), calls=%async_computation | async-start | bytes 327680 | tf_op jit(solution)/shard_map/all_to_all | solution.py:316
  55.5 17.0 %collective-permute-start.1 = (bf16[256,1152]{1,0:T(8,128)(2,1)S(1)}, bf16[256,1152]{1,0:T(8,128)(2,1)}, u32[]{:S(2)}, u32[]{:S(2)}) collective-permute-start(bf16[256,1152]{1,0:T(8,128)(2,1)S(1)} %shard_map.85), channel_id=1, source_target_pairs={{0,1},{1,0},{2,33},{3,32},{32,3},{33,2},{34,35},{35,34},{4,5},{5,4... | collective-permute-start | bytes 1769480 | tf_op jit(solution)/shard_map/ppermute | solution.py:46
  58.3 14.2 %collective-permute-start = (bf16[256,1152]{1,0:T(8,128)(2,1)S(1)}, bf16[256,1152]{1,0:T(8,128)(2,1)}, u32[]{:S(2)}, u32[]{:S(2)}) collective-permute-start(bf16[256,1152]{1,0:T(8,128)(2,1)S(1)} %shard_map.85), channel_id=1, source_target_pairs={{0,0},{1,1},{2,32},{3,33},{32,2},{33,3},{34,34},{35,35},{4,4},{5,5... | collective-permute-start | bytes 1769480 | tf_op jit(solution)/shard_map/ppermute | solution.py:46
  72.5 1.0 copy-start.7
  73.5 1.3 copy-start.4
  74.8 1.3 copy-start.8
  83.5 3.0 %collective-permute-start.11 = (f32[8,512]{1,0:T(8,128)S(1)}, f32[8,512]{1,0:T(8,128)S(1)}, u32[]{:S(2)}, u32[]{:S(2)}) collective-permute-start(f32[8,512]{1,0:T(8,128)S(1)} %get-tuple-element.23.st), channel_id=1, source_target_pairs={{0,1},{1,0},{2,3},{3,2},{4,5},{5,4},{6,7},{7,6},{8,9},{9,8},{10,11... | collective-permute-start | bytes 49160 | tf_op jit(solution)/shard_map/ppermute | solution.py:65
  91.6 1.1 copy-start.1
  96.2 19.9 %copy-start = (bf16[512,1024]{1,0:T(8,128)(2,1)S(1)}, bf16[512,1024]{1,0:T(8,128)(2,1)}, u32[]{:S(2)}) copy-start(bf16[512,1024]{1,0:T(8,128)(2,1)} %w.3) | copy-start | bytes 3145732
  96.2 14.7 %collective-permute-start.12 = (bf16[256,1152]{1,0:T(8,128)(2,1)S(1)}, bf16[256,1152]{1,0:T(8,128)(2,1)S(1)}, u32[]{:S(2)}, u32[]{:S(2)}) collective-permute-start(bf16[256,1152]{1,0:T(8,128)(2,1)S(1)} %get-tuple-element.28), channel_id=1, source_target_pairs={{0,0},{1,1},{2,32},{3,33},{32,2},{33,3},{34,34},{35,35},{4,4},{5,5... | collective-permute-start | bytes 1769480 | tf_op jit(solution)/shard_map/ppermute | solution.py:46
  102.1 13.9 %collective-permute-start.13 = (bf16[256,1152]{1,0:T(8,128)(2,1)S(1)}, bf16[256,1152]{1,0:T(8,128)(2,1)S(1)}, u32[]{:S(2)}, u32[]{:S(2)}) collective-permute-start(bf16[256,1152]{1,0:T(8,128)(2,1)S(1)} %get-tuple-element.29), channel_id=1, source_target_pairs={{0,1},{1,0},{2,33},{3,32},{32,3},{33,2},{34,35},{35,34},{4,5},{5,4... | collective-permute-start | bytes 1769480 | tf_op jit(solution)/shard_map/ppermute | solution.py:46
  102.7 32.8 %collective-permute-start.14 = (bf16[8,576,128]{2,1,0:T(8,128)(2,1)}, bf16[8,576,128]{2,1,0:T(8,128)(2,1)}, u32[]{:S(2)}, u32[]{:S(2)}) collective-permute-start(bf16[8,576,128]{2,1,0:T(8,128)(2,1)} %get-tuple-element.32), channel_id=1, source_target_pairs={{0,32},{32,0},{1,33},{33,1},{2,34},{34,2},{3,35},{35,3},{4,36},{36... | collective-permute-start | bytes 3538952 | tf_op jit(solution)/shard_map/ppermute | solution.py:61
  118.0 0.8 copy-start.5
  118.9 18.8 %collective-permute-start.23 = (bf16[256,1024]{1,0:T(8,128)(2,1)}, bf16[256,1024]{1,0:T(8,128)(2,1)}, u32[]{:S(2)}, u32[]{:S(2)}) collective-permute-start(bf16[256,1024]{1,0:T(8,128)(2,1)} %get-tuple-element.42), channel_id=1, source_target_pairs={{0,32},{32,0},{1,33},{33,1},{2,34},{34,2},{3,35},{35,3},{4,36},{36... | collective-permute-start | bytes 1572872 | tf_op jit(solution)/shard_map/ppermute | solution.py:61
  119.6 15.2 %all-to-all-start.1 = ((bf16[32,2,768]{2,1,0:T(2,128)(2,1)}), bf16[32,2,768]{2,1,0:T(2,128)(2,1)S(1)}, u32[]{:S(2)}, u32[]{:S(2)}) async-start(bf16[32,2,768]{2,1,0:T(2,128)(2,1)} %reshape.36), calls=%async_computation.1 | async-start | bytes 196608 | tf_op jit(solution)/shard_map/all_to_all | solution.py:409
  125.5 1.3 copy-start.2
  135.5 2.2 %copy-start.6 = (bf16[256,1024]{1,0:T(8,128)(2,1)S(1)}, bf16[256,1024]{1,0:T(8,128)(2,1)}, u32[]{:S(2)}) copy-start(bf16[256,1024]{1,0:T(8,128)(2,1)} %copy-done.5) | copy-start | bytes 1572868
  137.1 11.6 %collective-permute-start.19 = (bf16[576,128]{1,0:T(8,128)(2,1)S(1)}, bf16[576,128]{1,0:T(8,128)(2,1)S(1)}, u32[]{:S(2)}, u32[]{:S(2)}) collective-permute-start(bf16[576,128]{1,0:T(8,128)(2,1)S(1)} %get-tuple-element.40), channel_id=1, source_target_pairs={{0,4},{4,8},{8,12},{12,16},{16,20},{20,24},{24,28},{28,0},{1,5},{5... | collective-permute-start | bytes 442376 | tf_op jit(solution)/shard_map/ppermute | solution.py:69
  138.8 35.0 %collective-permute-start.24 = (bf16[64,1024]{1,0:T(8,128)(2,1)S(1)}, bf16[64,1024]{1,0:T(8,128)(2,1)S(1)}, u32[]{:S(2)}, u32[]{:S(2)}) collective-permute-start(bf16[64,1024]{1,0:T(8,128)(2,1)S(1)} %get-tuple-element.43), channel_id=1, source_target_pairs={{0,64},{64,128},{128,192},{192,0},{1,65},{65,129},{129,193},{193,1... | collective-permute-start | bytes 393224 | tf_op jit(solution)/shard_map/ppermute | solution.py:407
  140.1 34.9 %collective-permute-start.26 = (bf16[64,1024]{1,0:T(8,128)(2,1)S(1)}, bf16[64,1024]{1,0:T(8,128)(2,1)S(1)}, u32[]{:S(2)}, u32[]{:S(2)}) collective-permute-start(bf16[64,1024]{1,0:T(8,128)(2,1)S(1)} %get-tuple-element.44), channel_id=1, source_target_pairs={{0,192},{64,0},{128,64},{192,128},{1,193},{65,1},{129,65},{193,129... | collective-permute-start | bytes 393224 | tf_op jit(solution)/shard_map/ppermute | solution.py:407
  141.7 33.3 %collective-permute-start.25 = (bf16[64,1024]{1,0:T(8,128)(2,1)S(1)}, bf16[64,1024]{1,0:T(8,128)(2,1)S(1)}, u32[]{:S(2)}, u32[]{:S(2)}) collective-permute-start(bf16[64,1024]{1,0:T(8,128)(2,1)S(1)} %get-tuple-element.45), channel_id=1, source_target_pairs={{0,128},{64,192},{128,0},{192,64},{1,129},{65,193},{129,1},{193,65... | collective-permute-start | bytes 393224 | tf_op jit(solution)/shard_map/ppermute | solution.py:407
  143.1 33.6 %collective-permute-start.15 = (bf16[576,128]{1,0:T(8,128)(2,1)S(1)}, bf16[576,128]{1,0:T(8,128)(2,1)S(1)}, u32[]{:S(2)}, u32[]{:S(2)}) collective-permute-start(bf16[576,128]{1,0:T(8,128)(2,1)S(1)} %get-tuple-element.33), channel_id=1, source_target_pairs={{0,0},{1,1},{2,33},{3,32},{4,4},{5,5},{6,37},{7,36},{8,8},{9,9},{1... | collective-permute-start | bytes 442376 | tf_op jit(solution)/shard_map/ppermute | solution.py:57
  148.7 4.4 %collective-permute-start.16 = (bf16[576,128]{1,0:T(8,128)(2,1)S(1)}, bf16[576,128]{1,0:T(8,128)(2,1)S(1)}, u32[]{:S(2)}, u32[]{:S(2)}) collective-permute-start(bf16[576,128]{1,0:T(8,128)(2,1)S(1)} %get-tuple-element.36), channel_id=1, source_target_pairs={{0,28},{4,0},{8,4},{12,8},{16,12},{20,16},{24,20},{28,24},{1,29},{... | collective-permute-start | bytes 442376 | tf_op jit(solution)/shard_map/ppermute | solution.py:69
  153.1 6.3 %collective-permute-start.20 = (bf16[576,128]{1,0:T(8,128)(2,1)S(1)}, bf16[576,128]{1,0:T(8,128)(2,1)S(1)}, u32[]{:S(2)}, u32[]{:S(2)}) collective-permute-start(bf16[576,128]{1,0:T(8,128)(2,1)S(1)} %add_convert_fusion.3), channel_id=1, source_target_pairs={{0,4},{4,8},{8,12},{12,16},{16,20},{20,24},{24,28},{28,0},{1,5},{5... | collective-permute-start | bytes 442376 | tf_op jit(solution)/shard_map/ppermute | solution.py:69
  159.4 5.6 %collective-permute-start.17 = (bf16[576,128]{1,0:T(8,128)(2,1)S(1)}, bf16[576,128]{1,0:T(8,128)(2,1)S(1)}, u32[]{:S(2)}, u32[]{:S(2)}) collective-permute-start(bf16[576,128]{1,0:T(8,128)(2,1)S(1)} %add_convert_fusion.5), channel_id=1, source_target_pairs={{0,28},{4,0},{8,4},{12,8},{16,12},{20,16},{24,20},{28,24},{1,29},{... | collective-permute-start | bytes 442376 | tf_op jit(solution)/shard_map/ppermute | solution.py:69
  165.1 6.0 %collective-permute-start.21 = (bf16[576,128]{1,0:T(8,128)(2,1)S(1)}, bf16[576,128]{1,0:T(8,128)(2,1)S(1)}, u32[]{:S(2)}, u32[]{:S(2)}) collective-permute-start(bf16[576,128]{1,0:T(8,128)(2,1)S(1)} %add_convert_fusion.2), channel_id=1, source_target_pairs={{0,4},{4,8},{8,12},{12,16},{16,20},{20,24},{24,28},{28,0},{1,5},{5... | collective-permute-start | bytes 442376 | tf_op jit(solution)/shard_map/ppermute | solution.py:69
  171.1 6.7 %collective-permute-start.18 = (bf16[576,128]{1,0:T(8,128)(2,1)S(1)}, bf16[576,128]{1,0:T(8,128)(2,1)S(1)}, u32[]{:S(2)}, u32[]{:S(2)}) collective-permute-start(bf16[576,128]{1,0:T(8,128)(2,1)S(1)} %add_convert_fusion.4), channel_id=1, source_target_pairs={{0,28},{1,29},{2,61},{3,60},{4,0},{5,1},{6,33},{7,32},{8,4},{9,5},... | collective-permute-start | bytes 442376 | tf_op jit(solution)/shard_map/ppermute | solution.py:57
  173.8 8.0 %collective-permute-start.22 = (bf16[576,128]{1,0:T(8,128)(2,1)S(1)}, bf16[576,128]{1,0:T(8,128)(2,1)S(1)}, u32[]{:S(2)}, u32[]{:S(2)}) collective-permute-start(bf16[576,128]{1,0:T(8,128)(2,1)S(1)} %add_convert_fusion.1), channel_id=1, source_target_pairs={{0,4},{1,5},{2,37},{3,36},{4,8},{5,9},{6,41},{7,40},{8,12},{9,13},... | collective-permute-start | bytes 442376 | tf_op jit(solution)/shard_map/ppermute | solution.py:57

commit v7 on v6

--- a/solution.py
+++ b/solution.py
@@ -273,7 +273,7 @@
         out[:, C + W :] = jnp.zeros((ROWS, DR), out.dtype)
 
 
-def tail_body(scal, qo, both, w, gq, keep, send, terms):
+def tail_body(scal, qo, both, w, rows_out, keep, send, terms, gq):
     for h in range(HEADS):
         rows = slice(h * NQ, (h + 1) * NQ)
         o = qo[rows, :C]
@@ -287,6 +287,8 @@
         q0 = h * (DN + DR)
         gq[:, q0 : q0 + DN] = dot(lat, w[:, c0 : c0 + DN]).astype(BF)
         gq[:, q0 + DN : q0 + DN + DR] = qo[rows, 2 * C : C + W]
+    for d in range(NZ * NY):
+        rows_out[d] = gq[2 * d : 2 * d + 2, :]
     x, c = scal[2], scal[3]
     n = C // 8
     for k in range(4):
@@ -391,10 +393,10 @@
     wide = HEADS * (DN + DV)
     gq, keep, send = call(
         tail_body,
-        [vmem((NQ, HEADS * (DN + DR)), BF)] + [vmem((C // 2, wide), BF)] * 2,
+        [vmem((ndev, own_q, HEADS * (DN + DR)), BF)] + [vmem((C // 2, wide), BF)] * 2,
         (scal, qo, both, latent_up),
         200_000_000,
-        (pltpu.VMEM((C, wide), BF),),
+        (pltpu.VMEM((C, wide), BF), pltpu.VMEM((NQ, HEADS * (DN + DR)), BF)),
         smem=1,
         mib=12,
     )
@@ -406,7 +408,7 @@
         pair = (keep[rows].astype(F32) + got[rows].astype(F32)).astype(BF)
         pair = lax.ppermute(pair, "x", [(i, (i + k) % 4) for i in range(4)])
         grad_weights = grad_weights + pair.astype(F32)
-    back = lax.all_to_all(gq.reshape(ndev, own_q, HEADS * (DN + DR)), CTX, 0, 0, tiled=True)
+    back = lax.all_to_all(gq, CTX, 0, 0, tiled=True)
     grad_queries = jnp.moveaxis(back, 0, 1).reshape(1, own_q, -1).astype(F32)
     return (grad_queries, key_grad[None], grad_weights)
 

time: 183 us -> 182 us (level)
  no operation moved by 1% of the time
where the time goes in v7:
time: 182 us
  waiting for transfers between devices  80.2 us (44%)
  starting transfers between devices  63.7 us (35%)
  Pallas kernels  23.3 us (13%)
  local copies, waits for them, and re-layouts  6.9 us (4%)
  other arithmetic  5.6 us (3%)
  between operations  2.18 us (1%)
    ppermute x10, waiting for transfers between devices, along_z(): return lax.ppermute(v, 'z', [(i, (i + step) % NZ) for i in range(NZ)])  25.7 us
    ppermute x4, waiting for transfers between devices, turn(): return lax.ppermute(v, ('core', 'y'), turned(flip))  25.4 us
    pallas_call x8, Pallas kernels, call(): pl.pallas_call(body, out_shape=out_shape, in_specs=specs, out_specs=[pl.B...  23.3 us
    ppermute x6, starting transfers between devices, homeward(): return lax.ppermute(v, ('core', 'z', 'y'), pairs)  22.1 us
    ppermute x6, waiting for transfers between devices, homeward(): return lax.ppermute(v, ('core', 'z', 'y'), pairs)  11.3 us
    ppermute x4, starting transfers between devices, turn(): return lax.ppermute(v, ('core', 'y'), turned(flip))  11.2 us
    ppermute x10, starting transfers between devices, along_z(): return lax.ppermute(v, 'z', [(i, (i + step) % NZ) for i in range(NZ)])  10.3 us
    all_to_all x1, waiting for transfers between devices, step(): both = lax.all_to_all(both, CTX, 0, 0, tiled=True)  8.94 us
  transfers between devices with their start and end apart: 29, of which 17 were waited for; matrix products, arithmetic and copies ran while one was open for 3% of the time, Pallas kernels for 4%

profile of v7, /device:TPU:1, one launch (start us, length us, event | category | flops | bytes accessed | tf_op | source)
XLA Modules:
  0.0 181.9 jit_solution(12844402954315420959)
XLA Ops:
  0.7 5.5 %collective-permute-start.3 = (bf16[576,128]{1,0:T(8,128)(2,1)}, bf16[576,128]{1,0:T(8,128)(2,1)S(1)}, u32[]{:S(2)}, u32[]{:S(2)}) collective-permute-start(bf16[576,128]{1,0:T(8,128)(2,1)} %bitcast.21), channel_id=1, source_target_pairs={{0,4},{1,5},{2,37},{3,36},{4,8},{5,9},{6,41},{7,40},{8,12},{9,13},... | collective-permute-start | bytes 442376 | tf_op jit(solution)/shard_map/ppermute | solution.py:57
  6.2 4.0 %collective-permute-start.7 = (bf16[576,128]{1,0:T(8,128)(2,1)}, bf16[576,128]{1,0:T(8,128)(2,1)S(1)}, u32[]{:S(2)}, u32[]{:S(2)}) collective-permute-start(bf16[576,128]{1,0:T(8,128)(2,1)} %bitcast.22), channel_id=1, source_target_pairs={{0,28},{1,29},{2,61},{3,60},{4,0},{5,1},{6,33},{7,32},{8,4},{9,5},... | collective-permute-start | bytes 442376 | tf_op jit(solution)/shard_map/ppermute | solution.py:57
  10.2 4.4 %collective-permute-done.3.refs_6_ = bf16[576,128]{1,0:T(8,128)(2,1)S(1)} collective-permute-done((bf16[576,128]{1,0:T(8,128)(2,1)}, bf16[576,128]{1,0:T(8,128)(2,1)S(1)}, u32[]{:S(2)}, u32[]{:S(2)}) %collective-permute-start.3) | collective-permute-done | bytes 147488 | tf_op jit(solution)/shard_map/ppermute | solution.py:57
  14.7 2.7 %collective-permute-start.8 = (bf16[576,128]{1,0:T(8,128)(2,1)S(1)}, bf16[576,128]{1,0:T(8,128)(2,1)S(1)}, u32[]{:S(2)}, u32[]{:S(2)}) collective-permute-start(bf16[576,128]{1,0:T(8,128)(2,1)S(1)} %collective-permute-done.7.refs_7_), channel_id=1, source_target_pairs={{0,28},{4,0},{8,4},{12,8},{16,12},{20,16},{24,20},{28,24},{1,29},{... | collective-permute-start | bytes 442376 | tf_op jit(solution)/shard_map/ppermute | solution.py:69
  17.3 2.5 %collective-permute-done.4.refs_4_ = bf16[576,128]{1,0:T(8,128)(2,1)S(1)} collective-permute-done((bf16[576,128]{1,0:T(8,128)(2,1)S(1)}, bf16[576,128]{1,0:T(8,128)(2,1)S(1)}, u32[]{:S(2)}, u32[]{:S(2)}) %collective-permute-start.4) | collective-permute-done | bytes 147488 | tf_op jit(solution)/shard_map/ppermute | solution.py:69
  19.9 3.0 %collective-permute-start.2 = (bf16[576,128]{1,0:T(8,128)(2,1)}, bf16[576,128]{1,0:T(8,128)(2,1)S(1)}, u32[]{:S(2)}, u32[]{:S(2)}) collective-permute-start(bf16[576,128]{1,0:T(8,128)(2,1)} %bitcast.23), channel_id=1, source_target_pairs={{0,0},{1,1},{2,33},{3,32},{4,4},{5,5},{6,37},{7,36},{8,8},{9,9},{1... | collective-permute-start | bytes 442376 | tf_op jit(solution)/shard_map/ppermute | solution.py:57
  22.9 3.0 %collective-permute-start.9 = (bf16[576,128]{1,0:T(8,128)(2,1)S(1)}, bf16[576,128]{1,0:T(8,128)(2,1)S(1)}, u32[]{:S(2)}, u32[]{:S(2)}) collective-permute-start(bf16[576,128]{1,0:T(8,128)(2,1)S(1)} %collective-permute-done.8.refs_5_), channel_id=1, source_target_pairs={{0,28},{4,0},{8,4},{12,8},{16,12},{20,16},{24,20},{28,24},{1,29},{... | collective-permute-start | bytes 442376 | tf_op jit(solution)/shard_map/ppermute | solution.py:69
  25.9 1.8 collective-permute-done.2.refs_0_
  28.0 4.7 %collective-permute-done.6.refs_1_ = bf16[576,128]{1,0:T(8,128)(2,1)S(1)} collective-permute-done((bf16[576,128]{1,0:T(8,128)(2,1)S(1)}, bf16[576,128]{1,0:T(8,128)(2,1)S(1)}, u32[]{:S(2)}, u32[]{:S(2)}) %collective-permute-start.6) | collective-permute-done | bytes 147488 | tf_op jit(solution)/shard_map/ppermute | solution.py:69
  34.7 8.8 %all-to-all-start = ((bf16[32,2,1280]{2,1,0:T(2,128)(2,1)}), bf16[32,2,1280]{2,1,0:T(2,128)(2,1)S(1)}, u32[]{:S(2)}, u32[]{:S(2)}) async-start(bf16[32,2,1280]{2,1,0:T(2,128)(2,1)} %maximum_bitcast_fusion), calls=%async_computation | async-start | bytes 327680 | tf_op jit(solution)/shard_map/all_to_all | solution.py:318
  44.7 8.9 %all-to-all-done = bf16[32,2,1280]{2,1,0:T(2,128)(2,1)S(1)} async-done(((bf16[32,2,1280]{2,1,0:T(2,128)(2,1)}), bf16[32,2,1280]{2,1,0:T(2,128)(2,1)S(1)}, u32[]{:S(2)}, u32[]{:S(2)}) %all-to-all-start) | async-done | bytes 163872 | tf_op jit(solution)/shard_map/all_to_all | solution.py:318
  53.7 1.7 shard_map.85
  55.5 2.8 %collective-permute-start.1 = (bf16[256,1152]{1,0:T(8,128)(2,1)S(1)}, bf16[256,1152]{1,0:T(8,128)(2,1)}, u32[]{:S(2)}, u32[]{:S(2)}) collective-permute-start(bf16[256,1152]{1,0:T(8,128)(2,1)S(1)} %shard_map.85), channel_id=1, source_target_pairs={{0,1},{1,0},{2,33},{3,32},{32,3},{33,2},{34,35},{35,34},{4,5},{5,4... | collective-permute-start | bytes 1769480 | tf_op jit(solution)/shard_map/ppermute | solution.py:46
  58.3 1.9 %collective-permute-start = (bf16[256,1152]{1,0:T(8,128)(2,1)S(1)}, bf16[256,1152]{1,0:T(8,128)(2,1)}, u32[]{:S(2)}, u32[]{:S(2)}) collective-permute-start(bf16[256,1152]{1,0:T(8,128)(2,1)S(1)} %shard_map.85), channel_id=1, source_target_pairs={{0,0},{1,1},{2,32},{3,33},{32,2},{33,3},{34,34},{35,35},{4,4},{5,5... | collective-permute-start | bytes 1769480 | tf_op jit(solution)/shard_map/ppermute | solution.py:46
  60.3 12.2 %collective-permute-done.1.refs_2_.other = bf16[256,1152]{1,0:T(8,128)(2,1)} collective-permute-done((bf16[256,1152]{1,0:T(8,128)(2,1)S(1)}, bf16[256,1152]{1,0:T(8,128)(2,1)}, u32[]{:S(2)}, u32[]{:S(2)}) %collective-permute-start.1) | collective-permute-done | bytes 589856 | tf_op jit(solution)/shard_map/ppermute | solution.py:46
  72.5 1.0 copy-done.7
  73.5 1.3 copy-done.4
  74.8 1.3 copy-done.8
  76.1 7.5 %shard_map.87 = (bf16[1024,1024]{1,0:T(8,128)(2,1)S(1)}, bf16[1024,1024]{1,0:T(8,128)(2,1)S(1)}, bf16[576,2048]{1,0:T(8,128)(2,1)S(1)}, f32[8,512]{1,0:T(8,128)S(1)}) custom-call(s32[4]{0:T(128)S(1)} %pad_add_fusion.refs_0_.scal, bf16[256,1152]{1,0:T(8,128)(2,1)} %collective-permute-done.refs_1_.mine, ...), custom_call_target="tpu_custom_call" | custom-call | flops 2280000000 | bytes 10108944 | tf_op jit(solution)/shard_map/pallas_call | solution.py:89
  83.8 2.8 %collective-permute-done.11.their = f32[8,512]{1,0:T(8,128)S(1)} collective-permute-done((f32[8,512]{1,0:T(8,128)S(1)}, f32[8,512]{1,0:T(8,128)S(1)}, u32[]{:S(2)}, u32[]{:S(2)}) %collective-permute-start.11) | collective-permute-done | bytes 16416 | tf_op jit(solution)/shard_map/ppermute | solution.py:65
  86.6 5.0 %shard_map.88 = (bf16[1024,576]{1,0:T(8,128)(2,1)S(1)}, bf16[8,576,128]{2,1,0:T(8,128)(2,1)}, f32[512,128]{1,0:T(8,128)S(1)}) custom-call(f32[8,512]{1,0:T(8,128)S(1)} %get-tuple-element.23.st, f32[8,512]{1,0:T(8,128)S(1)} %collective-permute-done.11.their, bf16[256,1152]{1,0:T(8,128)(2,1)} %collective-permute-done.refs_1_.mine, ...), custom_call_target="tpu_custom_call" | custom-call | flops 1300000000 | bytes 5931008 | tf_op jit(solution)/shard_map/pallas_call | solution.py:89
  91.6 1.1 copy-done.1
  92.7 3.5 %shard_map.89 = (bf16[256,1152]{1,0:T(8,128)(2,1)S(1)}, bf16[256,1152]{1,0:T(8,128)(2,1)S(1)}) custom-call(f32[512,128]{1,0:T(8,128)S(1)} %get-tuple-element.25.ws, bf16[576,2048]{1,0:T(8,128)(2,1)S(1)} %get-tuple-element.26.kt, bf16[1024,1024]{1,0:T(8,128)(2,1)S(1)} %get-tuple-element.27.e0.ee, bf16[1024,1024]{1,0:T(8,128)(2,1)S(1)} %get-tuple-element.24.ee.e1), custom_call_target="tpu_custom_call" | custom-call | flops 2400000000 | bytes 7995392 | tf_op jit(solution)/shard_map/pallas_call | solution.py:89
  96.2 5.8 %collective-permute-start.12 = (bf16[256,1152]{1,0:T(8,128)(2,1)S(1)}, bf16[256,1152]{1,0:T(8,128)(2,1)S(1)}, u32[]{:S(2)}, u32[]{:S(2)}) collective-permute-start(bf16[256,1152]{1,0:T(8,128)(2,1)S(1)} %get-tuple-element.28), channel_id=1, source_target_pairs={{0,0},{1,1},{2,32},{3,33},{32,2},{33,3},{34,34},{35,35},{4,4},{5,5... | collective-permute-start | bytes 1769480 | tf_op jit(solution)/shard_map/ppermute | solution.py:46
  102.7 8.2 %collective-permute-done.12 = bf16[256,1152]{1,0:T(8,128)(2,1)S(1)} collective-permute-done((bf16[256,1152]{1,0:T(8,128)(2,1)S(1)}, bf16[256,1152]{1,0:T(8,128)(2,1)S(1)}, u32[]{:S(2)}, u32[]{:S(2)}) %collective-permute-start.12) | collective-permute-done | bytes 589856 | tf_op jit(solution)/shard_map/ppermute | solution.py:46
  110.9 5.0 %collective-permute-done.13 = bf16[256,1152]{1,0:T(8,128)(2,1)S(1)} collective-permute-done((bf16[256,1152]{1,0:T(8,128)(2,1)S(1)}, bf16[256,1152]{1,0:T(8,128)(2,1)S(1)}, u32[]{:S(2)}, u32[]{:S(2)}) %collective-permute-start.13) | collective-permute-done | bytes 589856 | tf_op jit(solution)/shard_map/ppermute | solution.py:46
  116.1 2.0 %shard_map.90 = (bf16[32,2,768]{2,1,0:T(2,128)(2,1)}, bf16[256,1024]{1,0:T(8,128)(2,1)S(1)}, bf16[256,1024]{1,0:T(8,128)(2,1)}) custom-call(s32[4]{0:T(128)S(1)} %pad_add_fusion.refs_0_.scal, bf16[256,1152]{1,0:T(8,128)(2,1)S(1)} %add_convert_fusion.qo, bf16[64,1280]{1,0:T(8,128)(2,1)S(1)} %reshape.32.both, bf16[512,1024]{1,0:T(8,128)(2,1)S(1)} %copy-done), custom_call_target="tpu_custom_call" | custom-call | flops 200000000 | bytes 2949136 | tf_op jit(solution)/shard_map/pallas_call | solution.py:89
  118.9 6.0 %all-to-all-start.1 = ((bf16[32,2,768]{2,1,0:T(2,128)(2,1)}), bf16[32,2,768]{2,1,0:T(2,128)(2,1)S(1)}, u32[]{:S(2)}, u32[]{:S(2)}) async-start(bf16[32,2,768]{2,1,0:T(2,128)(2,1)} %get-tuple-element.30), calls=%async_computation.1 | async-start | bytes 196608 | tf_op jit(solution)/shard_map/all_to_all | solution.py:411
  124.9 1.3 copy-done.2
  126.2 1.7 shard_map.91.a
  127.9 6.2 %all-to-all-done.1 = bf16[32,2,768]{2,1,0:T(2,128)(2,1)S(1)} async-done(((bf16[32,2,768]{2,1,0:T(2,128)(2,1)}), bf16[32,2,768]{2,1,0:T(2,128)(2,1)S(1)}, u32[]{:S(2)}, u32[]{:S(2)}) %all-to-all-start.1) | async-done | bytes 98336 | tf_op jit(solution)/shard_map/all_to_all | solution.py:411
  134.9 1.6 shard_map.92
  137.0 1.2 add_convert_fusion.8
  138.2 1.3 collective-permute-start.24
  139.5 1.6 collective-permute-start.26
  141.1 1.4 collective-permute-start.25
  142.5 5.5 %collective-permute-start.15 = (bf16[576,128]{1,0:T(8,128)(2,1)S(1)}, bf16[576,128]{1,0:T(8,128)(2,1)S(1)}, u32[]{:S(2)}, u32[]{:S(2)}) collective-permute-start(bf16[576,128]{1,0:T(8,128)(2,1)S(1)} %get-tuple-element.33), channel_id=1, source_target_pairs={{0,0},{1,1},{2,33},{3,32},{4,4},{5,5},{6,37},{7,36},{8,8},{9,9},{1... | collective-permute-start | bytes 442376 | tf_op jit(solution)/shard_map/ppermute | solution.py:57
  148.0 2.3 %collective-permute-start.16 = (bf16[576,128]{1,0:T(8,128)(2,1)S(1)}, bf16[576,128]{1,0:T(8,128)(2,1)S(1)}, u32[]{:S(2)}, u32[]{:S(2)}) collective-permute-start(bf16[576,128]{1,0:T(8,128)(2,1)S(1)} %get-tuple-element.36), channel_id=1, source_target_pairs={{0,28},{4,0},{8,4},{12,8},{16,12},{20,16},{24,20},{28,24},{1,29},{... | collective-permute-start | bytes 442376 | tf_op jit(solution)/shard_map/ppermute | solution.py:69
  150.4 2.1 %collective-permute-done.16 = bf16[576,128]{1,0:T(8,128)(2,1)S(1)} collective-permute-done((bf16[576,128]{1,0:T(8,128)(2,1)S(1)}, bf16[576,128]{1,0:T(8,128)(2,1)S(1)}, u32[]{:S(2)}, u32[]{:S(2)}) %collective-permute-start.16) | collective-permute-done | bytes 147488 | tf_op jit(solution)/shard_map/ppermute | solution.py:69
  152.5 6.2 %collective-permute-done.20 = bf16[576,128]{1,0:T(8,128)(2,1)S(1)} collective-permute-done((bf16[576,128]{1,0:T(8,128)(2,1)S(1)}, bf16[576,128]{1,0:T(8,128)(2,1)S(1)}, u32[]{:S(2)}, u32[]{:S(2)}) %collective-permute-start.20) | collective-permute-done | bytes 147488 | tf_op jit(solution)/shard_map/ppermute | solution.py:69
  158.8 1.7 collective-permute-start.17
  160.6 3.9 %collective-permute-done.17 = bf16[576,128]{1,0:T(8,128)(2,1)S(1)} collective-permute-done((bf16[576,128]{1,0:T(8,128)(2,1)S(1)}, bf16[576,128]{1,0:T(8,128)(2,1)S(1)}, u32[]{:S(2)}, u32[]{:S(2)}) %collective-permute-start.17) | collective-permute-done | bytes 147488 | tf_op jit(solution)/shard_map/ppermute | solution.py:69
  164.5 5.9 %collective-permute-done.21 = bf16[576,128]{1,0:T(8,128)(2,1)S(1)} collective-permute-done((bf16[576,128]{1,0:T(8,128)(2,1)S(1)}, bf16[576,128]{1,0:T(8,128)(2,1)S(1)}, u32[]{:S(2)}, u32[]{:S(2)}) %collective-permute-start.21) | collective-permute-done | bytes 147488 | tf_op jit(solution)/shard_map/ppermute | solution.py:69
  170.4 2.7 %collective-permute-start.18 = (bf16[576,128]{1,0:T(8,128)(2,1)S(1)}, bf16[576,128]{1,0:T(8,128)(2,1)S(1)}, u32[]{:S(2)}, u32[]{:S(2)}) collective-permute-start(bf16[576,128]{1,0:T(8,128)(2,1)S(1)} %add_convert_fusion.4), channel_id=1, source_target_pairs={{0,28},{1,29},{2,61},{3,60},{4,0},{5,1},{6,33},{7,32},{8,4},{9,5},... | collective-permute-start | bytes 442376 | tf_op jit(solution)/shard_map/ppermute | solution.py:57
  173.2 1.2 collective-permute-start.22
  174.4 1.7 convert_add_fusion
  176.1 1.0 collective-permute-done.18
  177.1 4.0 %collective-permute-done.22 = bf16[576,128]{1,0:T(8,128)(2,1)S(1)} collective-permute-done((bf16[576,128]{1,0:T(8,128)(2,1)S(1)}, bf16[576,128]{1,0:T(8,128)(2,1)S(1)}, u32[]{:S(2)}, u32[]{:S(2)}) %collective-permute-start.22) | collective-permute-done | bytes 147488 | tf_op jit(solution)/shard_map/ppermute | solution.py:57
  (53 shorter events, 6.5 us)
Async XLA Ops:
  0.6 33.2 %copy-start.9 = (bf16[1,2,24576]{2,1,0:T(2,128)(2,1)S(1)}, bf16[1,2,24576]{2,1,0:T(2,128)(2,1)}, u32[]{:S(2)}) copy-start(bf16[1,2,24576]{2,1,0:T(2,128)(2,1)} %param.6) | copy-start | bytes 294916
  0.6 33.2 %copy-start.10 = (bf16[1,2,16384]{2,1,0:T(2,128)(2,1)S(1)}, bf16[1,2,16384]{2,1,0:T(2,128)(2,1)}, u32[]{:S(2)}) copy-start(bf16[1,2,16384]{2,1,0:T(2,128)(2,1)} %param.7) | copy-start | bytes 196612
  0.7 14.0 %collective-permute-start.3 = (bf16[576,128]{1,0:T(8,128)(2,1)}, bf16[576,128]{1,0:T(8,128)(2,1)S(1)}, u32[]{:S(2)}, u32[]{:S(2)}) collective-permute-start(bf16[576,128]{1,0:T(8,128)(2,1)} %bitcast.21), channel_id=1, source_target_pairs={{0,4},{1,5},{2,37},{3,36},{4,8},{5,9},{6,41},{7,40},{8,12},{9,13},... | collective-permute-start | bytes 442376 | tf_op jit(solution)/shard_map/ppermute | solution.py:57
  6.2 8.5 %collective-permute-start.7 = (bf16[576,128]{1,0:T(8,128)(2,1)}, bf16[576,128]{1,0:T(8,128)(2,1)S(1)}, u32[]{:S(2)}, u32[]{:S(2)}) collective-permute-start(bf16[576,128]{1,0:T(8,128)(2,1)} %bitcast.22), channel_id=1, source_target_pairs={{0,28},{1,29},{2,61},{3,60},{4,0},{5,1},{6,33},{7,32},{8,4},{9,5},... | collective-permute-start | bytes 442376 | tf_op jit(solution)/shard_map/ppermute | solution.py:57
  14.7 5.2 %collective-permute-start.4 = (bf16[576,128]{1,0:T(8,128)(2,1)S(1)}, bf16[576,128]{1,0:T(8,128)(2,1)S(1)}, u32[]{:S(2)}, u32[]{:S(2)}) collective-permute-start(bf16[576,128]{1,0:T(8,128)(2,1)S(1)} %collective-permute-done.3.refs_6_), channel_id=1, source_target_pairs={{0,4},{4,8},{8,12},{12,16},{16,20},{20,24},{24,28},{28,0},{1,5},{5... | collective-permute-start | bytes 442376 | tf_op jit(solution)/shard_map/ppermute | solution.py:69
  14.7 8.2 %collective-permute-start.8 = (bf16[576,128]{1,0:T(8,128)(2,1)S(1)}, bf16[576,128]{1,0:T(8,128)(2,1)S(1)}, u32[]{:S(2)}, u32[]{:S(2)}) collective-permute-start(bf16[576,128]{1,0:T(8,128)(2,1)S(1)} %collective-permute-done.7.refs_7_), channel_id=1, source_target_pairs={{0,28},{4,0},{8,4},{12,8},{16,12},{20,16},{24,20},{28,24},{1,29},{... | collective-permute-start | bytes 442376 | tf_op jit(solution)/shard_map/ppermute | solution.py:69
  19.9 6.1 %collective-permute-start.5 = (bf16[576,128]{1,0:T(8,128)(2,1)S(1)}, bf16[576,128]{1,0:T(8,128)(2,1)S(1)}, u32[]{:S(2)}, u32[]{:S(2)}) collective-permute-start(bf16[576,128]{1,0:T(8,128)(2,1)S(1)} %collective-permute-done.4.refs_4_), channel_id=1, source_target_pairs={{0,4},{4,8},{8,12},{12,16},{16,20},{20,24},{24,28},{28,0},{1,5},{5... | collective-permute-start | bytes 442376 | tf_op jit(solution)/shard_map/ppermute | solution.py:69
  19.9 7.9 %collective-permute-start.2 = (bf16[576,128]{1,0:T(8,128)(2,1)}, bf16[576,128]{1,0:T(8,128)(2,1)S(1)}, u32[]{:S(2)}, u32[]{:S(2)}) collective-permute-start(bf16[576,128]{1,0:T(8,128)(2,1)} %bitcast.23), channel_id=1, source_target_pairs={{0,0},{1,1},{2,33},{3,32},{4,4},{5,5},{6,37},{7,36},{8,8},{9,9},{1... | collective-permute-start | bytes 442376 | tf_op jit(solution)/shard_map/ppermute | solution.py:57
  22.9 5.1 %collective-permute-start.9 = (bf16[576,128]{1,0:T(8,128)(2,1)S(1)}, bf16[576,128]{1,0:T(8,128)(2,1)S(1)}, u32[]{:S(2)}, u32[]{:S(2)}) collective-permute-start(bf16[576,128]{1,0:T(8,128)(2,1)S(1)} %collective-permute-done.8.refs_5_), channel_id=1, source_target_pairs={{0,28},{4,0},{8,4},{12,8},{16,12},{20,16},{24,20},{28,24},{1,29},{... | collective-permute-start | bytes 442376 | tf_op jit(solution)/shard_map/ppermute | solution.py:69
  25.9 6.8 %collective-permute-start.6 = (bf16[576,128]{1,0:T(8,128)(2,1)S(1)}, bf16[576,128]{1,0:T(8,128)(2,1)S(1)}, u32[]{:S(2)}, u32[]{:S(2)}) collective-permute-start(bf16[576,128]{1,0:T(8,128)(2,1)S(1)} %collective-permute-done.5.refs_2_), channel_id=1, source_target_pairs={{0,4},{4,8},{8,12},{12,16},{16,20},{20,24},{24,28},{28,0},{1,5},{5... | collective-permute-start | bytes 442376 | tf_op jit(solution)/shard_map/ppermute | solution.py:69
  33.1 22.3 %copy-start.3 = (bf16[576,1024]{1,0:T(8,128)(2,1)}, bf16[576,1024]{1,0:T(8,128)(2,1)S(1)}, u32[]{:S(2)}) copy-start(bf16[576,1024]{1,0:T(8,128)(2,1)S(1)} %shard_map.86.refs_3_) | copy-start | bytes 3538948
  33.1 39.4 %collective-permute-start.10 = (bf16[576,1024]{1,0:T(8,128)(2,1)S(1)}, bf16[576,1024]{1,0:T(8,128)(2,1)S(1)}, u32[]{:S(2)}, u32[]{:S(2)}) collective-permute-start(bf16[576,1024]{1,0:T(8,128)(2,1)S(1)} %shard_map.86.refs_3_), channel_id=1, source_target_pairs={{0,32},{32,0},{1,33},{33,1},{2,34},{34,2},{3,35},{35,3},{4,36},{36... | collective-permute-start | bytes 3538952 | tf_op jit(solution)/shard_map/ppermute | solution.py:61
  34.7 19.0 %all-to-all-start = ((bf16[32,2,1280]{2,1,0:T(2,128)(2,1)}), bf16[32,2,1280]{2,1,0:T(2,128)(2,1)S(1)}, u32[]{:S(2)}, u32[]{:S(2)}) async-start(bf16[32,2,1280]{2,1,0:T(2,128)(2,1)} %maximum_bitcast_fusion), calls=%async_computation | async-start | bytes 327680 | tf_op jit(solution)/shard_map/all_to_all | solution.py:318
  55.5 17.0 %collective-permute-start.1 = (bf16[256,1152]{1,0:T(8,128)(2,1)S(1)}, bf16[256,1152]{1,0:T(8,128)(2,1)}, u32[]{:S(2)}, u32[]{:S(2)}) collective-permute-start(bf16[256,1152]{1,0:T(8,128)(2,1)S(1)} %shard_map.85), channel_id=1, source_target_pairs={{0,1},{1,0},{2,33},{3,32},{32,3},{33,2},{34,35},{35,34},{4,5},{5,4... | collective-permute-start | bytes 1769480 | tf_op jit(solution)/shard_map/ppermute | solution.py:46
  58.3 14.2 %collective-permute-start = (bf16[256,1152]{1,0:T(8,128)(2,1)S(1)}, bf16[256,1152]{1,0:T(8,128)(2,1)}, u32[]{:S(2)}, u32[]{:S(2)}) collective-permute-start(bf16[256,1152]{1,0:T(8,128)(2,1)S(1)} %shard_map.85), channel_id=1, source_target_pairs={{0,0},{1,1},{2,32},{3,33},{32,2},{33,3},{34,34},{35,35},{4,4},{5,5... | collective-permute-start | bytes 1769480 | tf_op jit(solution)/shard_map/ppermute | solution.py:46
  72.5 1.0 copy-start.7
  73.5 1.3 copy-start.4
  74.8 1.3 copy-start.8
  83.5 3.0 %collective-permute-start.11 = (f32[8,512]{1,0:T(8,128)S(1)}, f32[8,512]{1,0:T(8,128)S(1)}, u32[]{:S(2)}, u32[]{:S(2)}) collective-permute-start(f32[8,512]{1,0:T(8,128)S(1)} %get-tuple-element.23.st), channel_id=1, source_target_pairs={{0,1},{1,0},{2,3},{3,2},{4,5},{5,4},{6,7},{7,6},{8,9},{9,8},{10,11... | collective-permute-start | bytes 49160 | tf_op jit(solution)/shard_map/ppermute | solution.py:65
  91.6 1.1 copy-start.1
  96.2 19.9 %copy-start = (bf16[512,1024]{1,0:T(8,128)(2,1)S(1)}, bf16[512,1024]{1,0:T(8,128)(2,1)}, u32[]{:S(2)}) copy-start(bf16[512,1024]{1,0:T(8,128)(2,1)} %w.3) | copy-start | bytes 3145732
  96.2 14.7 %collective-permute-start.12 = (bf16[256,1152]{1,0:T(8,128)(2,1)S(1)}, bf16[256,1152]{1,0:T(8,128)(2,1)S(1)}, u32[]{:S(2)}, u32[]{:S(2)}) collective-permute-start(bf16[256,1152]{1,0:T(8,128)(2,1)S(1)} %get-tuple-element.28), channel_id=1, source_target_pairs={{0,0},{1,1},{2,32},{3,33},{32,2},{33,3},{34,34},{35,35},{4,4},{5,5... | collective-permute-start | bytes 1769480 | tf_op jit(solution)/shard_map/ppermute | solution.py:46
  102.1 13.9 %collective-permute-start.13 = (bf16[256,1152]{1,0:T(8,128)(2,1)S(1)}, bf16[256,1152]{1,0:T(8,128)(2,1)S(1)}, u32[]{:S(2)}, u32[]{:S(2)}) collective-permute-start(bf16[256,1152]{1,0:T(8,128)(2,1)S(1)} %get-tuple-element.29), channel_id=1, source_target_pairs={{0,1},{1,0},{2,33},{3,32},{32,3},{33,2},{34,35},{35,34},{4,5},{5,4... | collective-permute-start | bytes 1769480 | tf_op jit(solution)/shard_map/ppermute | solution.py:46
  102.7 32.1 %collective-permute-start.14 = (bf16[8,576,128]{2,1,0:T(8,128)(2,1)}, bf16[8,576,128]{2,1,0:T(8,128)(2,1)}, u32[]{:S(2)}, u32[]{:S(2)}) collective-permute-start(bf16[8,576,128]{2,1,0:T(8,128)(2,1)} %get-tuple-element.32), channel_id=1, source_target_pairs={{0,32},{32,0},{1,33},{33,1},{2,34},{34,2},{3,35},{35,3},{4,36},{36... | collective-permute-start | bytes 3538952 | tf_op jit(solution)/shard_map/ppermute | solution.py:61
  118.1 0.8 copy-start.5
  118.9 18.1 %collective-permute-start.23 = (bf16[256,1024]{1,0:T(8,128)(2,1)}, bf16[256,1024]{1,0:T(8,128)(2,1)}, u32[]{:S(2)}, u32[]{:S(2)}) collective-permute-start(bf16[256,1024]{1,0:T(8,128)(2,1)} %get-tuple-element.42), channel_id=1, source_target_pairs={{0,32},{32,0},{1,33},{33,1},{2,34},{34,2},{3,35},{35,3},{4,36},{36... | collective-permute-start | bytes 1572872 | tf_op jit(solution)/shard_map/ppermute | solution.py:61
  118.9 15.2 %all-to-all-start.1 = ((bf16[32,2,768]{2,1,0:T(2,128)(2,1)}), bf16[32,2,768]{2,1,0:T(2,128)(2,1)S(1)}, u32[]{:S(2)}, u32[]{:S(2)}) async-start(bf16[32,2,768]{2,1,0:T(2,128)(2,1)} %get-tuple-element.30), calls=%async_computation.1 | async-start | bytes 196608 | tf_op jit(solution)/shard_map/all_to_all | solution.py:411
  124.9 1.3 copy-start.2
  134.9 2.2 %copy-start.6 = (bf16[256,1024]{1,0:T(8,128)(2,1)S(1)}, bf16[256,1024]{1,0:T(8,128)(2,1)}, u32[]{:S(2)}) copy-start(bf16[256,1024]{1,0:T(8,128)(2,1)} %copy-done.5) | copy-start | bytes 1572868
  136.5 11.6 %collective-permute-start.19 = (bf16[576,128]{1,0:T(8,128)(2,1)S(1)}, bf16[576,128]{1,0:T(8,128)(2,1)S(1)}, u32[]{:S(2)}, u32[]{:S(2)}) collective-permute-start(bf16[576,128]{1,0:T(8,128)(2,1)S(1)} %get-tuple-element.40), channel_id=1, source_target_pairs={{0,4},{4,8},{8,12},{12,16},{16,20},{20,24},{24,28},{28,0},{1,5},{5... | collective-permute-start | bytes 442376 | tf_op jit(solution)/shard_map/ppermute | solution.py:69
  138.2 35.0 %collective-permute-start.24 = (bf16[64,1024]{1,0:T(8,128)(2,1)S(1)}, bf16[64,1024]{1,0:T(8,128)(2,1)S(1)}, u32[]{:S(2)}, u32[]{:S(2)}) collective-permute-start(bf16[64,1024]{1,0:T(8,128)(2,1)S(1)} %get-tuple-element.43), channel_id=1, source_target_pairs={{0,64},{64,128},{128,192},{192,0},{1,65},{65,129},{129,193},{193,1... | collective-permute-start | bytes 393224 | tf_op jit(solution)/shard_map/ppermute | solution.py:409
  139.5 34.9 %collective-permute-start.26 = (bf16[64,1024]{1,0:T(8,128)(2,1)S(1)}, bf16[64,1024]{1,0:T(8,128)(2,1)S(1)}, u32[]{:S(2)}, u32[]{:S(2)}) collective-permute-start(bf16[64,1024]{1,0:T(8,128)(2,1)S(1)} %get-tuple-element.44), channel_id=1, source_target_pairs={{0,192},{64,0},{128,64},{192,128},{1,193},{65,1},{129,65},{193,129... | collective-permute-start | bytes 393224 | tf_op jit(solution)/shard_map/ppermute | solution.py:409
  141.1 33.3 %collective-permute-start.25 = (bf16[64,1024]{1,0:T(8,128)(2,1)S(1)}, bf16[64,1024]{1,0:T(8,128)(2,1)S(1)}, u32[]{:S(2)}, u32[]{:S(2)}) collective-permute-start(bf16[64,1024]{1,0:T(8,128)(2,1)S(1)} %get-tuple-element.45), channel_id=1, source_target_pairs={{0,128},{64,192},{128,0},{192,64},{1,129},{65,193},{129,1},{193,65... | collective-permute-start | bytes 393224 | tf_op jit(solution)/shard_map/ppermute | solution.py:409
  142.5 33.6 %collective-permute-start.15 = (bf16[576,128]{1,0:T(8,128)(2,1)S(1)}, bf16[576,128]{1,0:T(8,128)(2,1)S(1)}, u32[]{:S(2)}, u32[]{:S(2)}) collective-permute-start(bf16[576,128]{1,0:T(8,128)(2,1)S(1)} %get-tuple-element.33), channel_id=1, source_target_pairs={{0,0},{1,1},{2,33},{3,32},{4,4},{5,5},{6,37},{7,36},{8,8},{9,9},{1... | collective-permute-start | bytes 442376 | tf_op jit(solution)/shard_map/ppermute | solution.py:57
  148.0 4.4 %collective-permute-start.16 = (bf16[576,128]{1,0:T(8,128)(2,1)S(1)}, bf16[576,128]{1,0:T(8,128)(2,1)S(1)}, u32[]{:S(2)}, u32[]{:S(2)}) collective-permute-start(bf16[576,128]{1,0:T(8,128)(2,1)S(1)} %get-tuple-element.36), channel_id=1, source_target_pairs={{0,28},{4,0},{8,4},{12,8},{16,12},{20,16},{24,20},{28,24},{1,29},{... | collective-permute-start | bytes 442376 | tf_op jit(solution)/shard_map/ppermute | solution.py:69
  152.5 6.3 %collective-permute-start.20 = (bf16[576,128]{1,0:T(8,128)(2,1)S(1)}, bf16[576,128]{1,0:T(8,128)(2,1)S(1)}, u32[]{:S(2)}, u32[]{:S(2)}) collective-permute-start(bf16[576,128]{1,0:T(8,128)(2,1)S(1)} %add_convert_fusion.3), channel_id=1, source_target_pairs={{0,4},{4,8},{8,12},{12,16},{16,20},{20,24},{24,28},{28,0},{1,5},{5... | collective-permute-start | bytes 442376 | tf_op jit(solution)/shard_map/ppermute | solution.py:69
  158.8 5.6 %collective-permute-start.17 = (bf16[576,128]{1,0:T(8,128)(2,1)S(1)}, bf16[576,128]{1,0:T(8,128)(2,1)S(1)}, u32[]{:S(2)}, u32[]{:S(2)}) collective-permute-start(bf16[576,128]{1,0:T(8,128)(2,1)S(1)} %add_convert_fusion.5), channel_id=1, source_target_pairs={{0,28},{4,0},{8,4},{12,8},{16,12},{20,16},{24,20},{28,24},{1,29},{... | collective-permute-start | bytes 442376 | tf_op jit(solution)/shard_map/ppermute | solution.py:69
  164.4 6.0 %collective-permute-start.21 = (bf16[576,128]{1,0:T(8,128)(2,1)S(1)}, bf16[576,128]{1,0:T(8,128)(2,1)S(1)}, u32[]{:S(2)}, u32[]{:S(2)}) collective-permute-start(bf16[576,128]{1,0:T(8,128)(2,1)S(1)} %add_convert_fusion.2), channel_id=1, source_target_pairs={{0,4},{4,8},{8,12},{12,16},{16,20},{20,24},{24,28},{28,0},{1,5},{5... | collective-permute-start | bytes 442376 | tf_op jit(solution)/shard_map/ppermute | solution.py:69
  170.4 6.7 %collective-permute-start.18 = (bf16[576,128]{1,0:T(8,128)(2,1)S(1)}, bf16[576,128]{1,0:T(8,128)(2,1)S(1)}, u32[]{:S(2)}, u32[]{:S(2)}) collective-permute-start(bf16[576,128]{1,0:T(8,128)(2,1)S(1)} %add_convert_fusion.4), channel_id=1, source_target_pairs={{0,28},{1,29},{2,61},{3,60},{4,0},{5,1},{6,33},{7,32},{8,4},{9,5},... | collective-permute-start | bytes 442376 | tf_op jit(solution)/shard_map/ppermute | solution.py:57
  173.2 8.0 %collective-permute-start.22 = (bf16[576,128]{1,0:T(8,128)(2,1)S(1)}, bf16[576,128]{1,0:T(8,128)(2,1)S(1)}, u32[]{:S(2)}, u32[]{:S(2)}) collective-permute-start(bf16[576,128]{1,0:T(8,128)(2,1)S(1)} %add_convert_fusion.1), channel_id=1, source_target_pairs={{0,4},{1,5},{2,37},{3,36},{4,8},{5,9},{6,41},{7,40},{8,12},{9,13},... | collective-permute-start | bytes 442376 | tf_op jit(solution)/shard_map/ppermute | solution.py:57
